TPU v7x, 32 devices: a whole 2x2x4 slice. The times are simulated.
32 devices in a mesh: slab: 4 (over y, x), dom: 8 (over z, core).
Axes of the slice: x: 2, y: 2, z: 4, core: 2. Of those that a mesh axis runs over, the one named last changes fastest.
Arguments:
- incoming: float32 [4, 2048, 4, 128], P('slab', 'dom'), may hold values from -8 to 65, as said below
- dest: int32 [4, 2048], P('slab', 'dom'), may hold values from 0 to 2047, as said below
- counts: int32 [8, 16, 64], P('slab', 'dom'), may hold values from 0 to 128, as said below
Outputs:
- density: float32 [8, 16, 64, 128], P('slab', 'dom')
- laplace: float32 [8, 16, 64, 128], P('slab', 'dom')
Inputs may be any that keep to these rules, and one draw needn't show every extreme that they name: `incoming`: positions lie inside the cell that dest assigns to their block, and slots beyond a cell's count hold positions too. dest holds each cell id of the slab exactly once; every block goes to a domain at most 2 indices away along dom, counted cyclically; from one domain exactly 64 blocks go to each of four domains and none to the others. `counts`: the lowest quarter of the z cells are full.
All inputs are finite; a program needn't handle non-finite values.
Results may differ from a plain program's by a relative error of at most 0.0003.
Values sent between devices are 32-bit elements; how exact they have to be, the bound alone decides.
No kernel may reach another device: no remote copies, remote signals or barrier semaphores. Data moves between devices by JAX's collectives and lax.ppermute only.
A program may use at most 64 MiB of HBM per device.

v0:
```python
import math

import jax
import jax.numpy as jnp
from jax import lax
from jax.sharding import PartitionSpec as P

radius_eff = 1.0
radius_min = 0.1
ref_density = 268.0825731


def shifted(value, axis, steps):
    count = lax.axis_size(axis)
    pairs = [(source, (source + steps) % count) for source in range(count)]
    return lax.ppermute(value, axis, pairs)


def padded(cells, sides, width):
    for axis, dim in sides:
        count = lax.axis_size(axis)
        ends = count - 1
        head = lax.slice_in_dim(cells, 0, width, axis=dim)
        tail = lax.slice_in_dim(cells, cells.shape[dim] - width, cells.shape[dim], axis=dim)
        cells = jnp.concatenate(
            [
                lax.ppermute(tail, axis, [(i, (i + 1) % count) for i in range(ends)]),
                cells,
                lax.ppermute(head, axis, [((i + 1) % count, i) for i in range(ends)]),
            ],
            axis=dim,
        )
    return cells


def from_behind(block, axis, distance):
    devices = range(lax.axis_size(axis))
    route = [(i - distance, i) for i in devices if i - distance in devices]
    return lax.ppermute(block, axis, route)


def pair_weights(own_cells, own_mask, far_cells, far_mask, diagonal):
    spread = own_cells[:, 0, :, None] - far_cells[:, 0, None, :]
    distance = spread * spread
    for channel in range(1, 3):
        spread = own_cells[:, channel, :, None] - far_cells[:, channel, None, :]
        distance = distance + spread * spread
    radius = jnp.sqrt(jnp.maximum(distance, radius_min * radius_min))
    weight = (
        jnp.maximum(radius_eff / radius - 1.0, 0.0) * own_mask[:, :, None] * far_mask[:, None, :]
    )
    if diagonal:
        weight = weight * (1.0 - jnp.eye(own_mask.shape[1], dtype=weight.dtype))
    return weight


def shell_sums(own_cells, own_mask, far_list, flag_list):
    total_cells = own_cells.shape[0]
    block_width = math.gcd(total_cells, 64)
    groups = total_cells // block_width

    def split_rows(array):
        return array.reshape((groups, block_width) + array.shape[1:])

    far_stacked = tuple(
        ((split_rows(far_part), split_rows(far_flag)) for far_part, far_flag in far_list)
    )

    def one_block(inputs):
        own_part, own_flag, far_pairs = inputs
        outputs = []
        for (far_part, far_flag), (diagonal, with_columns) in zip(far_pairs, flag_list):
            weight = pair_weights(own_part, own_flag, far_part, far_flag, diagonal)
            results = (weight.sum(2), (weight * far_part[:, 3, None, :]).sum(2))
            if with_columns:
                results = results + (weight.sum(1), (weight * own_part[:, 3, :, None]).sum(1))
            outputs.append(results)
        return tuple(outputs)

    mapped = lax.map(one_block, (split_rows(own_cells), split_rows(own_mask), far_stacked))
    return tuple(
        (
            tuple((result.reshape((total_cells,) + result.shape[2:]) for result in results))
            for results in mapped
        )
    )


def local(incoming, dest, counts):
    cells_x, cells_y, cells_z = counts.shape
    slots = incoming.shape[3]
    cell_total = cells_x * cells_y * cells_z
    capacity = cell_total // 4
    domains = lax.axis_size("dom")
    channels = incoming.shape[2] * slots
    blocks = incoming.reshape(cell_total, channels)
    targets = dest.reshape(cell_total)
    target_dom = targets // cell_total
    target_local = (targets % cell_total).astype(jnp.float32)
    my_index = lax.axis_index("dom")
    distance = (target_dom - my_index) % domains
    distance = jnp.where(distance > domains // 2, distance - domains, distance)
    stay_home = distance == 0
    arrived_data = [blocks]
    arrived_index = [jnp.where(stay_home, target_local, -1.0)]
    for offset in (-2, -1, 1, 2):
        chosen = distance == offset
        ranking = jnp.cumsum(chosen.astype(jnp.int32)) - 1
        slot_ids = jnp.where(chosen, ranking, capacity)
        pack_blocks = (
            jnp.zeros((capacity + 1, channels), jnp.float32).at[slot_ids].set(blocks)[:capacity]
        )
        pack_local = (
            jnp.full((capacity + 1,), -1.0, jnp.float32).at[slot_ids].set(target_local)[:capacity]
        )
        got_blocks, got_local = shifted((pack_blocks, pack_local), "dom", offset)
        arrived_data.append(got_blocks)
        arrived_index.append(got_local)
    merged_data = jnp.concatenate(arrived_data, 0)
    merged_index = jnp.concatenate(arrived_index, 0)
    rows_at = jnp.where(merged_index >= 0, merged_index, float(cell_total)).astype(jnp.int32)
    home_cells = (
        jnp.zeros((cell_total + 1, channels), jnp.float32).at[rows_at].set(merged_data)[:cell_total]
    )
    home_cells = home_cells.reshape(cells_x, cells_y, cells_z, channels)
    filled = counts.astype(jnp.float32)
    side_cells, side_count = (
        padded(home_cells, (("dom", 1),), 1),
        padded(filled, (("dom", 1),), 1),
    )
    front_cells, front_count = from_behind((side_cells[0], side_count[0]), "slab", -1)
    padded_grid = jnp.concatenate([side_cells, front_cells[None]], 0)
    grid_count = jnp.concatenate([side_count, front_count[None]], 0)
    start_x = 0
    pair_offsets = [(0, 0, 0), (0, 0, 1)]
    for plane_x, plane_y in ((1, 0), (0, 1), (1, 1), (1, -1)):
        for shift_z in (-1, 0, 1):
            pair_offsets.append((plane_x, plane_y, shift_z))
    padded_grid = jnp.pad(padded_grid, ((0, 0), (0, 0), (1, 1), (0, 0)))
    grid_count = jnp.pad(grid_count, ((0, 0), (0, 0), (1, 1)))
    slot_index = jnp.arange(slots).astype(jnp.float32)
    grid_mask = (slot_index < grid_count[..., None]).astype(jnp.float32)
    grid_cells = padded_grid.reshape(padded_grid.shape[:3] + (4, slots))
    sum_n = jnp.zeros(grid_mask.shape, jnp.float32)
    sum_s = jnp.zeros(grid_mask.shape, jnp.float32)
    own_cells = grid_cells[start_x : start_x + cells_x, 1 : 1 + cells_y, 1 : 1 + cells_z].reshape(
        cell_total, 4, slots
    )
    own_mask = grid_mask[start_x : start_x + cells_x, 1 : 1 + cells_y, 1 : 1 + cells_z].reshape(
        cell_total, slots
    )
    block_shape = (cells_x, cells_y, cells_z, slots)
    far_list = []
    flag_list = []
    for shift_x, shift_y, shift_z in pair_offsets:
        lower_x = start_x + shift_x
        lower_y = 1 + shift_y
        lower_z = 1 + shift_z
        far_cells = grid_cells[
            lower_x : lower_x + cells_x, lower_y : lower_y + cells_y, lower_z : lower_z + cells_z
        ].reshape(cell_total, 4, slots)
        far_mask = grid_mask[
            lower_x : lower_x + cells_x, lower_y : lower_y + cells_y, lower_z : lower_z + cells_z
        ].reshape(cell_total, slots)
        diagonal = shift_x == 0 and shift_y == 0 and (shift_z == 0)
        with_columns = not diagonal
        far_list.append((far_cells, far_mask))
        flag_list.append((diagonal, with_columns))
    all_results = shell_sums(own_cells, own_mask, tuple(far_list), tuple(flag_list))
    for (shift_x, shift_y, shift_z), (diagonal, with_columns), results in zip(
        pair_offsets, flag_list, all_results
    ):
        lower_x = start_x + shift_x
        lower_y = 1 + shift_y
        lower_z = 1 + shift_z
        sum_n = sum_n.at[start_x : start_x + cells_x, 1 : 1 + cells_y, 1 : 1 + cells_z].add(
            results[0].reshape(block_shape)
        )
        sum_s = sum_s.at[start_x : start_x + cells_x, 1 : 1 + cells_y, 1 : 1 + cells_z].add(
            results[1].reshape(block_shape)
        )
        if with_columns:
            sum_n = sum_n.at[
                lower_x : lower_x + cells_x,
                lower_y : lower_y + cells_y,
                lower_z : lower_z + cells_z,
            ].add(results[2].reshape(block_shape))
            sum_s = sum_s.at[
                lower_x : lower_x + cells_x,
                lower_y : lower_y + cells_y,
                lower_z : lower_z + cells_z,
            ].add(results[3].reshape(block_shape))
    back_n, back_s = from_behind((sum_n[cells_x], sum_s[cells_x]), "slab", 1)
    sum_n = sum_n.at[0].add(back_n)
    sum_s = sum_s.at[0].add(back_s)
    lower_n, lower_s = from_behind((sum_n[:cells_x, 0], sum_s[:cells_x, 0]), "dom", -1)
    sum_n = sum_n.at[:cells_x, cells_y].add(lower_n)
    sum_s = sum_s.at[:cells_x, cells_y].add(lower_s)
    upper_n, upper_s = from_behind(
        (sum_n[:cells_x, cells_y + 1], sum_s[:cells_x, cells_y + 1]), "dom", 1
    )
    sum_n = sum_n.at[:cells_x, 1].add(upper_n)
    sum_s = sum_s.at[:cells_x, 1].add(upper_s)
    totals_n = sum_n[start_x : start_x + cells_x, 1 : 1 + cells_y, 1 : 1 + cells_z]
    totals_s = sum_s[start_x : start_x + cells_x, 1 : 1 + cells_y, 1 : 1 + cells_z]
    potential = home_cells[..., 3 * slots : 4 * slots]
    density = totals_n / ref_density
    laplace = (totals_s - potential * totals_n) / ref_density
    return (density, laplace)


def solution(mesh):
    in_specs = (P("slab", "dom", None, None), P("slab", "dom"), P("slab", "dom", None))
    out_specs = (P("slab", "dom", None, None), P("slab", "dom", None, None))
    return jax.shard_map(local, mesh=mesh, in_specs=in_specs, out_specs=out_specs, check_vma=False)
```

profile of v0, /device:TPU:0, one launch (start us, length us, event | category | flops | bytes accessed | tf_op | source)
XLA Modules:
  0.0 648.2 jit_solution(5697303127007685463)
XLA Ops:
  6.5 4.6 collective-permute-start.1
  17.5 2.0 scatter_custom_fusion.4
  19.5 2.9 collective-permute-start.4
  30.0 2.0 collective-permute-start.5
  33.7 2.0 collective-permute-start.11
  40.3 2.4 scatter_custom_fusion.8
  42.8 2.4 collective-permute-start.8
  50.4 2.8 collective-permute-done.13
  54.6 9.6 %collective-permute-done.10 = f32[4,64,512]{2,1,0:T(8,128)S(1)} collective-permute-done((f32[4,64,512]{2,1,0:T(8,128)S(1)}, f32[4,64,512]{2,1,0:T(8,128)S(1)}, u32[]{:S(2)}, u32[]{:S(2)}) %collective-permute-start.10) | collective-permute-done | bytes 524320 | tf_op jit(solution)/shard_map/ppermute | solution.py:39
  65.7 1.9 reshape.2958
  76.9 517.9 %while.180 = (s32[]{:T(128)}, f32[4,64,128]{2,1,0:T(8,128)}, f32[4,64,128]{2,1,0:T(8,128)}, f32[4,64,128]{2,1,0:T(8,128)}, f32[4,64,128]{2,1,0:T(8,128)}, /*inde...) while((s32[]{:T(128)}, f32[4,64,128]{2,1,0:T(8,128)}, ...), condition=%wide.region_72.73_spmd, body=%wide.region_17.72_spmd.sunk | while | flops 276430848 | bytes 17002220 | solution.py:80
  81.2 12.4 %multiply_reduce_fusion.37 = (f32[64,128]{1,0:T(8,128)S(1)}, f32[64,128]{1,0:T(8,128)S(1)}, f32[64,128]{1,0:T(8,128)S(1)}, f32[64,128]{1,0:T(8,128)S(1)}, f32[64...) fusion(f32[64,128]{1,0:T(8,128)S(1)} %get-tuple-element.3216, ...), kind=kLoop, calls=%fused_computation.15.clone.1 | loop fusion | flops 39780352 | bytes 753664 | tf_op jit(solution)/shard_map/while/body/eval_jaxpr/reduce_sum | solution.py:76
  96.1 12.4 %multiply_reduce_fusion.38 = (f32[64,128]{1,0:T(8,128)S(1)}, f32[64,128]{1,0:T(8,128)S(1)}, f32[64,128]{1,0:T(8,128)S(1)}, f32[64,128]{1,0:T(8,128)S(1)}, f32[64...) fusion(f32[64,128]{1,0:T(8,128)S(1)} %get-tuple-element.3216, ...), kind=kLoop, calls=%fused_computation.18.clone.1 | loop fusion | flops 39780352 | bytes 753664 | tf_op jit(solution)/shard_map/while/body/eval_jaxpr/reduce_sum | solution.py:76
  114.5 12.4 %multiply_reduce_fusion.39 = (f32[64,128]{1,0:T(8,128)S(1)}, f32[64,128]{1,0:T(8,128)S(1)}, f32[64,128]{1,0:T(8,128)S(1)}, f32[64,128]{1,0:T(8,128)S(1)}, f32[64...) fusion(f32[64,128]{1,0:T(8,128)S(1)} %get-tuple-element.3216, ...), kind=kLoop, calls=%fused_computation.21.clone.1 | loop fusion | flops 39780352 | bytes 753664 | tf_op jit(solution)/shard_map/while/body/eval_jaxpr/reduce_sum | solution.py:76
  129.4 12.4 %multiply_reduce_fusion.40 = (f32[64,128]{1,0:T(8,128)S(1)}, f32[64,128]{1,0:T(8,128)S(1)}, f32[64,128]{1,0:T(8,128)S(1)}, f32[64,128]{1,0:T(8,128)S(1)}, f32[64...) fusion(f32[64,128]{1,0:T(8,128)S(1)} %get-tuple-element.3216, ...), kind=kLoop, calls=%fused_computation.24.clone.1 | loop fusion | flops 39780352 | bytes 753664 | tf_op jit(solution)/shard_map/while/body/eval_jaxpr/reduce_sum | solution.py:76
  155.7 12.4 %multiply_reduce_fusion.36 = (f32[64,128]{1,0:T(8,128)S(1)}, f32[64,128]{1,0:T(8,128)S(1)}, f32[64,128]{1,0:T(8,128)S(1)}, f32[64,128]{1,0:T(8,128)S(1)}, f32[64...) fusion(f32[64,128]{1,0:T(8,128)S(1)} %get-tuple-element.3216, ...), kind=kLoop, calls=%fused_computation.12.clone.1 | loop fusion | flops 39780352 | bytes 753664 | tf_op jit(solution)/shard_map/while/body/eval_jaxpr/reduce_sum | solution.py:76
  173.0 9.7 %multiply_reduce_fusion.35 = (f32[64,128]{1,0:T(8,128)S(1)}, f32[64,128]{1,0:T(8,128)S(1)}, f32[64,128]{1,0:T(8,128)S(1)}, f32[64,128]{1,0:T(8,128)S(1)}) fusion(f32[64,128]{1,0:T(8,128)S(1)} %get-tuple-element.3216, f32[64,128]{1,0:T(8,128)S(1)} %get-tuple-element.3235, f32[64,128]{1,0:T(8,128)S(1)} %get-tuple-element.3218, ...), kind=kLoop, calls=%fused_computation.45.clone.1 | loop fusion | flops 19890176 | bytes 458752 | tf_op jit(solution)/shard_map/while/body/eval_jaxpr/reduce_sum | solution.py:76
  185.1 15.0 %multiply_reduce_fusion.34 = (f32[64,128]{1,0:T(8,128)S(1)}, f32[64,128]{1,0:T(8,128)S(1)}, f32[64,128]{1,0:T(8,128)S(1)}, f32[64,128]{1,0:T(8,128)S(1)}, f32[64...) fusion(f32[64,128]{1,0:T(8,128)S(1)} %get-tuple-element.3216, ...), kind=kLoop, calls=%fused_computation.9.clone.1 | loop fusion | flops 57589760 | bytes 884736 | tf_op jit(solution)/shard_map/while/body/eval_jaxpr/reduce_sum | solution.py:76
  210.6 12.4 %multiply_reduce_fusion.37 = (f32[64,128]{1,0:T(8,128)S(1)}, f32[64,128]{1,0:T(8,128)S(1)}, f32[64,128]{1,0:T(8,128)S(1)}, f32[64,128]{1,0:T(8,128)S(1)}, f32[64...) fusion(f32[64,128]{1,0:T(8,128)S(1)} %get-tuple-element.3216, ...), kind=kLoop, calls=%fused_computation.15.clone.1 | loop fusion | flops 39780352 | bytes 753664 | tf_op jit(solution)/shard_map/while/body/eval_jaxpr/reduce_sum | solution.py:76
  225.4 12.4 %multiply_reduce_fusion.38 = (f32[64,128]{1,0:T(8,128)S(1)}, f32[64,128]{1,0:T(8,128)S(1)}, f32[64,128]{1,0:T(8,128)S(1)}, f32[64,128]{1,0:T(8,128)S(1)}, f32[64...) fusion(f32[64,128]{1,0:T(8,128)S(1)} %get-tuple-element.3216, ...), kind=kLoop, calls=%fused_computation.18.clone.1 | loop fusion | flops 39780352 | bytes 753664 | tf_op jit(solution)/shard_map/while/body/eval_jaxpr/reduce_sum | solution.py:76
  243.9 12.4 %multiply_reduce_fusion.39 = (f32[64,128]{1,0:T(8,128)S(1)}, f32[64,128]{1,0:T(8,128)S(1)}, f32[64,128]{1,0:T(8,128)S(1)}, f32[64,128]{1,0:T(8,128)S(1)}, f32[64...) fusion(f32[64,128]{1,0:T(8,128)S(1)} %get-tuple-element.3216, ...), kind=kLoop, calls=%fused_computation.21.clone.1 | loop fusion | flops 39780352 | bytes 753664 | tf_op jit(solution)/shard_map/while/body/eval_jaxpr/reduce_sum | solution.py:76
  258.8 12.4 %multiply_reduce_fusion.40 = (f32[64,128]{1,0:T(8,128)S(1)}, f32[64,128]{1,0:T(8,128)S(1)}, f32[64,128]{1,0:T(8,128)S(1)}, f32[64,128]{1,0:T(8,128)S(1)}, f32[64...) fusion(f32[64,128]{1,0:T(8,128)S(1)} %get-tuple-element.3216, ...), kind=kLoop, calls=%fused_computation.24.clone.1 | loop fusion | flops 39780352 | bytes 753664 | tf_op jit(solution)/shard_map/while/body/eval_jaxpr/reduce_sum | solution.py:76
  285.2 12.4 %multiply_reduce_fusion.36 = (f32[64,128]{1,0:T(8,128)S(1)}, f32[64,128]{1,0:T(8,128)S(1)}, f32[64,128]{1,0:T(8,128)S(1)}, f32[64,128]{1,0:T(8,128)S(1)}, f32[64...) fusion(f32[64,128]{1,0:T(8,128)S(1)} %get-tuple-element.3216, ...), kind=kLoop, calls=%fused_computation.12.clone.1 | loop fusion | flops 39780352 | bytes 753664 | tf_op jit(solution)/shard_map/while/body/eval_jaxpr/reduce_sum | solution.py:76
  302.5 9.7 %multiply_reduce_fusion.35 = (f32[64,128]{1,0:T(8,128)S(1)}, f32[64,128]{1,0:T(8,128)S(1)}, f32[64,128]{1,0:T(8,128)S(1)}, f32[64,128]{1,0:T(8,128)S(1)}) fusion(f32[64,128]{1,0:T(8,128)S(1)} %get-tuple-element.3216, f32[64,128]{1,0:T(8,128)S(1)} %get-tuple-element.3235, f32[64,128]{1,0:T(8,128)S(1)} %get-tuple-element.3218, ...), kind=kLoop, calls=%fused_computation.45.clone.1 | loop fusion | flops 19890176 | bytes 458752 | tf_op jit(solution)/shard_map/while/body/eval_jaxpr/reduce_sum | solution.py:76
  314.7 15.0 %multiply_reduce_fusion.34 = (f32[64,128]{1,0:T(8,128)S(1)}, f32[64,128]{1,0:T(8,128)S(1)}, f32[64,128]{1,0:T(8,128)S(1)}, f32[64,128]{1,0:T(8,128)S(1)}, f32[64...) fusion(f32[64,128]{1,0:T(8,128)S(1)} %get-tuple-element.3216, ...), kind=kLoop, calls=%fused_computation.9.clone.1 | loop fusion | flops 57589760 | bytes 884736 | tf_op jit(solution)/shard_map/while/body/eval_jaxpr/reduce_sum | solution.py:76
  340.1 12.4 %multiply_reduce_fusion.37 = (f32[64,128]{1,0:T(8,128)S(1)}, f32[64,128]{1,0:T(8,128)S(1)}, f32[64,128]{1,0:T(8,128)S(1)}, f32[64,128]{1,0:T(8,128)S(1)}, f32[64...) fusion(f32[64,128]{1,0:T(8,128)S(1)} %get-tuple-element.3216, ...), kind=kLoop, calls=%fused_computation.15.clone.1 | loop fusion | flops 39780352 | bytes 753664 | tf_op jit(solution)/shard_map/while/body/eval_jaxpr/reduce_sum | solution.py:76
  355.0 12.4 %multiply_reduce_fusion.38 = (f32[64,128]{1,0:T(8,128)S(1)}, f32[64,128]{1,0:T(8,128)S(1)}, f32[64,128]{1,0:T(8,128)S(1)}, f32[64,128]{1,0:T(8,128)S(1)}, f32[64...) fusion(f32[64,128]{1,0:T(8,128)S(1)} %get-tuple-element.3216, ...), kind=kLoop, calls=%fused_computation.18.clone.1 | loop fusion | flops 39780352 | bytes 753664 | tf_op jit(solution)/shard_map/while/body/eval_jaxpr/reduce_sum | solution.py:76
  373.4 12.4 %multiply_reduce_fusion.39 = (f32[64,128]{1,0:T(8,128)S(1)}, f32[64,128]{1,0:T(8,128)S(1)}, f32[64,128]{1,0:T(8,128)S(1)}, f32[64,128]{1,0:T(8,128)S(1)}, f32[64...) fusion(f32[64,128]{1,0:T(8,128)S(1)} %get-tuple-element.3216, ...), kind=kLoop, calls=%fused_computation.21.clone.1 | loop fusion | flops 39780352 | bytes 753664 | tf_op jit(solution)/shard_map/while/body/eval_jaxpr/reduce_sum | solution.py:76
  388.3 12.4 %multiply_reduce_fusion.40 = (f32[64,128]{1,0:T(8,128)S(1)}, f32[64,128]{1,0:T(8,128)S(1)}, f32[64,128]{1,0:T(8,128)S(1)}, f32[64,128]{1,0:T(8,128)S(1)}, f32[64...) fusion(f32[64,128]{1,0:T(8,128)S(1)} %get-tuple-element.3216, ...), kind=kLoop, calls=%fused_computation.24.clone.1 | loop fusion | flops 39780352 | bytes 753664 | tf_op jit(solution)/shard_map/while/body/eval_jaxpr/reduce_sum | solution.py:76
  414.7 12.4 %multiply_reduce_fusion.36 = (f32[64,128]{1,0:T(8,128)S(1)}, f32[64,128]{1,0:T(8,128)S(1)}, f32[64,128]{1,0:T(8,128)S(1)}, f32[64,128]{1,0:T(8,128)S(1)}, f32[64...) fusion(f32[64,128]{1,0:T(8,128)S(1)} %get-tuple-element.3216, ...), kind=kLoop, calls=%fused_computation.12.clone.1 | loop fusion | flops 39780352 | bytes 753664 | tf_op jit(solution)/shard_map/while/body/eval_jaxpr/reduce_sum | solution.py:76
  431.9 9.7 %multiply_reduce_fusion.35 = (f32[64,128]{1,0:T(8,128)S(1)}, f32[64,128]{1,0:T(8,128)S(1)}, f32[64,128]{1,0:T(8,128)S(1)}, f32[64,128]{1,0:T(8,128)S(1)}) fusion(f32[64,128]{1,0:T(8,128)S(1)} %get-tuple-element.3216, f32[64,128]{1,0:T(8,128)S(1)} %get-tuple-element.3235, f32[64,128]{1,0:T(8,128)S(1)} %get-tuple-element.3218, ...), kind=kLoop, calls=%fused_computation.45.clone.1 | loop fusion | flops 19890176 | bytes 458752 | tf_op jit(solution)/shard_map/while/body/eval_jaxpr/reduce_sum | solution.py:76
  444.1 15.0 %multiply_reduce_fusion.34 = (f32[64,128]{1,0:T(8,128)S(1)}, f32[64,128]{1,0:T(8,128)S(1)}, f32[64,128]{1,0:T(8,128)S(1)}, f32[64,128]{1,0:T(8,128)S(1)}, f32[64...) fusion(f32[64,128]{1,0:T(8,128)S(1)} %get-tuple-element.3216, ...), kind=kLoop, calls=%fused_computation.9.clone.1 | loop fusion | flops 57589760 | bytes 884736 | tf_op jit(solution)/shard_map/while/body/eval_jaxpr/reduce_sum | solution.py:76
  469.5 12.4 %multiply_reduce_fusion.37 = (f32[64,128]{1,0:T(8,128)S(1)}, f32[64,128]{1,0:T(8,128)S(1)}, f32[64,128]{1,0:T(8,128)S(1)}, f32[64,128]{1,0:T(8,128)S(1)}, f32[64...) fusion(f32[64,128]{1,0:T(8,128)S(1)} %get-tuple-element.3216, ...), kind=kLoop, calls=%fused_computation.15.clone.1 | loop fusion | flops 39780352 | bytes 753664 | tf_op jit(solution)/shard_map/while/body/eval_jaxpr/reduce_sum | solution.py:76
  484.4 12.4 %multiply_reduce_fusion.38 = (f32[64,128]{1,0:T(8,128)S(1)}, f32[64,128]{1,0:T(8,128)S(1)}, f32[64,128]{1,0:T(8,128)S(1)}, f32[64,128]{1,0:T(8,128)S(1)}, f32[64...) fusion(f32[64,128]{1,0:T(8,128)S(1)} %get-tuple-element.3216, ...), kind=kLoop, calls=%fused_computation.18.clone.1 | loop fusion | flops 39780352 | bytes 753664 | tf_op jit(solution)/shard_map/while/body/eval_jaxpr/reduce_sum | solution.py:76
  502.9 12.4 %multiply_reduce_fusion.39 = (f32[64,128]{1,0:T(8,128)S(1)}, f32[64,128]{1,0:T(8,128)S(1)}, f32[64,128]{1,0:T(8,128)S(1)}, f32[64,128]{1,0:T(8,128)S(1)}, f32[64...) fusion(f32[64,128]{1,0:T(8,128)S(1)} %get-tuple-element.3216, ...), kind=kLoop, calls=%fused_computation.21.clone.1 | loop fusion | flops 39780352 | bytes 753664 | tf_op jit(solution)/shard_map/while/body/eval_jaxpr/reduce_sum | solution.py:76
  517.7 12.4 %multiply_reduce_fusion.40 = (f32[64,128]{1,0:T(8,128)S(1)}, f32[64,128]{1,0:T(8,128)S(1)}, f32[64,128]{1,0:T(8,128)S(1)}, f32[64,128]{1,0:T(8,128)S(1)}, f32[64...) fusion(f32[64,128]{1,0:T(8,128)S(1)} %get-tuple-element.3216, ...), kind=kLoop, calls=%fused_computation.24.clone.1 | loop fusion | flops 39780352 | bytes 753664 | tf_op jit(solution)/shard_map/while/body/eval_jaxpr/reduce_sum | solution.py:76
  544.1 12.4 %multiply_reduce_fusion.36 = (f32[64,128]{1,0:T(8,128)S(1)}, f32[64,128]{1,0:T(8,128)S(1)}, f32[64,128]{1,0:T(8,128)S(1)}, f32[64,128]{1,0:T(8,128)S(1)}, f32[64...) fusion(f32[64,128]{1,0:T(8,128)S(1)} %get-tuple-element.3216, ...), kind=kLoop, calls=%fused_computation.12.clone.1 | loop fusion | flops 39780352 | bytes 753664 | tf_op jit(solution)/shard_map/while/body/eval_jaxpr/reduce_sum | solution.py:76
  561.4 9.7 %multiply_reduce_fusion.35 = (f32[64,128]{1,0:T(8,128)S(1)}, f32[64,128]{1,0:T(8,128)S(1)}, f32[64,128]{1,0:T(8,128)S(1)}, f32[64,128]{1,0:T(8,128)S(1)}) fusion(f32[64,128]{1,0:T(8,128)S(1)} %get-tuple-element.3216, f32[64,128]{1,0:T(8,128)S(1)} %get-tuple-element.3235, f32[64,128]{1,0:T(8,128)S(1)} %get-tuple-element.3218, ...), kind=kLoop, calls=%fused_computation.45.clone.1 | loop fusion | flops 19890176 | bytes 458752 | tf_op jit(solution)/shard_map/while/body/eval_jaxpr/reduce_sum | solution.py:76
  573.6 15.0 %multiply_reduce_fusion.34 = (f32[64,128]{1,0:T(8,128)S(1)}, f32[64,128]{1,0:T(8,128)S(1)}, f32[64,128]{1,0:T(8,128)S(1)}, f32[64,128]{1,0:T(8,128)S(1)}, f32[64...) fusion(f32[64,128]{1,0:T(8,128)S(1)} %get-tuple-element.3216, ...), kind=kLoop, calls=%fused_computation.9.clone.1 | loop fusion | flops 57589760 | bytes 884736 | tf_op jit(solution)/shard_map/while/body/eval_jaxpr/reduce_sum | solution.py:76
  597.1 2.8 dynamic-slice_add_fusion.1
  599.8 2.1 scatter-add.204
  609.3 5.5 collective-permute-start.14
  615.2 1.9 dynamic-slice_add_fusion
  617.0 2.1 scatter-add.254
  626.2 4.3 collective-permute-start.17
  631.9 2.2 collective-permute-done.17
  637.3 3.0 collective-permute-start.16
  642.2 2.6 collective-permute-start.19
  (706 shorter events, 238.1 us)
Async XLA Ops:
  0.6 22.9 %copy-start = (f32[1,256,4,128]{3,2,1,0:T(4,128)S(1)}, f32[1,256,4,128]{3,2,1,0:T(4,128)}, u32[]{:S(2)}) copy-start(f32[1,256,4,128]{3,2,1,0:T(4,128)} %param.125) | copy-start | bytes 1572868
  0.6 24.4 %copy-start.52 = (s32[2,2,64]{2,1,0:T(2,128)S(1)}, s32[2,2,64]{2,1,0:T(2,128)}, u32[]{:S(2)}) copy-start(s32[2,2,64]{2,1,0:T(2,128)} %param.127) | copy-start | bytes 3076
  6.5 23.4 %collective-permute-start.1 = (f32[64]{0:T(128)S(1)}, f32[64]{0:T(128)S(1)}, u32[]{:S(2)}, u32[]{:S(2)}) collective-permute-start(f32[64]{0:T(128)S(1)} %bitcast.737), channel_id=1, source_target_pairs={{0,7},{1,0},{2,1},{3,2},{4,3},{5,4},{6,5},{7,6},{8,15},{9,8},{10,9... | collective-permute-start | bytes 776 | tf_op jit(solution)/shard_map/ppermute | solution.py:16
  12.5 19.4 %collective-permute-start.2 = (f32[64]{0:T(128)S(1)}, f32[64]{0:T(128)S(1)}, u32[]{:S(2)}, u32[]{:S(2)}) collective-permute-start(f32[64]{0:T(128)S(1)} %bitcast.736), channel_id=1, source_target_pairs={{0,1},{1,2},{2,3},{3,4},{4,5},{5,6},{6,7},{7,0},{8,9},{9,10},{10,1... | collective-permute-start | bytes 776 | tf_op jit(solution)/shard_map/ppermute | solution.py:16
  14.0 18.1 %collective-permute-start = (f32[64]{0:T(128)S(1)}, f32[64]{0:T(128)S(1)}, u32[]{:S(2)}, u32[]{:S(2)}) collective-permute-start(f32[64]{0:T(128)S(1)} %bitcast.735), channel_id=1, source_target_pairs={{0,6},{1,7},{2,0},{3,1},{4,2},{5,3},{6,4},{7,5},{8,14},{9,15},{10,... | collective-permute-start | bytes 776 | tf_op jit(solution)/shard_map/ppermute | solution.py:16
  16.5 17.3 %collective-permute-start.3 = (f32[64]{0:T(128)S(1)}, f32[64]{0:T(128)S(1)}, u32[]{:S(2)}, u32[]{:S(2)}) collective-permute-start(f32[64]{0:T(128)S(1)} %bitcast.734), channel_id=1, source_target_pairs={{0,2},{1,3},{2,4},{3,5},{4,6},{5,7},{6,0},{7,1},{8,10},{9,11},{10,... | collective-permute-start | bytes 776 | tf_op jit(solution)/shard_map/ppermute | solution.py:16
  19.5 16.3 %collective-permute-start.4 = (f32[64,512]{1,0:T(8,128)S(1)}, f32[64,512]{1,0:T(8,128)S(1)}, u32[]{:S(2)}, u32[]{:S(2)}) collective-permute-start(f32[64,512]{1,0:T(8,128)S(1)} %slice.3001), channel_id=1, source_target_pairs={{0,6},{1,7},{2,0},{3,1},{4,2},{5,3},{6,4},{7,5},{8,14},{9,15},{10,... | collective-permute-start | bytes 393224 | tf_op jit(solution)/shard_map/ppermute | solution.py:16
  30.0 7.2 %collective-permute-start.5 = (f32[64,512]{1,0:T(8,128)S(1)}, f32[64,512]{1,0:T(8,128)S(1)}, u32[]{:S(2)}, u32[]{:S(2)}) collective-permute-start(f32[64,512]{1,0:T(8,128)S(1)} %slice.3002), channel_id=1, source_target_pairs={{0,7},{1,0},{2,1},{3,2},{4,3},{5,4},{6,5},{7,6},{8,15},{9,8},{10,9... | collective-permute-start | bytes 393224 | tf_op jit(solution)/shard_map/ppermute | solution.py:16
  31.9 6.8 %collective-permute-start.6 = (f32[64,512]{1,0:T(8,128)S(1)}, f32[64,512]{1,0:T(8,128)S(1)}, u32[]{:S(2)}, u32[]{:S(2)}) collective-permute-start(f32[64,512]{1,0:T(8,128)S(1)} %slice.3003), channel_id=1, source_target_pairs={{0,1},{1,2},{2,3},{3,4},{4,5},{5,6},{6,7},{7,0},{8,9},{9,10},{10,1... | collective-permute-start | bytes 393224 | tf_op jit(solution)/shard_map/ppermute | solution.py:16
  32.1 8.2 %collective-permute-start.7 = (f32[64,512]{1,0:T(8,128)S(1)}, f32[64,512]{1,0:T(8,128)S(1)}, u32[]{:S(2)}, u32[]{:S(2)}) collective-permute-start(f32[64,512]{1,0:T(8,128)S(1)} %slice.3004), channel_id=1, source_target_pairs={{0,2},{1,3},{2,4},{3,5},{4,6},{5,7},{6,0},{7,1},{8,10},{9,11},{10,... | collective-permute-start | bytes 393224 | tf_op jit(solution)/shard_map/ppermute | solution.py:16
  33.7 14.0 %collective-permute-start.11 = (f32[2,1,64]{2,1,0:T(1,128)S(1)}, f32[2,1,64]{2,1,0:T(1,128)S(1)}, u32[]{:S(2)}, u32[]{:S(2)}) collective-permute-start(f32[2,1,64]{2,1,0:T(1,128)S(1)} %get-tuple-element.2559), channel_id=1, source_target_pairs={{0,1},{1,2},{2,3},{3,4},{4,5},{5,6},{6,7},{8,9},{9,10},{10,11},{11... | collective-permute-start | bytes 1544 | tf_op jit(solution)/shard_map/ppermute | solution.py:27
  35.8 11.9 %collective-permute-start.12 = (f32[2,1,64]{2,1,0:T(1,128)S(1)}, f32[2,1,64]{2,1,0:T(1,128)S(1)}, u32[]{:S(2)}, u32[]{:S(2)}) collective-permute-start(f32[2,1,64]{2,1,0:T(1,128)S(1)} %get-tuple-element.2560), channel_id=1, source_target_pairs={{1,0},{2,1},{3,2},{4,3},{5,4},{6,5},{7,6},{9,8},{10,9},{11,10},{12... | collective-permute-start | bytes 1544 | tf_op jit(solution)/shard_map/ppermute | solution.py:29
  37.1 9.8 %copy-start.53 = (s32[4]{0:T(128)S(1)}, s32[4]{0:T(128)}, u32[]{:S(2)}) copy-start(s32[4]{0:T(128)} %constant.1667.clone.1) | copy-start | bytes 52
  42.8 6.3 collective-permute-start.8
  45.2 3.9 collective-permute-start.9
  47.7 5.5 collective-permute-start.13
  49.1 15.1 %collective-permute-start.10 = (f32[4,64,512]{2,1,0:T(8,128)S(1)}, f32[4,64,512]{2,1,0:T(8,128)S(1)}, u32[]{:S(2)}, u32[]{:S(2)}) collective-permute-start(f32[4,64,512]{2,1,0:T(8,128)S(1)} %fusion.36), channel_id=1, source_target_pairs={{8,0},{16,8},{24,16},{9,1},{17,9},{25,17},{10,2},{18,10},{26,18},{... | collective-permute-start | bytes 1572872 | tf_op jit(solution)/shard_map/ppermute | solution.py:39
  594.7 7.2 %copy-start.48 = (f32[4,64,128]{2,1,0:T(8,128)S(1)}, f32[4,64,128]{2,1,0:T(8,128)}, u32[]{:S(2)}) copy-start(f32[4,64,128]{2,1,0:T(8,128)} %get-tuple-element.2140) | copy-start | bytes 393220
  594.7 7.5 %copy-start.50 = (f32[4,64,128]{2,1,0:T(8,128)S(1)}, f32[4,64,128]{2,1,0:T(8,128)}, u32[]{:S(2)}) copy-start(f32[4,64,128]{2,1,0:T(8,128)} %get-tuple-element.2141) | copy-start | bytes 393220
  594.7 7.6 %copy-start.3 = (f32[4,64,128]{2,1,0:T(8,128)S(1)}, f32[4,64,128]{2,1,0:T(8,128)}, u32[]{:S(2)}) copy-start(f32[4,64,128]{2,1,0:T(8,128)} %get-tuple-element.2142) | copy-start | bytes 393220
  594.7 7.9 %copy-start.5 = (f32[4,64,128]{2,1,0:T(8,128)S(1)}, f32[4,64,128]{2,1,0:T(8,128)}, u32[]{:S(2)}) copy-start(f32[4,64,128]{2,1,0:T(8,128)} %get-tuple-element.2143) | copy-start | bytes 393220
  595.7 7.3 %copy-start.7 = (f32[4,64,128]{2,1,0:T(8,128)S(1)}, f32[4,64,128]{2,1,0:T(8,128)}, u32[]{:S(2)}) copy-start(f32[4,64,128]{2,1,0:T(8,128)} %get-tuple-element.2144) | copy-start | bytes 393220
  597.1 6.3 copy-start.9
  603.7 1.8 copy-start.23
  604.0 1.8 copy-start.25
  604.1 1.8 copy-start.27
  604.4 1.8 copy-start.29
  605.1 2.0 copy-start.34
  605.5 2.0 copy-start.36
  605.8 2.0 copy-start.38
  605.9 2.0 copy-start.40
  606.2 2.0 copy-start.42
  606.6 2.0 copy-start.44
  607.9 6.9 %copy-start.1 = (f32[4,64,128]{2,1,0:T(8,128)S(1)}, f32[4,64,128]{2,1,0:T(8,128)}, u32[]{:S(2)}) copy-start(f32[4,64,128]{2,1,0:T(8,128)} %get-tuple-element.2164) | copy-start | bytes 393220
  608.2 6.6 %copy-start.32 = (f32[4,64,128]{2,1,0:T(8,128)S(1)}, f32[4,64,128]{2,1,0:T(8,128)}, u32[]{:S(2)}) copy-start(f32[4,64,128]{2,1,0:T(8,128)} %get-tuple-element.2165) | copy-start | bytes 393220
  608.6 6.6 %copy-start.51 = (f32[4,64,128]{2,1,0:T(8,128)S(1)}, f32[4,64,128]{2,1,0:T(8,128)}, u32[]{:S(2)}) copy-start(f32[4,64,128]{2,1,0:T(8,128)} %get-tuple-element.2166) | copy-start | bytes 393220
  608.9 10.2 %copy-start.49 = (f32[4,64,128]{2,1,0:T(8,128)S(1)}, f32[4,64,128]{2,1,0:T(8,128)}, u32[]{:S(2)}) copy-start(f32[4,64,128]{2,1,0:T(8,128)} %get-tuple-element.2167) | copy-start | bytes 393220
  609.2 10.3 %copy-start.2 = (f32[4,64,128]{2,1,0:T(8,128)S(1)}, f32[4,64,128]{2,1,0:T(8,128)}, u32[]{:S(2)}) copy-start(f32[4,64,128]{2,1,0:T(8,128)} %get-tuple-element.2168) | copy-start | bytes 393220
  609.3 10.3 %copy-start.4 = (f32[4,64,128]{2,1,0:T(8,128)S(1)}, f32[4,64,128]{2,1,0:T(8,128)}, u32[]{:S(2)}) copy-start(f32[4,64,128]{2,1,0:T(8,128)} %get-tuple-element.2169) | copy-start | bytes 393220
  609.3 21.2 %collective-permute-start.14 = (f32[4,66,128]{2,1,0:T(8,128)S(1)}, f32[4,66,128]{2,1,0:T(8,128)S(1)}, u32[]{:S(2)}, u32[]{:S(2)}) collective-permute-start(f32[4,66,128]{2,1,0:T(8,128)S(1)} %slice_bitcast_fusion.58), channel_id=1, source_target_pairs={{0,8},{8,16},{16,24},{1,9},{9,17},{17,25},{2,10},{10,18},{18,26},{... | collective-permute-start | bytes 405512 | tf_op jit(solution)/shard_map/ppermute | solution.py:39
  614.8 5.1 copy-start.6
  614.8 5.4 copy-start.8
  615.2 5.4 copy-start.10
  626.2 7.9 %collective-permute-start.17 = (f32[4,66,128]{2,1,0:T(8,128)S(1)}, f32[4,66,128]{2,1,0:T(8,128)S(1)}, u32[]{:S(2)}, u32[]{:S(2)}) collective-permute-start(f32[4,66,128]{2,1,0:T(8,128)S(1)} %slice_bitcast_fusion.56), channel_id=1, source_target_pairs={{0,8},{8,16},{16,24},{1,9},{9,17},{17,25},{2,10},{10,18},{18,26},{... | collective-permute-start | bytes 405512 | tf_op jit(solution)/shard_map/ppermute | solution.py:39
  630.6 4.9 collective-permute-start.15
  634.1 6.2 collective-permute-start.18
  637.3 7.6 %collective-permute-start.16 = (f32[2,66,128]{2,1,0:T(8,128)S(1)}, f32[2,66,128]{2,1,0:T(8,128)S(1)}, u32[]{:S(2)}, u32[]{:S(2)}) collective-permute-start(f32[2,66,128]{2,1,0:T(8,128)S(1)} %slice_bitcast_fusion.62), channel_id=1, source_target_pairs={{0,1},{1,2},{2,3},{3,4},{4,5},{5,6},{6,7},{8,9},{9,10},{10,11},{11... | collective-permute-start | bytes 202760 | tf_op jit(solution)/shard_map/ppermute | solution.py:39
  642.2 3.9 collective-permute-start.19
  (26 other events, 45.6 us)
where the time goes:
time: 652 us; the launch traced here: 648 us
  other arithmetic  367 us (56%)
  local copies, waits for them, and re-layouts  218 us (33%)
  starting transfers between devices  41 us (6%)
  waiting for transfers between devices  17.7 us (3%)
    reduce_sum x28, other arithmetic, one_block(): (weight * own_part[:, 3, :, None]).sum(1)  347 us
    dynamic_update_slice x216, local copies, waits for them, and re-layouts, shell_sums(): lax.map(one_block, (split_rows(own_cells), split_rows(own_mask), far_stac...  131 us
    ppermute x8, starting transfers between devices, from_behind(): return lax.ppermute(block, axis, route)  20.6 us
    squeeze x28, local copies, waits for them, and re-layouts, shell_sums(): lax.map(one_block, (split_rows(own_cells), split_rows(own_mask), far_stac...  19.7 us
    mul x28, local copies, waits for them, and re-layouts, pair_weights(): jnp.maximum(radius_eff / radius - 1.0, 0.0) * own_mask[:, :, None]  18.8 us
    ppermute x8, waiting for transfers between devices, from_behind(): return lax.ppermute(block, axis, route)  14.6 us
    ppermute x8, starting transfers between devices, shifted(): return lax.ppermute(value, axis, pairs)  13.4 us
  transfers between devices with their start and end apart: 20, of which 5 were waited for; matrix products, arithmetic and copies ran while one was open for 5% of the time, Pallas kernels for 0%

commit v1 on v0

v1 whole, which is shorter than its diff:
```python
import functools

import jax
import jax.numpy as jnp
from jax import lax
from jax.experimental import pallas as pl
from jax.experimental.pallas import tpu as pltpu
from jax.sharding import PartitionSpec as P

ref_density = 268.0825731
min_square = 0.01
far_away = -1024.0
far_norm = 4096.0
reach = 2
offsets = (-2, -1, 1, 2)

smem = pl.BlockSpec(memory_space=pltpu.SMEM)
vmem = pl.BlockSpec(memory_space=pltpu.VMEM)
params = pltpu.CompilerParams(vmem_limit_bytes=58 * 1024 * 1024)


def pack_kernel(dest, where_am_i, blocks, *refs, cells, capacity, domains):
    outs, home, slots, ids = refs[:4], refs[4], refs[5], refs[6]
    me = where_am_i[1]
    groups = len(offsets)

    def clear(k, _):
        for g in range(groups):
            slots[g, k] = 0
            ids[g, k] = -1
        return 0

    lax.fori_loop(0, capacity, clear, 0)

    def sort_block(b, fill):
        target = dest[b]
        owner = target // cells
        rel = (owner - me + reach + domains) % domains
        stays = rel == reach
        group = jnp.where(rel > reach, rel - 1, rel)
        local = target - owner * cells
        slot = jnp.where(
            stays, fill[4], jnp.where(
                group == 0, fill[0], jnp.where(
                    group == 1, fill[1], jnp.where(group == 2, fill[2], fill[3]))))

        @pl.when(stays)
        def _():
            home[local] = blocks[b]

        @pl.when(jnp.logical_not(stays))
        def _():
            slots[group, slot] = b
            ids[group, slot] = local

        moved = jnp.where(stays, 4, group)
        return tuple(fill[g] + jnp.where(moved == g, 1, 0) for g in range(5))

    lax.fori_loop(0, cells, sort_block, (jnp.int32(0),) * 5)
    lane = lax.broadcasted_iota(jnp.int32, (4, 128), 1) + 128 * lax.broadcasted_iota(
        jnp.int32, (4, 128), 0
    )
    for g in range(groups):

        def copy(k, marks, g=g):
            for u in range(8):
                outs[g][k * 8 + u] = blocks[slots[g, k * 8 + u]]
                marks = jnp.where(lane == k * 8 + u, ids[g, k * 8 + u], marks)
            return marks

        marks = lax.fori_loop(0, capacity // 8, copy, jnp.full((4, 128), -1, jnp.int32))
        outs[g][capacity] = marks.astype(jnp.float32)


def place_kernel(*refs, cells, capacity, levels):
    got, stayed, counts = refs[:4], refs[4], refs[5]
    home, to_dom, to_slab, to_up, to_down = refs[6:11]
    kept, marks, sem = refs[11], refs[12], refs[13]
    copies = [
        pltpu.make_async_copy(got[g].at[capacity], marks.at[g], sem.at[g]) for g in range(4)
    ]
    for copy in copies:
        copy.start()

    def keep(k, _):
        for u in range(8):
            kept[k * 8 + u] = stayed[k * 8 + u]
        return 0

    lax.fori_loop(0, cells // 8, keep, 0)
    for copy in copies:
        copy.wait()
    for g in range(4):

        def put(k, _, g=g):
            for u in range(4):
                slot = k * 4 + u
                cell = marks[g, slot // 128, slot % 128].astype(jnp.int32)

                @pl.when(cell >= 0)
                def _():
                    kept[cell] = got[g][slot]
            return 0

        lax.fori_loop(0, capacity // 4, put, 0)
    lane = lax.broadcasted_iota(jnp.int32, (4, 128), 1)
    row = lax.broadcasted_iota(jnp.int32, (4, 128), 0)
    blank = jnp.where(row == 0, far_away, 0.0)

    def finish(z, _):
        for col in range(4):
            cell = col * levels + z
            block = jnp.where(lane < counts[cell], kept[cell], blank)
            home[cell] = block
            if col == 0:
                to_dom[z] = block
                to_slab[z] = block
                to_up[z] = block
            if col == 1:
                to_slab[levels + z] = block
                to_down[z] = block
            if col == 2:
                to_dom[levels + z] = block
        return 0

    lax.fori_loop(0, levels, finish, 0)


def split3(value):
    high = value.astype(jnp.bfloat16).astype(jnp.float32)
    rest = value - high
    mid = rest.astype(jnp.bfloat16).astype(jnp.float32)
    return high, mid, rest - mid


def load_points(raw, first, corner_x, corner_y, level, valid):
    x = raw[pl.ds(first, 8, 4), :]
    y = raw[pl.ds(first + 1, 8, 4), :]
    z = raw[pl.ds(first + 2, 8, 4), :]
    f = raw[pl.ds(first + 3, 8, 4), :]
    if valid is not None:
        x = jnp.where(valid, x, far_away)
        f = jnp.where(valid, f, 0.0)
    rows = lax.broadcasted_iota(jnp.int32, (8, 128), 0) + level
    return x - corner_x, y - corner_y, z - (rows.astype(jnp.float32) + 0.5), f


def make_lanes(raw, base, col, levels, corner_x, corner_y, valid, flat, side, lanes, values):
    span = levels + 2
    zero = jnp.zeros((8, 128), jnp.float32)
    one = jnp.ones((8, 128), jnp.float32)

    def chunk(k, _):
        level = k * 8
        first = pl.multiple_of((base + level) * 4, 32)
        x, y, z, f = load_points(raw, first, corner_x, corner_y, level, valid)
        values[pl.ds(pl.multiple_of(col * (levels + 16) + 8 + level, 8), 8), :] = f
        x3, y3 = split3(x), split3(y)
        rows = []
        for part in (x3, y3):
            rows += [part[0], part[1], part[0], part[1], part[2], part[0]]
        rows += [one, one, one, zero]
        for r, value in enumerate(rows):
            flat[pl.ds(level * 16 + r, 8, 16), :] = value
        flat_norm = x * x + y * y
        for shift in range(3):
            moved = z + float(shift - 1)
            z3 = split3(moved)
            norm = split3(flat_norm + moved * moved)
            rows = [z3[0], z3[1], z3[0], z3[1], z3[2], z3[0], norm[0], norm[1], norm[2]]
            rows += [zero] * 7
            for r, value in enumerate(rows):
                side[shift, pl.ds(level * 16 + r, 8, 16), :] = value
        return 0

    lax.fori_loop(0, levels // 8, chunk, 0)
    rows16 = lax.broadcasted_iota(jnp.int32, (16, 128), 0)
    empty = jnp.where(rows16 == 6, far_norm, 0.0).astype(jnp.bfloat16)
    for edge in (0, levels + 1):
        lanes[0, col * span + edge] = jnp.zeros((16, 128), jnp.bfloat16)
        for shift in range(3):
            lanes[1 + shift, col * span + edge] = empty
    values[pl.ds(col * (levels + 16), 8), :] = zero
    values[pl.ds(col * (levels + 16) + 8 + levels, 8), :] = zero

    def narrow(k, _):
        for u in range(4):
            z = k * 4 + u
            at = pl.multiple_of(z * 16, 16)
            lanes[0, col * span + 1 + z] = flat[pl.ds(at, 16), :].astype(jnp.bfloat16)
            for shift in range(3):
                lanes[1 + shift, col * span + 1 + z] = side[shift, pl.ds(at, 16), :].astype(
                    jnp.bfloat16
                )
        return 0

    lax.fori_loop(0, levels // 4, narrow, 0)


def make_rows(raw, base, row, levels, corner_x, corner_y, tall, lefts, spread):
    zero = jnp.zeros((8, 128), jnp.float32)
    one = jnp.ones((8, 128), jnp.float32)

    def chunk(k, _):
        level = k * 8
        first = pl.multiple_of((base + level) * 4, 32)
        x, y, z, f = load_points(raw, first, corner_x, corner_y, level, None)
        norm = split3(x * x + y * y + z * z)
        parts = []
        for value in (x, y, z):
            high, mid, low = split3(value)
            high, mid, low = -2.0 * high, -2.0 * mid, -2.0 * low
            parts.append([high, high, mid, mid, high, low])
        rows = parts[0] + parts[1] + [norm[0], norm[1], norm[2], zero]
        rows += parts[2] + [one, one, one] + [zero] * 7 + [f]
        for r, value in enumerate(rows):
            tall[pl.ds(level * 40 + r, 8, 40), :] = value
        return 0

    lax.fori_loop(0, levels // 8, chunk, 0)

    def turn(z, _):
        turned = jnp.transpose(tall[pl.ds(pl.multiple_of(z * 40, 8), 40), :])
        lefts[row * levels + z] = turned[:, :32].astype(jnp.bfloat16)
        spread[row * levels + z] = jnp.broadcast_to(turned[:, 32:33], (128, 128))
        return 0

    lax.fori_loop(0, levels, turn, 0)


def pair_sums(tasks, levels, lefts, spread, lanes, values, col_n, col_s, row_n, row_s, half):
    span = levels + 2
    row_n[...] = jnp.zeros_like(row_n)
    row_s[...] = jnp.zeros_like(row_s)
    col_n[...] = jnp.zeros_like(col_n)
    col_s[...] = jnp.zeros_like(col_s)
    groups = half // 8

    def right(z, tile):
        col, shift, _ = tile
        at = col * span + 1 + z + shift
        return jnp.concatenate([lanes[0, at], lanes[2 + shift, at]], axis=0)

    def level_step(z, _):
        mine = lax.broadcasted_iota(jnp.int32, (half, 128), 1) == z
        for row, tiles in tasks:
            total = None
            fields = []
            for col, shift, _ in tiles:
                f = values[pl.ds(col * (levels + 16) + 8 + z + shift, 1), :]
                fields.append(f)
                total = f if total is None else total + f
            for part in range(128 // half):
                left = lefts[row * levels + z, part * half : (part + 1) * half, :]
                own = [
                    spread[row * levels + z, part * half + g * 8 : part * half + g * 8 + 8, :]
                    for g in range(groups)
                ]
                own_sum = functools.reduce(jnp.add, own)
                sums_n = [jnp.full((8, 128), -float(len(tiles)), jnp.float32)] * groups
                sums_s = [jnp.broadcast_to(-total, (8, 128))] * groups
                for t in range(0, len(tiles), 2):
                    pair = tiles[t : t + 2]
                    rights = [right(z, tile) for tile in pair]
                    square = lax.dot_general(
                        left,
                        jnp.concatenate(rights, axis=1) if len(pair) == 2 else rights[0],
                        (((1,), (0,)), ((), ())),
                        preferred_element_type=jnp.float32,
                    )
                    for p, (col, shift, both) in enumerate(pair):
                        f = fields[t + p]
                        down_n = jnp.full((8, 128), -float(groups), jnp.float32)
                        down_s = -own_sum
                        for g in range(groups):
                            w = lax.rsqrt(
                                jnp.minimum(
                                    jnp.maximum(
                                        square[g * 8 : g * 8 + 8, p * 128 : p * 128 + 128],
                                        min_square,
                                    ),
                                    1.0,
                                )
                            )
                            sums_n[g] = sums_n[g] + w
                            sums_s[g] = sums_s[g] + w * f
                            if both:
                                down_n = down_n + w
                                down_s = down_s + w * own[g]
                        if both:
                            at = pl.ds(pl.multiple_of((col * span + 1 + z + shift) * 8, 8), 8)
                            col_n[at, :] += down_n
                            col_s[at, :] += down_s
                for totals, sums in ((row_n, sums_n), (row_s, sums_s)):
                    for g in range(groups):
                        at = slice(part * half + g * 8, part * half + g * 8 + 8)
                        totals[row, at, :] = jnp.where(
                            mine[:8], jnp.sum(sums[g], axis=1, keepdims=True), totals[row, at, :]
                        )
        return 0

    lax.fori_loop(0, levels, level_step, 0)


def fold_column(ref, col, levels):
    base = (col * (levels + 2) + 1) * 8
    total = None
    for k in range(8):
        part = ref[pl.ds(base + k, levels, 8), :]
        total = part if total is None else total + part
    return total


def own_tasks():
    tasks = []
    for row in range(4):
        tiles = [(row, 0, False), (row, 1, True)]
        for col in range(row + 1, 4):
            tiles += [(col, shift, True) for shift in (-1, 0, 1)]
        tasks.append((row, tiles))
    return tasks


def far_tasks():
    wanted = ((0, (0, 1)), (1, (2, 3, 4)), (2, (0, 1, 3, 4, 5)))
    return [
        (row, [(col, shift, True) for col in cols for shift in (-1, 0, 1)])
        for row, cols in wanted
    ]


def own_kernel(position, raw, out_n, out_s, *scratch, levels, half):
    flat, side, lanes, values, tall, lefts, spread, col_n, col_s, row_n, row_s = scratch
    corner_x = (position[2] + 1).astype(jnp.float32)
    corner_y = (position[3] + 1).astype(jnp.float32)
    for col in range(4):
        make_lanes(
            raw, col * levels, col, levels, corner_x, corner_y, None, flat, side, lanes, values
        )
        make_rows(raw, col * levels, col, levels, corner_x, corner_y, tall, lefts, spread)
    pair_sums(
        own_tasks(), levels, lefts, spread, lanes, values, col_n, col_s, row_n, row_s, half
    )
    for col in range(4):
        f = values[pl.ds(col * (levels + 16) + 8, levels), :]
        itself = lax.rsqrt(jnp.maximum(0.0 * f, min_square)) - 1.0
        out_n[col] = jnp.transpose(row_n[col])[:levels] + fold_column(col_n, col, levels) - itself
        out_s[col] = (
            jnp.transpose(row_s[col])[:levels] + fold_column(col_s, col, levels) - itself * f
        )


def far_kernel(position, raw, dom_raw, slab_raw, up_raw, down_raw, *refs, levels, half):
    out_n, out_s, to_dom, to_slab, to_up, to_down = refs[:6]
    flat, side, lanes, values, tall, lefts, spread, col_n, col_s, row_n, row_s = refs[6:]
    corner_x = (position[2] + 1).astype(jnp.float32)
    corner_y = (position[3] + 1).astype(jnp.float32)
    slab, dom, slabs, doms = position[0], position[1], position[4], position[5]
    next_slab = slab + 1 < slabs
    next_dom = dom + 1 < doms
    previous_dom = dom > 0
    sources = (
        (dom_raw, 0, next_dom),
        (dom_raw, levels, next_dom),
        (down_raw, 0, jnp.logical_and(next_slab, previous_dom)),
        (slab_raw, 0, next_slab),
        (slab_raw, levels, next_slab),
        (up_raw, 0, jnp.logical_and(next_slab, next_dom)),
    )
    for col, (source, base, valid) in enumerate(sources):
        make_lanes(
            source, base, col, levels, corner_x, corner_y, valid, flat, side, lanes, values
        )
    for row in range(3):
        make_rows(raw, (row + 1) * levels, row, levels, corner_x, corner_y, tall, lefts, spread)
    pair_sums(
        far_tasks(), levels, lefts, spread, lanes, values, col_n, col_s, row_n, row_s, half
    )
    for row in range(3):
        out_n[row] = jnp.transpose(row_n[row])[:levels]
        out_s[row] = jnp.transpose(row_s[row])[:levels]
    for channel, ref in enumerate((col_n, col_s)):
        for k in range(2):
            to_dom[channel, k] = fold_column(ref, k, levels)
            to_slab[channel, k] = fold_column(ref, 3 + k, levels)
        to_down[channel] = fold_column(ref, 2, levels)
        to_up[channel] = fold_column(ref, 5, levels)


def finish_kernel(counts, raw, own_n, own_s, far_n, far_s, *refs, levels):
    from_dom, from_slab, from_up, from_down, density, laplace = refs
    lane = lax.broadcasted_iota(jnp.int32, (levels, 128), 1)
    for col in range(4):
        sums = []
        for channel, (near, far) in enumerate(((own_n, far_n), (own_s, far_s))):
            total = near[col]
            if col > 0:
                total = total + far[col - 1]
            if col in (0, 2):
                total = total + from_dom[channel, col // 2]
            if col in (0, 1):
                total = total + from_slab[channel, col]
            if col == 0:
                total = total + from_up[channel]
            if col == 1:
                total = total + from_down[channel]
            sums.append(total)
        filled = lane < counts[col]
        n = jnp.where(filled, sums[0], 0.0)
        s = jnp.where(filled, sums[1], 0.0)
        f = raw[pl.ds(col * levels * 4 + 3, levels, 4), :]
        density[col] = n / ref_density
        laplace[col] = (s - f * n) / ref_density


def scratch_for(levels, cols, rows):
    span = levels + 2
    f32, bf16 = jnp.float32, jnp.bfloat16
    return [
        pltpu.VMEM((levels * 16, 128), f32),
        pltpu.VMEM((3, levels * 16, 128), f32),
        pltpu.VMEM((4, cols * span, 16, 128), bf16),
        pltpu.VMEM((cols * (levels + 16), 128), f32),
        pltpu.VMEM((levels * 40, 128), f32),
        pltpu.VMEM((rows * levels, 128, 32), bf16),
        pltpu.VMEM((rows * levels, 128, 128), f32),
        pltpu.VMEM((cols * span * 8, 128), f32),
        pltpu.VMEM((cols * span * 8, 128), f32),
        pltpu.VMEM((rows, 128, 128), f32),
        pltpu.VMEM((rows, 128, 128), f32),
    ]


def local(incoming, dest, counts):
    cells_x, cells_y, levels = counts.shape
    slots = incoming.shape[3]
    cells = cells_x * cells_y * levels
    capacity = cells // 4
    slabs, doms = lax.axis_size("slab"), lax.axis_size("dom")
    slab, dom = lax.axis_index("slab"), lax.axis_index("dom")
    assert (cells_x, cells_y, slots) == (2, 2, 128) and levels % 8 == 0 and levels <= 128
    assert capacity % 8 == 0 and capacity <= 512 and doms >= 5
    f32 = jnp.float32
    shape = jax.ShapeDtypeStruct
    position = jnp.stack(
        [slab, dom, slab * cells_x, dom * cells_y, jnp.int32(slabs), jnp.int32(doms)]
    ).astype(jnp.int32)
    blocks = incoming.reshape(cells, 4, slots)
    flat_counts = counts.reshape(cells)
    block_bytes = 4 * slots * 4
    *packs, stayed = pl.pallas_call(
        functools.partial(pack_kernel, cells=cells, capacity=capacity, domains=doms),
        out_shape=[shape((capacity + 1, 4, slots), f32)] * 4 + [shape((cells, 4, slots), f32)],
        in_specs=[smem, smem, vmem],
        out_specs=[vmem] * 5,
        scratch_shapes=[pltpu.SMEM((4, capacity), jnp.int32), pltpu.SMEM((4, capacity), jnp.int32)],
        compiler_params=params,
        name="pack",
    )(dest.reshape(cells), position, blocks)
    got = [
        lax.ppermute(pack, "dom", [(i, (i + step) % doms) for i in range(doms)])
        for step, pack in zip(offsets, packs)
    ]
    column = (levels, 4, slots)
    home, to_dom, to_slab, to_up, to_down = pl.pallas_call(
        functools.partial(place_kernel, cells=cells, capacity=capacity, levels=levels),
        out_shape=[shape((cells, 4, slots), f32)]
        + [shape((2 * levels, 4, slots), f32)] * 2
        + [shape(column, f32)] * 2,
        in_specs=[vmem] * 5 + [smem],
        out_specs=[vmem] * 5,
        scratch_shapes=[
            pltpu.VMEM((cells, 4, slots), f32),
            pltpu.SMEM((4, 4, slots), f32),
            pltpu.SemaphoreType.DMA((4,)),
        ],
        compiler_params=params,
        name="place",
    )(*got, stayed, flat_counts)

    both = ("slab", "dom")

    def route(step_slab, step_dom):
        pairs = []
        for s in range(slabs):
            for d in range(doms):
                if 0 <= s + step_slab < slabs and 0 <= d + step_dom < doms:
                    pairs.append((s * doms + d, (s + step_slab) * doms + d + step_dom))
        return pairs

    def send(value, step_slab, step_dom):
        return lax.ppermute(value, both, route(step_slab, step_dom))

    def rows_of(value):
        return value.reshape(-1, slots)

    slab_raw = send(to_slab, -1, 0)
    dom_raw = send(to_dom, 0, -1)
    up_raw = send(to_up, -1, -1)
    down_raw = send(to_down, -1, 1)
    raw = rows_of(home)
    half = 64
    plane = (4, levels, slots)
    tile_flops = 2 * 128 * 128 * 32
    own_n, own_s = pl.pallas_call(
        functools.partial(own_kernel, levels=levels, half=half),
        out_shape=[shape(plane, f32)] * 2,
        in_specs=[smem, vmem],
        out_specs=[vmem] * 2,
        scratch_shapes=scratch_for(levels, 4, 4),
        compiler_params=params,
        cost_estimate=pl.CostEstimate(
            flops=1000 * levels * tile_flops, bytes_accessed=cells * block_bytes, transcendentals=0
        ),
        name="own",
    )(position, raw)
    far_n, far_s, ret_dom, ret_slab, ret_up, ret_down = pl.pallas_call(
        functools.partial(far_kernel, levels=levels, half=half),
        out_shape=[shape((3, levels, slots), f32)] * 2
        + [shape((2, 2, levels, slots), f32)] * 2
        + [shape((2, levels, slots), f32)] * 2,
        in_specs=[smem] + [vmem] * 5,
        out_specs=[vmem] * 6,
        scratch_shapes=scratch_for(levels, 6, 3),
        compiler_params=params,
        name="far",
    )(position, raw, rows_of(dom_raw), rows_of(slab_raw), rows_of(up_raw), rows_of(down_raw))
    from_slab = send(ret_slab, 1, 0)
    from_dom = send(ret_dom, 0, 1)
    from_up = send(ret_up, 1, 1)
    from_down = send(ret_down, 1, -1)
    wide_counts = jnp.broadcast_to(counts.reshape(4, levels, 1), plane)
    density, laplace = pl.pallas_call(
        functools.partial(finish_kernel, levels=levels),
        out_shape=[shape(plane, f32)] * 2,
        in_specs=[vmem] * 10,
        out_specs=[vmem] * 2,
        compiler_params=params,
        name="finish",
    )(wide_counts, raw, own_n, own_s, far_n, far_s, from_dom, from_slab, from_up, from_down)
    final = (cells_x, cells_y, levels, slots)
    return density.reshape(final), laplace.reshape(final)


def solution(mesh):
    in_specs = (P("slab", "dom", None, None), P("slab", "dom"), P("slab", "dom", None))
    out_specs = (P("slab", "dom", None, None), P("slab", "dom", None, None))
    return jax.shard_map(local, mesh=mesh, in_specs=in_specs, out_specs=out_specs, check_vma=False)
```

time: 652 us -> 265 us (0.41)
  other arithmetic: 367 us -> 0 us
  Pallas kernels: 0 us -> 217 us
  local copies, waits for them, and re-layouts: 218 us -> 3.62 us
  starting transfers between devices: 41 us -> 23 us
    reduce_sum x28 -> x0, other arithmetic: 347 us -> none  [one_block(): (weight * own_part[:, 3, :, None]).sum(1)]
    pallas_call x0 -> x5, Pallas kernels: none -> 217 us  [the longest x1 97.4 us: local(): pl.pallas_call(functools.partial(own_kernel, levels=levels, half=half), o...]
    dynamic_update_slice x216 -> x0, local copies, waits for them, and re-layouts: 131 us -> none  [shell_sums(): lax.map(one_block, (split_rows(own_cells), split_rows(own_mask), far_stac...]
    squeeze x34 -> x0, local copies, waits for them, and re-layouts: 19.7 us -> none  [the longest x28 19.7 us: shell_sums(): lax.map(one_block, (split_rows(own_cells), split_rows(own_mask), far_stac...]
    mul x80 -> x0, local copies, waits for them, and re-layouts: 19.4 us -> none  [the longest x28 18.8 us: pair_weights(): jnp.maximum(radius_eff / radius - 1.0, 0.0) * own_mask[:, :, None]]
    ppermute x20 -> x12, starting transfers between devices: 41 us -> 23 us  [the longest x8 16.7 us: send(): return lax.ppermute(value, both, route(step_slab, step_dom))]
    scatter-add x49 -> x0, local copies, waits for them, and re-layouts: 17.6 us -> none  [the longest x14 4.95 us: local(): sum_n.at[start_x:start_x + cells_x, 1:1 + cells_y, 1:1 + cells_z]]
    scatter x9 -> x0, local copies, waits for them, and re-layouts: 14.3 us -> none  [the longest x4 6.41 us: local(): jnp.zeros((capacity + 1, channels), jnp.float32).at[slot_ids].set(blocks)]
  transfers between devices with their start and end apart: 20 -> 12, of which waited for: 5 -> 5; matrix products, arithmetic and copies ran while one was open for 5% -> 0% of each run, Pallas kernels for 0% -> 37%
where the time goes in v1:
time: 265 us; the launch traced here: 263 us
  Pallas kernels  217 us (82%)
  starting transfers between devices  23 us (9%)
  waiting for transfers between devices  19.3 us (7%)
  local copies, waits for them, and re-layouts  3.62 us (1%)
    pallas_call x1, Pallas kernels, local(): pl.pallas_call(functools.partial(own_kernel, levels=levels, half=half), o...  97.4 us
    pallas_call x1, Pallas kernels, local(): pl.pallas_call(functools.partial(far_kernel, levels=levels, half=half), o...  96 us
    ppermute x8, starting transfers between devices, send(): return lax.ppermute(value, both, route(step_slab, step_dom))  16.7 us
    ppermute x8, waiting for transfers between devices, send(): return lax.ppermute(value, both, route(step_slab, step_dom))  12.2 us
    pallas_call x1, Pallas kernels, local(): pl.pallas_call(functools.partial(pack_kernel, cells=cells, capacity=capac...  12.2 us
    pallas_call x1, Pallas kernels, local(): pl.pallas_call(functools.partial(place_kernel, cells=cells, capacity=capa...  8.81 us
    ppermute x4, waiting for transfers between devices, local(): lax.ppermute(pack, 'dom', [(i, (i + step) % doms) for i in range(doms)])  7.06 us
    ppermute x4, starting transfers between devices, local(): lax.ppermute(pack, 'dom', [(i, (i + step) % doms) for i in range(doms)])  6.27 us
  transfers between devices with their start and end apart: 12, of which 5 were waited for; matrix products, arithmetic and copies ran while one was open for 0% of the time, Pallas kernels for 37%

profile of v1, /device:TPU:0, one launch (start us, length us, event | category | flops | bytes accessed | tf_op | source)
XLA Modules:
  0.0 263.3 jit_solution(487262351407541924)
XLA Ops:
  0.6 0.7 stack.19.where_am_i.position
  1.3 12.2 %pack.1 = (f32[65,4,128]{2,1,0:T(4,128)}, f32[65,4,128]{2,1,0:T(4,128)}, f32[65,4,128]{2,1,0:T(4,128)}, f32[65,4,128]{2,1,0:T(4,128)}, f32[256,4,128]{2,1,0:T(4,128)}) custom-call(s32[256]{0:T(256)} %bitcast.23, s32[6]{0:T(128)} %stack.19.where_am_i.position, f32[256,4,128]{2,1,0:T(4,128)} %bitcast.17), custom_call_target="tpu_custom_call" | custom-call | tf_op jit(solution)/shard_map/pack/pallas_call | solution.py:451
  13.5 5.1 %collective-permute-start = (f32[65,4,128]{2,1,0:T(4,128)}, f32[65,4,128]{2,1,0:T(4,128)S(1)}, u32[]{:S(2)}, u32[]{:S(2)}) collective-permute-start(f32[65,4,128]{2,1,0:T(4,128)} %get-tuple-element.22), channel_id=1, source_target_pairs={{0,6},{1,7},{2,0},{3,1},{4,2},{5,3},{6,4},{7,5},{8,14},{9,15},{10,... | collective-permute-start | bytes 399368 | tf_op jit(solution)/shard_map/ppermute | solution.py:461
  18.6 0.0 collective-permute-start.1
  18.6 0.5 collective-permute-start.2
  19.1 0.7 collective-permute-start.3
  19.8 0.0 copy-done.12
  19.8 0.7 reshape.38.refs_5_
  20.5 2.4 collective-permute-done.refs_0_
  22.8 2.9 %collective-permute-done.1.refs_1_ = f32[65,4,128]{2,1,0:T(4,128)S(1)} collective-permute-done((f32[65,4,128]{2,1,0:T(4,128)}, f32[65,4,128]{2,1,0:T(4,128)S(1)}, u32[]{:S(2)}, u32[]{:S(2)}) %collective-permute-start.1) | collective-permute-done | bytes 133152 | tf_op jit(solution)/shard_map/ppermute | solution.py:461
  25.7 0.3 collective-permute-done.2.refs_2_
  26.0 1.5 collective-permute-done.3.refs_3_
  27.5 0.0 copy-done.2
  27.5 0.0 copy-done.3
  27.5 0.0 copy-done.4
  27.5 0.7 copy-done.5
  28.2 8.8 %place.1 = (f32[256,4,128]{2,1,0:T(4,128)}, f32[128,4,128]{2,1,0:T(4,128)}, f32[128,4,128]{2,1,0:T(4,128)}, f32[64,4,128]{2,1,0:T(4,128)}, f32[64,4,128]{2,1,0:T(4,128)}) custom-call(f32[65,4,128]{2,1,0:T(4,128)} %copy-done.2, f32[65,4,128]{2,1,0:T(4,128)} %copy-done.3, f32[65,4,128]{2,1,0:T(4,128)} %copy-done.4, f32[65,4,128]{2,1,0:T(4,128)} %copy-done.5, ...), custom_call_target="tpu_custom_call" | custom-call | tf_op jit(solution)/shard_map/place/pallas_call | solution.py:465
  37.0 1.3 collective-permute-start.4
  38.3 1.3 collective-permute-start.5
  39.6 1.3 collective-permute-start.6
  40.9 0.7 collective-permute-start.7
  41.6 12.2 %collective-permute-done.6 = f32[64,4,128]{2,1,0:T(4,128)S(1)} collective-permute-done((f32[64,4,128]{2,1,0:T(4,128)}, f32[64,4,128]{2,1,0:T(4,128)S(1)}, u32[]{:S(2)}, u32[]{:S(2)}) %collective-permute-start.6) | collective-permute-done | bytes 131104 | tf_op jit(solution)/shard_map/ppermute | solution.py:492
  53.8 0.0 collective-permute-done.7
  53.8 0.0 collective-permute-done.4
  53.8 0.0 copy-start
  53.8 0.0 collective-permute-done.5
  53.8 0.0 copy-start.1
  53.9 0.6 copy-done.8
  54.5 0.0 copy-done.9
  54.5 0.1 copy-done
  54.6 0.1 copy-done.1
  54.7 96.0 %far.1 = (f32[3,64,128]{2,1,0:T(8,128)}, f32[3,64,128]{2,1,0:T(8,128)}, f32[2,2,64,128]{3,2,1,0:T(8,128)}, f32[2,2,64,128]{3,2,1,0:T(8,128)}, f32[2,64,128]{2,1,0:T(8,128)}, /*index=5*/f32[2,64,128]{2,1,0:T(8,128)}) custom-call(s32[6]{0:T(128)} %stack.19.where_am_i.position, f32[1024,128]{1,0:T(8,128)} %bitcast.14, f32[512,128]{1,0:T(8,128)} %bitcast.18, ...), custom_call_target="tpu_custom_call" | custom-call | tf_op jit(solution)/shard_map/far/pallas_call | solution.py:517
  150.7 1.8 collective-permute-start.8
  152.5 4.2 %collective-permute-start.9 = (f32[2,2,64,128]{3,2,1,0:T(8,128)}, f32[2,2,64,128]{3,2,1,0:T(8,128)S(1)}, u32[]{:S(2)}, u32[]{:S(2)}) collective-permute-start(f32[2,2,64,128]{3,2,1,0:T(8,128)} %get-tuple-element.37), channel_id=1, source_target_pairs={{0,8},{1,9},{2,10},{3,11},{4,12},{5,13},{6,14},{7,15},{8,16},{9,17... | collective-permute-start | bytes 393224 | tf_op jit(solution)/shard_map/ppermute | solution.py:492
  156.8 5.5 %collective-permute-start.10 = (f32[2,64,128]{2,1,0:T(8,128)}, f32[2,64,128]{2,1,0:T(8,128)S(1)}, u32[]{:S(2)}, u32[]{:S(2)}) collective-permute-start(f32[2,64,128]{2,1,0:T(8,128)} %get-tuple-element.38), channel_id=1, source_target_pairs={{0,9},{1,10},{2,11},{3,12},{4,13},{5,14},{6,15},{8,17},{9,18},{10,... | collective-permute-start | bytes 196616 | tf_op jit(solution)/shard_map/ppermute | solution.py:492
  162.3 0.7 collective-permute-start.11
  162.9 97.4 %own.1 = (f32[4,64,128]{2,1,0:T(8,128)}, f32[4,64,128]{2,1,0:T(8,128)}) custom-call(s32[6]{0:T(128)} %stack.19.where_am_i.position, f32[1024,128]{1,0:T(8,128)} %bitcast.15), custom_call_target="tpu_custom_call" | custom-call | flops 67108864000 | bytes 524288 | tf_op jit(solution)/shard_map/own/pallas_call | solution.py:505
  260.4 0.0 collective-permute-done.10.refs_2_
  260.4 0.0 collective-permute-done.11.refs_3_
  260.4 0.0 copy-start.11
  260.4 0.0 collective-permute-done.8.refs_0_
  260.4 0.0 copy-start.6
  260.4 0.0 collective-permute-done.9.refs_1_
  260.4 0.0 copy-start.7
  260.5 0.8 broadcast_in_dim.8.counts
  261.2 0.0 copy-done.10
  261.2 0.0 copy-done.11
  261.2 2.0 finish.1
  (10 shorter events, 0.0 us)
Async XLA Ops:
  13.5 9.3 %collective-permute-start = (f32[65,4,128]{2,1,0:T(4,128)}, f32[65,4,128]{2,1,0:T(4,128)S(1)}, u32[]{:S(2)}, u32[]{:S(2)}) collective-permute-start(f32[65,4,128]{2,1,0:T(4,128)} %get-tuple-element.22), channel_id=1, source_target_pairs={{0,6},{1,7},{2,0},{3,1},{4,2},{5,3},{6,4},{7,5},{8,14},{9,15},{10,... | collective-permute-start | bytes 399368 | tf_op jit(solution)/shard_map/ppermute | solution.py:461
  18.6 1.2 copy-start.12
  18.6 7.1 %collective-permute-start.1 = (f32[65,4,128]{2,1,0:T(4,128)}, f32[65,4,128]{2,1,0:T(4,128)S(1)}, u32[]{:S(2)}, u32[]{:S(2)}) collective-permute-start(f32[65,4,128]{2,1,0:T(4,128)} %get-tuple-element.23), channel_id=1, source_target_pairs={{0,7},{1,0},{2,1},{3,2},{4,3},{5,4},{6,5},{7,6},{8,15},{9,8},{10,9... | collective-permute-start | bytes 399368 | tf_op jit(solution)/shard_map/ppermute | solution.py:461
  18.6 7.4 %collective-permute-start.2 = (f32[65,4,128]{2,1,0:T(4,128)}, f32[65,4,128]{2,1,0:T(4,128)S(1)}, u32[]{:S(2)}, u32[]{:S(2)}) collective-permute-start(f32[65,4,128]{2,1,0:T(4,128)} %get-tuple-element.24), channel_id=1, source_target_pairs={{0,1},{1,2},{2,3},{3,4},{4,5},{5,6},{6,7},{7,0},{8,9},{9,10},{10,1... | collective-permute-start | bytes 399368 | tf_op jit(solution)/shard_map/ppermute | solution.py:461
  19.1 8.4 %collective-permute-start.3 = (f32[65,4,128]{2,1,0:T(4,128)}, f32[65,4,128]{2,1,0:T(4,128)S(1)}, u32[]{:S(2)}, u32[]{:S(2)}) collective-permute-start(f32[65,4,128]{2,1,0:T(4,128)} %get-tuple-element.25), channel_id=1, source_target_pairs={{0,2},{1,3},{2,4},{3,5},{4,6},{5,7},{6,0},{7,1},{8,10},{9,11},{10,... | collective-permute-start | bytes 399368 | tf_op jit(solution)/shard_map/ppermute | solution.py:461
  22.8 4.7 %copy-start.2 = (f32[65,4,128]{2,1,0:T(4,128)}, f32[65,4,128]{2,1,0:T(4,128)S(1)}, u32[]{:S(2)}) copy-start(f32[65,4,128]{2,1,0:T(4,128)S(1)} %collective-permute-done.refs_0_) | copy-start | bytes 399364
  25.7 1.8 copy-start.3
  26.0 1.5 copy-start.4
  27.5 0.7 copy-start.5
  37.0 16.8 %collective-permute-start.4 = (f32[128,4,128]{2,1,0:T(4,128)}, f32[128,4,128]{2,1,0:T(4,128)S(1)}, u32[]{:S(2)}, u32[]{:S(2)}) collective-permute-start(f32[128,4,128]{2,1,0:T(4,128)} %get-tuple-element.30), channel_id=1, source_target_pairs={{1,0},{2,1},{3,2},{4,3},{5,4},{6,5},{7,6},{9,8},{10,9},{11,10},{12... | collective-permute-start | bytes 786440 | tf_op jit(solution)/shard_map/ppermute | solution.py:492
  38.3 15.5 %collective-permute-start.5 = (f32[128,4,128]{2,1,0:T(4,128)}, f32[128,4,128]{2,1,0:T(4,128)S(1)}, u32[]{:S(2)}, u32[]{:S(2)}) collective-permute-start(f32[128,4,128]{2,1,0:T(4,128)} %get-tuple-element.31), channel_id=1, source_target_pairs={{8,0},{9,1},{10,2},{11,3},{12,4},{13,5},{14,6},{15,7},{16,8},{17,9... | collective-permute-start | bytes 786440 | tf_op jit(solution)/shard_map/ppermute | solution.py:492
  39.6 14.2 %collective-permute-start.6 = (f32[64,4,128]{2,1,0:T(4,128)}, f32[64,4,128]{2,1,0:T(4,128)S(1)}, u32[]{:S(2)}, u32[]{:S(2)}) collective-permute-start(f32[64,4,128]{2,1,0:T(4,128)} %get-tuple-element.32), channel_id=1, source_target_pairs={{9,0},{10,1},{11,2},{12,3},{13,4},{14,5},{15,6},{17,8},{18,9},{19,... | collective-permute-start | bytes 393224 | tf_op jit(solution)/shard_map/ppermute | solution.py:492
  40.9 12.9 %collective-permute-start.7 = (f32[64,4,128]{2,1,0:T(4,128)}, f32[64,4,128]{2,1,0:T(4,128)S(1)}, u32[]{:S(2)}, u32[]{:S(2)}) collective-permute-start(f32[64,4,128]{2,1,0:T(4,128)} %get-tuple-element.33), channel_id=1, source_target_pairs={{8,1},{9,2},{10,3},{11,4},{12,5},{13,6},{14,7},{16,9},{17,10},{18,... | collective-permute-start | bytes 393224 | tf_op jit(solution)/shard_map/ppermute | solution.py:492
  53.8 0.7 copy-start.8
  53.8 0.7 copy-start.9
  53.8 0.8 copy-start
  53.8 0.9 copy-start.1
  150.7 109.7 %collective-permute-start.8 = (f32[2,2,64,128]{3,2,1,0:T(8,128)}, f32[2,2,64,128]{3,2,1,0:T(8,128)S(1)}, u32[]{:S(2)}, u32[]{:S(2)}) collective-permute-start(f32[2,2,64,128]{3,2,1,0:T(8,128)} %get-tuple-element.36), channel_id=1, source_target_pairs={{0,1},{1,2},{2,3},{3,4},{4,5},{5,6},{6,7},{8,9},{9,10},{10,11},{11... | collective-permute-start | bytes 393224 | tf_op jit(solution)/shard_map/ppermute | solution.py:492
  152.5 107.9 %collective-permute-start.9 = (f32[2,2,64,128]{3,2,1,0:T(8,128)}, f32[2,2,64,128]{3,2,1,0:T(8,128)S(1)}, u32[]{:S(2)}, u32[]{:S(2)}) collective-permute-start(f32[2,2,64,128]{3,2,1,0:T(8,128)} %get-tuple-element.37), channel_id=1, source_target_pairs={{0,8},{1,9},{2,10},{3,11},{4,12},{5,13},{6,14},{7,15},{8,16},{9,17... | collective-permute-start | bytes 393224 | tf_op jit(solution)/shard_map/ppermute | solution.py:492
  156.8 103.6 %collective-permute-start.10 = (f32[2,64,128]{2,1,0:T(8,128)}, f32[2,64,128]{2,1,0:T(8,128)S(1)}, u32[]{:S(2)}, u32[]{:S(2)}) collective-permute-start(f32[2,64,128]{2,1,0:T(8,128)} %get-tuple-element.38), channel_id=1, source_target_pairs={{0,9},{1,10},{2,11},{3,12},{4,13},{5,14},{6,15},{8,17},{9,18},{10,... | collective-permute-start | bytes 196616 | tf_op jit(solution)/shard_map/ppermute | solution.py:492
  162.3 98.1 %collective-permute-start.11 = (f32[2,64,128]{2,1,0:T(8,128)}, f32[2,64,128]{2,1,0:T(8,128)S(1)}, u32[]{:S(2)}, u32[]{:S(2)}) collective-permute-start(f32[2,64,128]{2,1,0:T(8,128)} %get-tuple-element.39), channel_id=1, source_target_pairs={{1,8},{2,9},{3,10},{4,11},{5,12},{6,13},{7,14},{9,16},{10,17},{11,... | collective-permute-start | bytes 196616 | tf_op jit(solution)/shard_map/ppermute | solution.py:492
  260.4 0.8 copy-start.10
  260.4 0.8 copy-start.11
  260.4 0.8 copy-start.6
  260.4 0.8 copy-start.7

commit v2 on v1

v2 whole, which is shorter than its diff:
```python
import functools

import jax
import jax.numpy as jnp
from jax import lax
from jax.experimental import pallas as pl
from jax.experimental.pallas import tpu as pltpu
from jax.sharding import PartitionSpec as P

ref_density = 268.0825731
min_square = 0.01
far_away = -1024.0
far_norm = 4096.0
reach = 2
offsets = (-2, -1, 1, 2)

smem = pl.BlockSpec(memory_space=pltpu.SMEM)
vmem = pl.BlockSpec(memory_space=pltpu.VMEM)
params = pltpu.CompilerParams(vmem_limit_bytes=58 * 1024 * 1024)


def pack_kernel(dest, blocks, *refs, cells, capacity, domains):
    outs, home, sorted_blocks, spots, places, sem = refs[:4], *refs[4:9]
    me = lax.axis_index("dom")
    rows = cells // 128
    target = dest[...]
    spot = jnp.zeros((rows, 128), jnp.int32)
    local = jnp.zeros((rows, 128), jnp.int32)
    lane = lax.broadcasted_iota(jnp.int32, (128, 128), 1)
    row = lax.broadcasted_iota(jnp.int32, (128, 128), 0)
    before = jnp.where(row < lane, 1.0, 0.0).astype(jnp.bfloat16)
    whole = jnp.ones((128, 128), jnp.bfloat16)
    for g, step in enumerate(offsets + (0,)):
        owner = lax.rem(me + step + domains, domains)
        within = target - owner * cells
        chosen = jnp.logical_and(within >= 0, within < cells)
        local = jnp.where(chosen, within, local)
        if step == 0:
            rank = within
        else:
            ones = jnp.concatenate(
                [jnp.where(chosen, 1.0, 0.0), jnp.zeros((16 - rows, 128), jnp.float32)], 0
            ).astype(jnp.bfloat16)
            inside = jnp.dot(ones, before, preferred_element_type=jnp.float32)[:rows]
            counted = jnp.dot(ones, whole, preferred_element_type=jnp.float32)[:rows]
            earlier = [jnp.zeros((1, 128), jnp.float32)]
            for r in range(rows - 1):
                earlier.append(earlier[-1] + counted[r : r + 1])
            rank = (inside + jnp.concatenate(earlier, 0)).astype(jnp.int32)
        spot = jnp.where(chosen, g * capacity + rank, spot)
    spots[...] = spot
    copy = pltpu.make_async_copy(spots, places, sem)
    copy.start()
    high = jnp.floor((local + 1).astype(jnp.float32) * (1.0 / 128.0))
    low = (local + 1).astype(jnp.float32) - 128.0 * high
    filler = jnp.zeros((7, 128), jnp.float32)
    sent = 4 * capacity
    marks = [jnp.zeros((8, sent), jnp.float32)] * 2
    slot = lax.broadcasted_iota(jnp.int32, (sent, 128), 0)
    for r in range(rows):
        hit = jnp.where(slot == spot[r : r + 1], 1.0, 0.0).astype(jnp.bfloat16)
        for k, value in enumerate((high, low)):
            marks[k] = marks[k] + lax.dot_general(
                jnp.concatenate([value[r : r + 1], filler], 0).astype(jnp.bfloat16),
                hit,
                (((1,), (1,)), ((), ())),
                preferred_element_type=jnp.float32,
            )
    marks = (128.0 * marks[0] + marks[1])[:1]
    copy.wait()

    def move(k, _):
        for u in range(16):
            b = k * 16 + u
            sorted_blocks[places[b // 128, lax.rem(b, 128)]] = blocks[b]
        return 0

    lax.fori_loop(0, cells // 16, move, 0)
    for g in range(4):
        for k in range(0, capacity, 8):
            outs[g][k : k + 8] = sorted_blocks[g * capacity + k : g * capacity + k + 8]
        for r in range(4):
            at = min(r * 128, sent - 128)
            outs[g][capacity, r : r + 1] = marks[:, at : at + 128]
    home[...] = sorted_blocks[4 * capacity :]


def place_kernel(*refs, cells, capacity, levels):
    got, stayed, counts = refs[:4], refs[4], refs[5]
    home, to_dom, to_slab, to_up, to_down = refs[6:11]
    kept, cell_ids, marks, sem = refs[11:]
    for g in range(4):
        sent = got[g][capacity].astype(jnp.int32) - 1
        cell_ids[g] = jnp.where(sent < 0, cells, sent)
    copy = pltpu.make_async_copy(cell_ids, marks, sem)
    copy.start()
    kept[:cells] = stayed[...]
    copy.wait()
    for g in range(4):

        def put(k, _, g=g):
            for u in range(8):
                slot = k * 8 + u
                spot = g * capacity + slot
                kept[marks[g, spot // 128, lax.rem(spot, 128)]] = got[g][slot]
            return 0

        lax.fori_loop(0, capacity // 8, put, 0)
    lane = lax.broadcasted_iota(jnp.int32, (4, 128), 1)
    row = lax.broadcasted_iota(jnp.int32, (4, 128), 0)
    blank = jnp.where(row == 0, far_away, 0.0)

    def finish(k, _):
        for u in range(4):
            z = k * 4 + u
            for col in range(4):
                cell = col * levels + z
                block = jnp.where(lane < counts[col // 2, col % 2, z], kept[cell], blank)
                home[cell] = block
                if col == 0:
                    to_dom[z] = block
                    to_slab[z] = block
                    to_up[z] = block
                if col == 1:
                    to_slab[levels + z] = block
                    to_down[z] = block
                if col == 2:
                    to_dom[levels + z] = block
        return 0

    lax.fori_loop(0, levels // 4, finish, 0)


def split3(value):
    high = value.astype(jnp.bfloat16).astype(jnp.float32)
    rest = value - high
    mid = rest.astype(jnp.bfloat16).astype(jnp.float32)
    return high, mid, rest - mid


def load_points(raw, first, corner_x, corner_y, level, valid):
    x = raw[pl.ds(first, 8, 4), :]
    y = raw[pl.ds(first + 1, 8, 4), :]
    z = raw[pl.ds(first + 2, 8, 4), :]
    f = raw[pl.ds(first + 3, 8, 4), :]
    if valid is not None:
        x = jnp.where(valid, x, far_away)
        f = jnp.where(valid, f, 0.0)
    rows = lax.broadcasted_iota(jnp.int32, (8, 128), 0) + level
    return x - corner_x, y - corner_y, z - (rows.astype(jnp.float32) + 0.5), f


def make_lanes(raw, base, col, levels, corner_x, corner_y, valid, flat, side, lanes, values):
    span = levels + 2
    zero = jnp.zeros((8, 128), jnp.float32)
    one = jnp.ones((8, 128), jnp.float32)

    def chunk(k, _):
        level = k * 8
        first = pl.multiple_of((base + level) * 4, 32)
        x, y, z, f = load_points(raw, first, corner_x, corner_y, level, valid)
        values[pl.ds(pl.multiple_of(col * (levels + 16) + 8 + level, 8), 8), :] = f
        x3, y3 = split3(x), split3(y)
        rows = []
        for part in (x3, y3):
            rows += [part[0], part[1], part[0], part[1], part[2], part[0]]
        rows += [one, one, one, zero]
        for r, value in enumerate(rows):
            flat[pl.ds(level * 16 + r, 8, 16), :] = value
        flat_norm = x * x + y * y
        for shift in range(3):
            moved = z + float(shift - 1)
            z3 = split3(moved)
            norm = split3(flat_norm + moved * moved)
            rows = [z3[0], z3[1], z3[0], z3[1], z3[2], z3[0], norm[0], norm[1], norm[2]]
            rows += [zero] * 7
            for r, value in enumerate(rows):
                side[shift, pl.ds(level * 16 + r, 8, 16), :] = value
        return 0

    lax.fori_loop(0, levels // 8, chunk, 0)
    rows16 = lax.broadcasted_iota(jnp.int32, (16, 128), 0)
    empty = jnp.where(rows16 == 6, far_norm, 0.0).astype(jnp.bfloat16)
    for edge in (0, levels + 1):
        lanes[0, col * span + edge] = jnp.zeros((16, 128), jnp.bfloat16)
        for shift in range(3):
            lanes[1 + shift, col * span + edge] = empty
    values[pl.ds(col * (levels + 16), 8), :] = zero
    values[pl.ds(col * (levels + 16) + 8 + levels, 8), :] = zero

    def narrow(k, _):
        for u in range(4):
            z = k * 4 + u
            at = pl.multiple_of(z * 16, 16)
            lanes[0, col * span + 1 + z] = flat[pl.ds(at, 16), :].astype(jnp.bfloat16)
            for shift in range(3):
                lanes[1 + shift, col * span + 1 + z] = side[shift, pl.ds(at, 16), :].astype(
                    jnp.bfloat16
                )
        return 0

    lax.fori_loop(0, levels // 4, narrow, 0)


def make_rows(raw, base, row, levels, corner_x, corner_y, tall, lefts):
    zero = jnp.zeros((8, 128), jnp.float32)
    one = jnp.ones((8, 128), jnp.float32)

    def chunk(k, _):
        level = k * 8
        first = pl.multiple_of((base + level) * 4, 32)
        x, y, z, f = load_points(raw, first, corner_x, corner_y, level, None)
        norm = split3(x * x + y * y + z * z)
        parts = []
        for value in (x, y, z):
            high, mid, low = split3(value)
            high, mid, low = -2.0 * high, -2.0 * mid, -2.0 * low
            parts.append([high, high, mid, mid, high, low])
        rows = parts[0] + parts[1] + [norm[0], norm[1], norm[2], zero]
        rows += parts[2] + [one, one, one] + list(split3(f)) + [zero] * 4
        for r, value in enumerate(rows):
            tall[pl.ds(level * 32 + r, 8, 32), :] = value
        return 0

    lax.fori_loop(0, levels // 8, chunk, 0)

    def narrow(k, _):
        for u in range(4):
            z = k * 4 + u
            lefts[row * levels + z] = tall[pl.ds(pl.multiple_of(z * 32, 32), 32), :].astype(
                jnp.bfloat16
            )
        return 0

    lax.fori_loop(0, levels // 4, narrow, 0)


def pair_sums(
    tasks, levels, lefts, lanes, values, col_n, col_s, row_n, row_s, half, unroll
):
    span = levels + 2
    row_n[...] = jnp.zeros_like(row_n)
    row_s[...] = jnp.zeros_like(row_s)
    col_n[...] = jnp.zeros_like(col_n)
    col_s[...] = jnp.zeros_like(col_s)
    groups = half // 8
    spots = lax.broadcasted_iota(jnp.int32, (32, 128), 0)
    picks = jnp.logical_and(spots >= 25, spots < 28)
    field_rows = jnp.where(picks, 1.0, 0.0).astype(jnp.bfloat16)

    def right(z, tile):
        if tile is None:
            return field_rows
        col, shift, _ = tile
        at = col * span + 1 + z + shift
        return jnp.concatenate([lanes[0, at], lanes[2 + shift, at]], axis=0)

    def weights(square):
        return lax.rsqrt(jnp.minimum(jnp.maximum(square, min_square), 1.0))

    def level_step(z):
        mine = lax.broadcasted_iota(jnp.int32, (8, 128), 1) == z
        for row, tiles in tasks:
            total = None
            fields = {}
            for tile in tiles:
                col, shift, _ = tile
                f = values[pl.ds(col * (levels + 16) + 8 + z + shift, 1), :]
                fields[tile] = f
                total = f if total is None else total + f
            queue = [None] + tiles
            whole = jnp.transpose(lefts[row * levels + z])
            for part in range(128 // half):
                left = whole[part * half : (part + 1) * half]
                sums_n = [jnp.full((8, 128), -float(len(tiles)), jnp.float32)] * groups
                sums_s = [jnp.broadcast_to(-total, (8, 128))] * groups
                own = own_sum = None
                for t in range(0, len(queue), 2):
                    pair = queue[t : t + 2]
                    rights = [right(z, tile) for tile in pair]
                    square = lax.dot_general(
                        left,
                        jnp.concatenate(rights, axis=1) if len(pair) == 2 else rights[0],
                        (((1,), (0,)), ((), ())),
                        preferred_element_type=jnp.float32,
                    )
                    for p, tile in enumerate(pair):
                        pieces = [
                            square[g * 8 : g * 8 + 8, p * 128 : p * 128 + 128]
                            for g in range(groups)
                        ]
                        if tile is None:
                            own = pieces
                            own_sum = functools.reduce(jnp.add, own)
                            continue
                        col, shift, both = tile
                        f = fields[tile]
                        down_n = jnp.full((8, 128), -float(groups), jnp.float32)
                        down_s = -own_sum
                        for g in range(groups):
                            w = weights(pieces[g])
                            sums_n[g] = sums_n[g] + w
                            sums_s[g] = sums_s[g] + w * f
                            if both:
                                down_n = down_n + w
                                down_s = down_s + w * own[g]
                        if both:
                            at = pl.ds(pl.multiple_of((col * span + 1 + z + shift) * 8, 8), 8)
                            col_n[at, :] += down_n
                            col_s[at, :] += down_s
                for totals, sums in ((row_n, sums_n), (row_s, sums_s)):
                    for g in range(groups):
                        at = slice(part * half + g * 8, part * half + g * 8 + 8)
                        totals[row, at, :] = jnp.where(
                            mine, jnp.sum(sums[g], axis=1, keepdims=True), totals[row, at, :]
                        )

    def some_levels(k, _):
        for u in range(unroll):
            level_step(k * unroll + u)
        return 0

    lax.fori_loop(0, levels // unroll, some_levels, 0)


def fold_column(ref, col, levels):
    base = (col * (levels + 2) + 1) * 8
    total = None
    for k in range(8):
        part = ref[pl.ds(base + k, levels, 8), :]
        total = part if total is None else total + part
    return total


def own_tasks(rows):
    tasks = []
    for row in rows:
        tiles = [(row, 0, False), (row, 1, True)]
        for col in range(row + 1, 4):
            tiles += [(col, shift, True) for shift in (-1, 0, 1)]
        tasks.append((row, tiles))
    return tasks


def far_tasks():
    wanted = ((0, (0, 1)), (1, (2, 3, 4)), (2, (0, 1, 3, 4, 5)))
    return [
        (row, [(col, shift, True) for col in cols for shift in (-1, 0, 1)])
        for row, cols in wanted
    ]


def corners():
    corner_x = (lax.axis_index("slab") * 2 + 1).astype(jnp.float32)
    corner_y = (lax.axis_index("dom") * 2 + 1).astype(jnp.float32)
    return corner_x, corner_y


def own_kernel(raw, *refs, levels, half, unroll, first, last):
    count = 4 - first
    starts, refs = (refs[:2], refs[2:]) if first else (None, refs)
    (out_n, out_s), scratch = refs[:2], refs[2:]
    flat, side, lanes, values, tall, lefts, col_n, col_s, row_n, row_s = scratch
    corner_x, corner_y = corners()
    for col in range(count):
        base = (col + first) * levels
        make_lanes(raw, base, col, levels, corner_x, corner_y, None, flat, side, lanes, values)
    for row in range(last - first):
        make_rows(raw, (row + first) * levels, row, levels, corner_x, corner_y, tall, lefts)
    tasks = [
        (row - first, [(col - first, shift, both) for col, shift, both in tiles])
        for row, tiles in own_tasks(range(first, last))
    ]
    pair_sums(tasks, levels, lefts, lanes, values, col_n, col_s, row_n, row_s, half, unroll)
    for col in range(4):
        if col < first:
            out_n[col] = starts[0][col]
            out_s[col] = starts[1][col]
            continue
        n = fold_column(col_n, col - first, levels)
        s = fold_column(col_s, col - first, levels)
        if col < last:
            f = values[pl.ds((col - first) * (levels + 16) + 8, levels), :]
            itself = lax.rsqrt(jnp.maximum(0.0 * f, min_square)) - 1.0
            n = n + jnp.transpose(row_n[col - first])[:levels] - itself
            s = s + jnp.transpose(row_s[col - first])[:levels] - itself * f
        if first:
            n = n + starts[0][col]
            s = s + starts[1][col]
        out_n[col] = n
        out_s[col] = s


def far_kernel(raw, dom_raw, slab_raw, up_raw, down_raw, *refs, levels, half, unroll, slabs, doms):
    start_n, start_s, out_n, out_s, to_dom, to_slab, to_up, to_down = refs[:8]
    flat, side, lanes, values, tall, lefts, col_n, col_s, row_n, row_s = refs[8:]
    corner_x, corner_y = corners()
    slab, dom = lax.axis_index("slab"), lax.axis_index("dom")
    next_slab = slab + 1 < slabs
    next_dom = dom + 1 < doms
    previous_dom = dom > 0
    sources = (
        (dom_raw, 0, next_dom),
        (dom_raw, levels, next_dom),
        (down_raw, 0, jnp.logical_and(next_slab, previous_dom)),
        (slab_raw, 0, next_slab),
        (slab_raw, levels, next_slab),
        (up_raw, 0, jnp.logical_and(next_slab, next_dom)),
    )
    for col, (source, base, valid) in enumerate(sources):
        make_lanes(
            source, base, col, levels, corner_x, corner_y, valid, flat, side, lanes, values
        )
    for row in range(3):
        make_rows(raw, (row + 1) * levels, row, levels, corner_x, corner_y, tall, lefts)
    pair_sums(
        far_tasks(), levels, lefts, lanes, values, col_n, col_s, row_n, row_s, half, unroll
    )
    out_n[0] = start_n[0]
    out_s[0] = start_s[0]
    for row in range(3):
        out_n[row + 1] = start_n[row + 1] + jnp.transpose(row_n[row])[:levels]
        out_s[row + 1] = start_s[row + 1] + jnp.transpose(row_s[row])[:levels]
    for channel, ref in enumerate((col_n, col_s)):
        for k in range(2):
            to_dom[channel, k] = fold_column(ref, k, levels)
            to_slab[channel, k] = fold_column(ref, 3 + k, levels)
        to_down[channel] = fold_column(ref, 2, levels)
        to_up[channel] = fold_column(ref, 5, levels)


def finish_kernel(raw, own_n, own_s, *refs, levels):
    from_dom, from_slab, from_up, from_down, density, laplace = refs
    for col in range(4):
        sums = []
        for channel, near in enumerate((own_n, own_s)):
            total = near[col]
            if col in (0, 2):
                total = total + from_dom[channel, col // 2]
            if col in (0, 1):
                total = total + from_slab[channel, col]
            if col == 0:
                total = total + from_up[channel]
            if col == 1:
                total = total + from_down[channel]
            sums.append(total)
        filled = raw[pl.ds(col * levels * 4, levels, 4), :] > 0.5 * far_away
        n = jnp.where(filled, sums[0], 0.0)
        s = jnp.where(filled, sums[1], 0.0)
        f = raw[pl.ds(col * levels * 4 + 3, levels, 4), :]
        density[col] = n / ref_density
        laplace[col] = (s - f * n) / ref_density


def scratch_for(levels, cols, rows):
    span = levels + 2
    f32, bf16 = jnp.float32, jnp.bfloat16
    return [
        pltpu.VMEM((levels * 16, 128), f32),
        pltpu.VMEM((3, levels * 16, 128), f32),
        pltpu.VMEM((4, cols * span, 16, 128), bf16),
        pltpu.VMEM((cols * (levels + 16), 128), f32),
        pltpu.VMEM((levels * 32, 128), f32),
        pltpu.VMEM((rows * levels, 32, 128), bf16),
        pltpu.VMEM((cols * span * 8, 128), f32),
        pltpu.VMEM((cols * span * 8, 128), f32),
        pltpu.VMEM((rows, 128, 128), f32),
        pltpu.VMEM((rows, 128, 128), f32),
    ]


def local(incoming, dest, counts):
    cells_x, cells_y, levels = counts.shape
    slots = incoming.shape[3]
    cells = cells_x * cells_y * levels
    capacity = cells // 4
    slabs, doms = lax.axis_size("slab"), lax.axis_size("dom")
    assert (cells_x, cells_y, slots) == (2, 2, 128) and levels % 8 == 0 and levels <= 128
    assert cells % 128 == 0 and cells <= 16 * 128 and doms >= 5
    assert capacity % 8 == 0 and 128 <= 4 * capacity <= 512
    f32, i32 = jnp.float32, jnp.int32
    shape = jax.ShapeDtypeStruct
    blocks = incoming.reshape(cells, 4, slots)
    *packs, stayed = pl.pallas_call(
        functools.partial(pack_kernel, cells=cells, capacity=capacity, domains=doms),
        out_shape=[shape((capacity + 1, 4, slots), f32)] * 4 + [shape((cells, 4, slots), f32)],
        in_specs=[vmem, vmem],
        out_specs=[vmem] * 5,
        scratch_shapes=[
            pltpu.VMEM((4 * capacity + cells, 4, slots), f32),
            pltpu.VMEM((cells // 128, 128), i32),
            pltpu.SMEM((cells // 128, 128), i32),
            pltpu.SemaphoreType.DMA,
        ],
        compiler_params=params,
        name="pack",
    )(dest.reshape(cells // 128, 128), blocks)
    got = [
        lax.ppermute(pack, "dom", [(i, (i + step) % doms) for i in range(doms)])
        for step, pack in zip(offsets, packs)
    ]
    column = (levels, 4, slots)
    home, to_dom, to_slab, to_up, to_down = pl.pallas_call(
        functools.partial(place_kernel, cells=cells, capacity=capacity, levels=levels),
        out_shape=[shape((cells, 4, slots), f32)]
        + [shape((2 * levels, 4, slots), f32)] * 2
        + [shape(column, f32)] * 2,
        in_specs=[vmem] * 5 + [smem],
        out_specs=[vmem] * 5,
        scratch_shapes=[
            pltpu.VMEM((cells + 1, 4, slots), f32),
            pltpu.VMEM((4, 4, 128), i32),
            pltpu.SMEM((4, 4, 128), i32),
            pltpu.SemaphoreType.DMA,
        ],
        compiler_params=params,
        name="place",
    )(*got, stayed, counts)

    both = ("slab", "dom")

    def route(step_slab, step_dom):
        pairs = []
        for s in range(slabs):
            for d in range(doms):
                if 0 <= s + step_slab < slabs and 0 <= d + step_dom < doms:
                    pairs.append((s * doms + d, (s + step_slab) * doms + d + step_dom))
        return pairs

    def send(value, step_slab, step_dom):
        return lax.ppermute(value, both, route(step_slab, step_dom))

    def rows_of(value):
        return value.reshape(-1, slots)

    slab_raw = send(to_slab, -1, 0)
    dom_raw = send(to_dom, 0, -1)
    up_raw = send(to_up, -1, -1)
    down_raw = send(to_down, -1, 1)
    raw = rows_of(home)
    half = 128
    plane = (4, levels, slots)

    def cost(tiles):
        return pl.CostEstimate(
            flops=levels * tiles * 128 * 128 * 600,
            bytes_accessed=cells * 4 * slots * 4,
            transcendentals=0,
        )

    def own_pairs(first, last, unroll, *start):
        return pl.pallas_call(
            functools.partial(
                own_kernel, levels=levels, half=half, unroll=unroll, first=first, last=last
            ),
            out_shape=[shape(plane, f32)] * 2,
            in_specs=[vmem] * (1 + len(start)),
            out_specs=[vmem] * 2,
            scratch_shapes=scratch_for(levels, 4 - first, last - first),
            compiler_params=params,
            cost_estimate=cost(26),
            name="own",
        )(raw, *start)

    early_n, early_s = own_pairs(0, 1, 4)
    far_n, far_s, ret_dom, ret_slab, ret_up, ret_down = pl.pallas_call(
        functools.partial(
            far_kernel, levels=levels, half=half, unroll=4, slabs=slabs, doms=doms
        ),
        out_shape=[shape(plane, f32)] * 2
        + [shape((2, 2, levels, slots), f32)] * 2
        + [shape((2, levels, slots), f32)] * 2,
        in_specs=[vmem] * 7,
        out_specs=[vmem] * 6,
        scratch_shapes=scratch_for(levels, 6, 3),
        compiler_params=params,
        cost_estimate=cost(30),
        name="far",
    )(
        raw,
        rows_of(dom_raw),
        rows_of(slab_raw),
        rows_of(up_raw),
        rows_of(down_raw),
        early_n,
        early_s,
    )
    from_slab = send(ret_slab, 1, 0)
    from_dom = send(ret_dom, 0, 1)
    from_up = send(ret_up, 1, 1)
    from_down = send(ret_down, 1, -1)
    own_n, own_s = own_pairs(1, 4, 4, far_n, far_s)
    density, laplace = pl.pallas_call(
        functools.partial(finish_kernel, levels=levels),
        out_shape=[shape(plane, f32)] * 2,
        in_specs=[vmem] * 7,
        out_specs=[vmem] * 2,
        compiler_params=params,
        name="finish",
    )(raw, own_n, own_s, from_dom, from_slab, from_up, from_down)
    final = (cells_x, cells_y, levels, slots)
    return density.reshape(final), laplace.reshape(final)


def solution(mesh):
    in_specs = (P("slab", "dom", None, None), P("slab", "dom"), P("slab", "dom", None))
    out_specs = (P("slab", "dom", None, None), P("slab", "dom", None, None))
    return jax.shard_map(local, mesh=mesh, in_specs=in_specs, out_specs=out_specs, check_vma=False)
```

time: 265 us -> 169 us (0.64)
  Pallas kernels: 217 us -> 127 us
  waiting for transfers between devices: 19.3 us -> 7.76 us
  starting transfers between devices: 23 us -> 29.4 us
    pallas_call x2 -> x3, Pallas kernels: 193 us -> 115 us  [the longest x1 57.7 us: local(): pl.pallas_call(functools.partial(far_kernel, levels=levels, half=half, un...]
    ppermute x8, waiting for transfers between devices: 12.2 us -> 0.02 us  [send(): return lax.ppermute(value, both, route(step_slab, step_dom))]
    pallas_call x1, Pallas kernels: 12.2 us -> 4.61 us  [local(): pl.pallas_call(functools.partial(pack_kernel, cells=cells, capacity=capac...]
    ppermute x8, starting transfers between devices: 16.7 us -> 23 us  [send(): return lax.ppermute(value, both, route(step_slab, step_dom))]
    pallas_call x1, Pallas kernels: 8.81 us -> 5.33 us  [local(): pl.pallas_call(functools.partial(place_kernel, cells=cells, capacity=capa...]
  transfers between devices with their start and end apart: 12 -> 12, of which waited for: 5 -> 4; matrix products, arithmetic and copies ran while one was open for 0% -> 0% of each run, Pallas kernels for 37% -> 34%
where the time goes in v2:
time: 169 us; the launch traced here: 167 us
  Pallas kernels  127 us (75%)
  starting transfers between devices  29.4 us (17%)
  waiting for transfers between devices  7.76 us (5%)
  local copies, waits for them, and re-layouts  2.21 us (1%)
    pallas_call x1, Pallas kernels, local(): pl.pallas_call(functools.partial(far_kernel, levels=levels, half=half, un...  57.7 us
    pallas_call x2, Pallas kernels, own_pairs(): pl.pallas_call(functools.partial(own_kernel, levels=levels, half=half, un...  57.1 us
    ppermute x8, starting transfers between devices, send(): return lax.ppermute(value, both, route(step_slab, step_dom))  23 us
    ppermute x4, waiting for transfers between devices, local(): lax.ppermute(pack, 'dom', [(i, (i + step) % doms) for i in range(doms)])  7.74 us
    ppermute x4, starting transfers between devices, local(): lax.ppermute(pack, 'dom', [(i, (i + step) % doms) for i in range(doms)])  6.32 us
    pallas_call x1, Pallas kernels, local(): pl.pallas_call(functools.partial(place_kernel, cells=cells, capacity=capa...  5.33 us
    pallas_call x1, Pallas kernels, local(): pl.pallas_call(functools.partial(pack_kernel, cells=cells, capacity=capac...  4.61 us
  transfers between devices with their start and end apart: 12, of which 4 were waited for; matrix products, arithmetic and copies ran while one was open for 0% of the time, Pallas kernels for 34%

profile of v2, /device:TPU:0, one launch (start us, length us, event | category | flops | bytes accessed | tf_op | source)
XLA Modules:
  0.0 166.9 jit_solution(7800904333561402017)
XLA Ops:
  0.6 4.6 %pack.1 = (f32[65,4,128]{2,1,0:T(4,128)}, f32[65,4,128]{2,1,0:T(4,128)}, f32[65,4,128]{2,1,0:T(4,128)}, f32[65,4,128]{2,1,0:T(4,128)}, f32[256,4,128]{2,1,0:T(4,128)}) custom-call(s32[2,128]{1,0:T(2,128)} %bitcast.14, f32[256,4,128]{2,1,0:T(4,128)} %bitcast.9), custom_call_target="tpu_custom_call" | custom-call | tf_op jit(solution)/shard_map/pack/pallas_call | solution.py:484
  5.2 5.1 %collective-permute-start = (f32[65,4,128]{2,1,0:T(4,128)}, f32[65,4,128]{2,1,0:T(4,128)S(1)}, u32[]{:S(2)}, u32[]{:S(2)}) collective-permute-start(f32[65,4,128]{2,1,0:T(4,128)} %get-tuple-element.24), channel_id=1, source_target_pairs={{0,6},{1,7},{2,0},{3,1},{4,2},{5,3},{6,4},{7,5},{8,14},{9,15},{10,... | collective-permute-start | bytes 399368 | tf_op jit(solution)/shard_map/ppermute | solution.py:499
  10.4 0.0 collective-permute-start.1
  10.4 0.5 collective-permute-start.2
  10.9 0.7 collective-permute-start.3
  11.6 3.1 %collective-permute-done.refs_0_ = f32[65,4,128]{2,1,0:T(4,128)S(1)} collective-permute-done((f32[65,4,128]{2,1,0:T(4,128)}, f32[65,4,128]{2,1,0:T(4,128)S(1)}, u32[]{:S(2)}, u32[]{:S(2)}) %collective-permute-start) | collective-permute-done | bytes 133152 | tf_op jit(solution)/shard_map/ppermute | solution.py:499
  14.6 2.9 %collective-permute-done.1.refs_1_ = f32[65,4,128]{2,1,0:T(4,128)S(1)} collective-permute-done((f32[65,4,128]{2,1,0:T(4,128)}, f32[65,4,128]{2,1,0:T(4,128)S(1)}, u32[]{:S(2)}, u32[]{:S(2)}) %collective-permute-start.1) | collective-permute-done | bytes 133152 | tf_op jit(solution)/shard_map/ppermute | solution.py:499
  17.5 0.3 collective-permute-done.2.refs_2_
  17.8 1.5 collective-permute-done.3.refs_3_
  19.3 0.0 copy-done
  19.3 0.0 copy-done.1
  19.3 0.0 copy-done.2
  19.3 0.7 copy-done.3
  20.0 5.3 %place.1 = (f32[256,4,128]{2,1,0:T(4,128)}, f32[128,4,128]{2,1,0:T(4,128)}, f32[128,4,128]{2,1,0:T(4,128)}, f32[64,4,128]{2,1,0:T(4,128)}, f32[64,4,128]{2,1,0:T(4,128)}) custom-call(f32[65,4,128]{2,1,0:T(4,128)} %copy-done, f32[65,4,128]{2,1,0:T(4,128)} %copy-done.1, f32[65,4,128]{2,1,0:T(4,128)} %copy-done.2, f32[65,4,128]{2,1,0:T(4,128)} %copy-done.3, ...), custom_call_target="tpu_custom_call" | custom-call | tf_op jit(solution)/shard_map/place/pallas_call | solution.py:503
  25.3 1.3 collective-permute-start.6
  26.6 0.7 collective-permute-start.7
  27.3 1.3 collective-permute-start.4
  28.6 1.3 collective-permute-start.5
  29.9 25.1 %own.2 = (f32[4,64,128]{2,1,0:T(8,128)}, f32[4,64,128]{2,1,0:T(8,128)}) custom-call(f32[1024,128]{1,0:T(8,128)} %bitcast.10), custom_call_target="tpu_custom_call" | custom-call | flops 16357785600 | bytes 524288 | tf_op jit(solution)/shard_map/own/pallas_call | solution.py:552
  55.0 0.0 collective-permute-done.6
  55.0 0.0 collective-permute-done.7
  55.0 0.0 copy-start.11
  55.0 0.0 collective-permute-done.4
  55.0 0.0 copy-start.8
  55.0 0.0 collective-permute-done.5
  55.0 0.0 copy-start.9
  55.1 0.6 copy-done.10
  55.7 0.0 copy-done.11
  55.7 0.1 copy-done.8
  55.8 0.1 copy-done.9
  55.9 57.7 %far.1 = (f32[4,64,128]{2,1,0:T(8,128)}, f32[4,64,128]{2,1,0:T(8,128)}, f32[2,2,64,128]{3,2,1,0:T(8,128)}, f32[2,2,64,128]{3,2,1,0:T(8,128)}, f32[2,64,128]{2,1,0:T(8,128)}, /*index=5*/f32[2,64,128]{2,1,0:T(8,128)}) custom-call(f32[1024,128]{1,0:T(8,128)} %bitcast.11, f32[512,128]{1,0:T(8,128)} %bitcast.15, f32[512,128]{1,0:T(8,128)} %bitcast.16, ...), custom_call_target="tpu_custom_call" | custom-call | flops 18874368000 | bytes 524288 | tf_op jit(solution)/shard_map/far/pallas_call | solution.py:566
  113.5 7.9 %collective-permute-start.10 = (f32[2,64,128]{2,1,0:T(8,128)}, f32[2,64,128]{2,1,0:T(8,128)S(1)}, u32[]{:S(2)}, u32[]{:S(2)}) collective-permute-start(f32[2,64,128]{2,1,0:T(8,128)} %get-tuple-element.42), channel_id=1, source_target_pairs={{0,9},{1,10},{2,11},{3,12},{4,13},{5,14},{6,15},{8,17},{9,18},{10,... | collective-permute-start | bytes 196616 | tf_op jit(solution)/shard_map/ppermute | solution.py:531
  121.4 0.7 collective-permute-start.11
  122.1 6.3 %collective-permute-start.8 = (f32[2,2,64,128]{3,2,1,0:T(8,128)}, f32[2,2,64,128]{3,2,1,0:T(8,128)S(1)}, u32[]{:S(2)}, u32[]{:S(2)}) collective-permute-start(f32[2,2,64,128]{3,2,1,0:T(8,128)} %get-tuple-element.40), channel_id=1, source_target_pairs={{0,1},{1,2},{2,3},{3,4},{4,5},{5,6},{6,7},{8,9},{9,10},{10,11},{11... | collective-permute-start | bytes 393224 | tf_op jit(solution)/shard_map/ppermute | solution.py:531
  128.4 3.7 %collective-permute-start.9 = (f32[2,2,64,128]{3,2,1,0:T(8,128)}, f32[2,2,64,128]{3,2,1,0:T(8,128)S(1)}, u32[]{:S(2)}, u32[]{:S(2)}) collective-permute-start(f32[2,2,64,128]{3,2,1,0:T(8,128)} %get-tuple-element.41), channel_id=1, source_target_pairs={{0,8},{1,9},{2,10},{3,11},{4,12},{5,13},{6,14},{7,15},{8,16},{9,17... | collective-permute-start | bytes 393224 | tf_op jit(solution)/shard_map/ppermute | solution.py:531
  132.1 32.0 %own.3 = (f32[4,64,128]{2,1,0:T(8,128)}, f32[4,64,128]{2,1,0:T(8,128)}) custom-call(f32[1024,128]{1,0:T(8,128)} %bitcast.12, f32[4,64,128]{2,1,0:T(8,128)} %get-tuple-element.36.refs_0_, f32[4,64,128]{2,1,0:T(8,128)} %get-tuple-element.37.refs_1_), custom_call_target="tpu_custom_call" | custom-call | flops 16357785600 | bytes 524288 | tf_op jit(solution)/shard_map/own/pallas_call | solution.py:552
  164.1 0.0 collective-permute-done.10.refs_2_
  164.1 0.0 collective-permute-done.11.refs_3_
  164.1 0.0 copy-start.7
  164.1 0.0 collective-permute-done.8.refs_0_
  164.1 0.0 copy-start.4
  164.2 0.0 collective-permute-done.9.refs_1_
  164.2 0.0 copy-start.5
  164.2 0.6 copy-done.6
  164.7 0.0 copy-done.7
  164.8 0.1 copy-done.4
  164.8 0.1 copy-done.5
  164.9 2.0 %finish.1 = (f32[4,64,128]{2,1,0:T(8,128)}, f32[4,64,128]{2,1,0:T(8,128)}) custom-call(f32[1024,128]{1,0:T(8,128)} %bitcast.13, f32[4,64,128]{2,1,0:T(8,128)} %get-tuple-element.38.own_n, f32[4,64,128]{2,1,0:T(8,128)} %get-tuple-element.39.own_s, f32[2,2,64,128]{3,2,1,0:T(8,128)} %copy-done.4, f32[2,2,64,128]{3,2,1,0:T(8,128)} %copy-done.5, ...), custom_call_target="tpu_custom_call" | custom-call | tf_op jit(solution)/shard_map/finish/pallas_call | solution.py:593
  (6 shorter events, 0.0 us)
Async XLA Ops:
  5.2 9.4 %collective-permute-start = (f32[65,4,128]{2,1,0:T(4,128)}, f32[65,4,128]{2,1,0:T(4,128)S(1)}, u32[]{:S(2)}, u32[]{:S(2)}) collective-permute-start(f32[65,4,128]{2,1,0:T(4,128)} %get-tuple-element.24), channel_id=1, source_target_pairs={{0,6},{1,7},{2,0},{3,1},{4,2},{5,3},{6,4},{7,5},{8,14},{9,15},{10,... | collective-permute-start | bytes 399368 | tf_op jit(solution)/shard_map/ppermute | solution.py:499
  10.4 7.1 %collective-permute-start.1 = (f32[65,4,128]{2,1,0:T(4,128)}, f32[65,4,128]{2,1,0:T(4,128)S(1)}, u32[]{:S(2)}, u32[]{:S(2)}) collective-permute-start(f32[65,4,128]{2,1,0:T(4,128)} %get-tuple-element.25), channel_id=1, source_target_pairs={{0,7},{1,0},{2,1},{3,2},{4,3},{5,4},{6,5},{7,6},{8,15},{9,8},{10,9... | collective-permute-start | bytes 399368 | tf_op jit(solution)/shard_map/ppermute | solution.py:499
  10.4 7.4 %collective-permute-start.2 = (f32[65,4,128]{2,1,0:T(4,128)}, f32[65,4,128]{2,1,0:T(4,128)S(1)}, u32[]{:S(2)}, u32[]{:S(2)}) collective-permute-start(f32[65,4,128]{2,1,0:T(4,128)} %get-tuple-element.26), channel_id=1, source_target_pairs={{0,1},{1,2},{2,3},{3,4},{4,5},{5,6},{6,7},{7,0},{8,9},{9,10},{10,1... | collective-permute-start | bytes 399368 | tf_op jit(solution)/shard_map/ppermute | solution.py:499
  10.9 8.4 %collective-permute-start.3 = (f32[65,4,128]{2,1,0:T(4,128)}, f32[65,4,128]{2,1,0:T(4,128)S(1)}, u32[]{:S(2)}, u32[]{:S(2)}) collective-permute-start(f32[65,4,128]{2,1,0:T(4,128)} %get-tuple-element.27), channel_id=1, source_target_pairs={{0,2},{1,3},{2,4},{3,5},{4,6},{5,7},{6,0},{7,1},{8,10},{9,11},{10,... | collective-permute-start | bytes 399368 | tf_op jit(solution)/shard_map/ppermute | solution.py:499
  14.6 4.7 %copy-start = (f32[65,4,128]{2,1,0:T(4,128)}, f32[65,4,128]{2,1,0:T(4,128)S(1)}, u32[]{:S(2)}) copy-start(f32[65,4,128]{2,1,0:T(4,128)S(1)} %collective-permute-done.refs_0_) | copy-start | bytes 399364
  17.5 1.8 %copy-start.1 = (f32[65,4,128]{2,1,0:T(4,128)}, f32[65,4,128]{2,1,0:T(4,128)S(1)}, u32[]{:S(2)}) copy-start(f32[65,4,128]{2,1,0:T(4,128)S(1)} %collective-permute-done.1.refs_1_) | copy-start | bytes 399364
  17.8 1.5 copy-start.2
  19.3 0.7 copy-start.3
  25.3 29.7 %collective-permute-start.6 = (f32[64,4,128]{2,1,0:T(4,128)}, f32[64,4,128]{2,1,0:T(4,128)S(1)}, u32[]{:S(2)}, u32[]{:S(2)}) collective-permute-start(f32[64,4,128]{2,1,0:T(4,128)} %get-tuple-element.32), channel_id=1, source_target_pairs={{9,0},{10,1},{11,2},{12,3},{13,4},{14,5},{15,6},{17,8},{18,9},{19,... | collective-permute-start | bytes 393224 | tf_op jit(solution)/shard_map/ppermute | solution.py:531
  26.6 28.4 %collective-permute-start.7 = (f32[64,4,128]{2,1,0:T(4,128)}, f32[64,4,128]{2,1,0:T(4,128)S(1)}, u32[]{:S(2)}, u32[]{:S(2)}) collective-permute-start(f32[64,4,128]{2,1,0:T(4,128)} %get-tuple-element.33), channel_id=1, source_target_pairs={{8,1},{9,2},{10,3},{11,4},{12,5},{13,6},{14,7},{16,9},{17,10},{18,... | collective-permute-start | bytes 393224 | tf_op jit(solution)/shard_map/ppermute | solution.py:531
  27.3 27.7 %collective-permute-start.4 = (f32[128,4,128]{2,1,0:T(4,128)}, f32[128,4,128]{2,1,0:T(4,128)S(1)}, u32[]{:S(2)}, u32[]{:S(2)}) collective-permute-start(f32[128,4,128]{2,1,0:T(4,128)} %get-tuple-element.30), channel_id=1, source_target_pairs={{1,0},{2,1},{3,2},{4,3},{5,4},{6,5},{7,6},{9,8},{10,9},{11,10},{12... | collective-permute-start | bytes 786440 | tf_op jit(solution)/shard_map/ppermute | solution.py:531
  28.6 26.4 %collective-permute-start.5 = (f32[128,4,128]{2,1,0:T(4,128)}, f32[128,4,128]{2,1,0:T(4,128)S(1)}, u32[]{:S(2)}, u32[]{:S(2)}) collective-permute-start(f32[128,4,128]{2,1,0:T(4,128)} %get-tuple-element.31), channel_id=1, source_target_pairs={{8,0},{9,1},{10,2},{11,3},{12,4},{13,5},{14,6},{15,7},{16,8},{17,9... | collective-permute-start | bytes 786440 | tf_op jit(solution)/shard_map/ppermute | solution.py:531
  55.0 0.7 copy-start.10
  55.0 0.7 copy-start.11
  55.0 0.8 copy-start.8
  55.0 0.8 copy-start.9
  113.5 50.6 %collective-permute-start.10 = (f32[2,64,128]{2,1,0:T(8,128)}, f32[2,64,128]{2,1,0:T(8,128)S(1)}, u32[]{:S(2)}, u32[]{:S(2)}) collective-permute-start(f32[2,64,128]{2,1,0:T(8,128)} %get-tuple-element.42), channel_id=1, source_target_pairs={{0,9},{1,10},{2,11},{3,12},{4,13},{5,14},{6,15},{8,17},{9,18},{10,... | collective-permute-start | bytes 196616 | tf_op jit(solution)/shard_map/ppermute | solution.py:531
  121.4 42.7 %collective-permute-start.11 = (f32[2,64,128]{2,1,0:T(8,128)}, f32[2,64,128]{2,1,0:T(8,128)S(1)}, u32[]{:S(2)}, u32[]{:S(2)}) collective-permute-start(f32[2,64,128]{2,1,0:T(8,128)} %get-tuple-element.43), channel_id=1, source_target_pairs={{1,8},{2,9},{3,10},{4,11},{5,12},{6,13},{7,14},{9,16},{10,17},{11,... | collective-permute-start | bytes 196616 | tf_op jit(solution)/shard_map/ppermute | solution.py:531
  122.1 42.0 %collective-permute-start.8 = (f32[2,2,64,128]{3,2,1,0:T(8,128)}, f32[2,2,64,128]{3,2,1,0:T(8,128)S(1)}, u32[]{:S(2)}, u32[]{:S(2)}) collective-permute-start(f32[2,2,64,128]{3,2,1,0:T(8,128)} %get-tuple-element.40), channel_id=1, source_target_pairs={{0,1},{1,2},{2,3},{3,4},{4,5},{5,6},{6,7},{8,9},{9,10},{10,11},{11... | collective-permute-start | bytes 393224 | tf_op jit(solution)/shard_map/ppermute | solution.py:531
  128.4 35.8 %collective-permute-start.9 = (f32[2,2,64,128]{3,2,1,0:T(8,128)}, f32[2,2,64,128]{3,2,1,0:T(8,128)S(1)}, u32[]{:S(2)}, u32[]{:S(2)}) collective-permute-start(f32[2,2,64,128]{3,2,1,0:T(8,128)} %get-tuple-element.41), channel_id=1, source_target_pairs={{0,8},{1,9},{2,10},{3,11},{4,12},{5,13},{6,14},{7,15},{8,16},{9,17... | collective-permute-start | bytes 393224 | tf_op jit(solution)/shard_map/ppermute | solution.py:531
  164.1 0.6 copy-start.6
  164.1 0.6 copy-start.7
  164.1 0.7 copy-start.4
  164.2 0.7 copy-start.5

commit v3 on v2

--- a/solution.py
+++ b/solution.py
@@ -87,8 +87,8 @@
 
 def place_kernel(*refs, cells, capacity, levels):
     got, stayed, counts = refs[:4], refs[4], refs[5]
-    home, to_dom, to_slab, to_up, to_down = refs[6:11]
-    kept, cell_ids, marks, sem = refs[11:]
+    home, to_dom, to_slab, to_edge = refs[6:10]
+    kept, cell_ids, marks, sem = refs[10:]
     for g in range(4):
         sent = got[g][capacity].astype(jnp.int32) - 1
         cell_ids[g] = jnp.where(sent < 0, cells, sent)
@@ -120,10 +120,9 @@
                 if col == 0:
                     to_dom[z] = block
                     to_slab[z] = block
-                    to_up[z] = block
+                    to_edge[z] = block
                 if col == 1:
                     to_slab[levels + z] = block
-                    to_down[z] = block
                 if col == 2:
                     to_dom[levels + z] = block
         return 0
@@ -150,32 +149,23 @@
     return x - corner_x, y - corner_y, z - (rows.astype(jnp.float32) + 0.5), f
 
 
-def make_lanes(raw, base, col, levels, corner_x, corner_y, valid, flat, side, lanes, values):
+def make_lanes(raw, base, col, levels, corner_x, corner_y, valid, parts, lanes, values):
     span = levels + 2
+    rows = lax.broadcasted_iota(jnp.int32, (8, 128), 0)
     zero = jnp.zeros((8, 128), jnp.float32)
-    one = jnp.ones((8, 128), jnp.float32)
 
     def chunk(k, _):
-        level = k * 8
+        level = pl.multiple_of(k * 8, 8)
         first = pl.multiple_of((base + level) * 4, 32)
         x, y, z, f = load_points(raw, first, corner_x, corner_y, level, valid)
         values[pl.ds(pl.multiple_of(col * (levels + 16) + 8 + level, 8), 8), :] = f
-        x3, y3 = split3(x), split3(y)
-        rows = []
-        for part in (x3, y3):
-            rows += [part[0], part[1], part[0], part[1], part[2], part[0]]
-        rows += [one, one, one, zero]
-        for r, value in enumerate(rows):
-            flat[pl.ds(level * 16 + r, 8, 16), :] = value
+        found = [*split3(x), *split3(y)]
         flat_norm = x * x + y * y
         for shift in range(3):
             moved = z + float(shift - 1)
-            z3 = split3(moved)
-            norm = split3(flat_norm + moved * moved)
-            rows = [z3[0], z3[1], z3[0], z3[1], z3[2], z3[0], norm[0], norm[1], norm[2]]
-            rows += [zero] * 7
-            for r, value in enumerate(rows):
-                side[shift, pl.ds(level * 16 + r, 8, 16), :] = value
+            found += [*split3(moved), *split3(flat_norm + moved * moved)]
+        for p, value in enumerate(found):
+            parts[p, pl.ds(level, 8), :] = value
         return 0
 
     lax.fori_loop(0, levels // 8, chunk, 0)
@@ -188,48 +178,102 @@
     values[pl.ds(col * (levels + 16), 8), :] = zero
     values[pl.ds(col * (levels + 16) + 8 + levels, 8), :] = zero
 
+    def is_in(*which):
+        return functools.reduce(jnp.logical_or, [rows == r for r in which])
+
+    mids, low, third, head = is_in(1, 3, 7), is_in(4), is_in(2), is_in(0)
+    tail = rows >= 6
+    units = jnp.where(rows < 7, 1.0, 0.0)
+
     def narrow(k, _):
         for u in range(4):
             z = k * 4 + u
-            at = pl.multiple_of(z * 16, 16)
-            lanes[0, col * span + 1 + z] = flat[pl.ds(at, 16), :].astype(jnp.bfloat16)
+
+            def part(p, z=z):
+                return jnp.broadcast_to(parts[p, pl.ds(z, 1), :], (8, 128))
+
+            def six(first, then):
+                high = jnp.where(tail, part(then), part(first))
+                mid = jnp.where(tail, part(then + 1), part(first + 1))
+                return jnp.where(mids, mid, jnp.where(low, part(first + 2), high))
+
+            upper = six(0, 3)
+            lower = jnp.where(is_in(1), part(4), jnp.where(third, part(5), part(3)))
+            lower = jnp.where(rows >= 4, units, lower)
+            at = col * span + 1 + z
+            lanes[0, at] = jnp.concatenate([upper, lower], 0).astype(jnp.bfloat16)
             for shift in range(3):
-                lanes[1 + shift, col * span + 1 + z] = side[shift, pl.ds(at, 16), :].astype(
-                    jnp.bfloat16
-                )
+                p = 6 + shift * 6
+                upper = six(p, p + 3)
+                lower = jnp.where(head, part(p + 5), zero)
+                lanes[1 + shift, at] = jnp.concatenate([upper, lower], 0).astype(jnp.bfloat16)
         return 0
 
     lax.fori_loop(0, levels // 4, narrow, 0)
 
 
-def make_rows(raw, base, row, levels, corner_x, corner_y, tall, lefts):
-    zero = jnp.zeros((8, 128), jnp.float32)
-    one = jnp.ones((8, 128), jnp.float32)
+def make_rows(raw, base, row, levels, corner_x, corner_y, valid, parts, lefts):
+    rows = lax.broadcasted_iota(jnp.int32, (8, 128), 0)
 
     def chunk(k, _):
-        level = k * 8
+        level = pl.multiple_of(k * 8, 8)
         first = pl.multiple_of((base + level) * 4, 32)
-        x, y, z, f = load_points(raw, first, corner_x, corner_y, level, None)
-        norm = split3(x * x + y * y + z * z)
-        parts = []
+        x, y, z, f = load_points(raw, first, corner_x, corner_y, level, valid)
+        found = []
         for value in (x, y, z):
-            high, mid, low = split3(value)
-            high, mid, low = -2.0 * high, -2.0 * mid, -2.0 * low
-            parts.append([high, high, mid, mid, high, low])
-        rows = parts[0] + parts[1] + [norm[0], norm[1], norm[2], zero]
-        rows += parts[2] + [one, one, one] + list(split3(f)) + [zero] * 4
-        for r, value in enumerate(rows):
-            tall[pl.ds(level * 32 + r, 8, 32), :] = value
+            found += [-2.0 * part for part in split3(value)]
+        found += [*split3(x * x + y * y + z * z), *split3(f)]
+        for p, value in enumerate(found):
+            parts[p, pl.ds(level, 8), :] = value
         return 0
 
     lax.fori_loop(0, levels // 8, chunk, 0)
+
+    def pick(choices):
+        value = choices[-1][1]
+        for which, other in choices[:-1]:
+            hit = functools.reduce(jnp.logical_or, [rows == r for r in which])
+            value = jnp.where(hit, other, value)
+        return value
 
     def narrow(k, _):
         for u in range(4):
             z = k * 4 + u
-            lefts[row * levels + z] = tall[pl.ds(pl.multiple_of(z * 32, 32), 32), :].astype(
-                jnp.bfloat16
-            )
+
+            def part(p, z=z):
+                return jnp.broadcast_to(parts[p, pl.ds(z, 1), :], (8, 128))
+
+            tile = [
+                pick([((2, 3), part(1)), ((5,), part(2)), ((6, 7), part(3)), ((), part(0))]),
+                pick(
+                    [
+                        ((0, 1), part(4)),
+                        ((2,), part(3)),
+                        ((3,), part(5)),
+                        ((4,), part(9)),
+                        ((5,), part(10)),
+                        ((6,), part(11)),
+                        ((), jnp.zeros((8, 128), jnp.float32)),
+                    ]
+                ),
+                pick(
+                    [
+                        ((2, 3), part(7)),
+                        ((5,), part(8)),
+                        ((6, 7), jnp.ones((8, 128), jnp.float32)),
+                        ((), part(6)),
+                    ]
+                ),
+                pick(
+                    [
+                        ((1,), part(12)),
+                        ((2,), part(13)),
+                        ((3,), part(14)),
+                        ((), jnp.where(rows == 0, 1.0, 0.0)),
+                    ]
+                ),
+            ]
+            lefts[row * levels + z] = jnp.concatenate(tile, 0).astype(jnp.bfloat16)
         return 0
 
     lax.fori_loop(0, levels // 4, narrow, 0)
@@ -343,7 +387,7 @@
 
 
 def far_tasks():
-    wanted = ((0, (0, 1)), (1, (2, 3, 4)), (2, (0, 1, 3, 4, 5)))
+    wanted = ((0, (0, 1)), (1, (2, 3)), (2, (0, 1, 2, 3, 4)), (3, (1,)))
     return [
         (row, [(col, shift, True) for col in cols for shift in (-1, 0, 1)])
         for row, cols in wanted
@@ -360,13 +404,15 @@
     count = 4 - first
     starts, refs = (refs[:2], refs[2:]) if first else (None, refs)
     (out_n, out_s), scratch = refs[:2], refs[2:]
-    flat, side, lanes, values, tall, lefts, col_n, col_s, row_n, row_s = scratch
+    parts, lanes, values, lefts, col_n, col_s, row_n, row_s = scratch
     corner_x, corner_y = corners()
     for col in range(count):
         base = (col + first) * levels
-        make_lanes(raw, base, col, levels, corner_x, corner_y, None, flat, side, lanes, values)
+        make_lanes(raw, base, col, levels, corner_x, corner_y, None, parts, lanes, values)
     for row in range(last - first):
-        make_rows(raw, (row + first) * levels, row, levels, corner_x, corner_y, tall, lefts)
+        make_rows(
+            raw, (row + first) * levels, row, levels, corner_x, corner_y, None, parts, lefts
+        )
     tasks = [
         (row - first, [(col - first, shift, both) for col, shift, both in tiles])
         for row, tiles in own_tasks(range(first, last))
@@ -391,46 +437,41 @@
         out_s[col] = s
 
 
-def far_kernel(raw, dom_raw, slab_raw, up_raw, down_raw, *refs, levels, half, unroll, slabs, doms):
-    start_n, start_s, out_n, out_s, to_dom, to_slab, to_up, to_down = refs[:8]
-    flat, side, lanes, values, tall, lefts, col_n, col_s, row_n, row_s = refs[8:]
+def far_kernel(raw, dom_raw, slab_raw, edge_raw, *refs, levels, half, unroll, slabs, doms):
+    start_n, start_s, out_n, out_s, to_dom, to_slab, to_edge = refs[:7]
+    parts, lanes, values, lefts, col_n, col_s, row_n, row_s = refs[7:]
     corner_x, corner_y = corners()
-    slab, dom = lax.axis_index("slab"), lax.axis_index("dom")
-    next_slab = slab + 1 < slabs
-    next_dom = dom + 1 < doms
-    previous_dom = dom > 0
+    next_slab = lax.axis_index("slab") + 1 < slabs
+    next_dom = lax.axis_index("dom") + 1 < doms
     sources = (
         (dom_raw, 0, next_dom),
         (dom_raw, levels, next_dom),
-        (down_raw, 0, jnp.logical_and(next_slab, previous_dom)),
         (slab_raw, 0, next_slab),
         (slab_raw, levels, next_slab),
-        (up_raw, 0, jnp.logical_and(next_slab, next_dom)),
+        (edge_raw, 0, jnp.logical_and(next_slab, next_dom)),
     )
     for col, (source, base, valid) in enumerate(sources):
-        make_lanes(
-            source, base, col, levels, corner_x, corner_y, valid, flat, side, lanes, values
-        )
+        make_lanes(source, base, col, levels, corner_x, corner_y, valid, parts, lanes, values)
     for row in range(3):
-        make_rows(raw, (row + 1) * levels, row, levels, corner_x, corner_y, tall, lefts)
+        make_rows(raw, (row + 1) * levels, row, levels, corner_x, corner_y, None, parts, lefts)
+    make_rows(slab_raw, levels, 3, levels, corner_x, corner_y, next_slab, parts, lefts)
     pair_sums(
         far_tasks(), levels, lefts, lanes, values, col_n, col_s, row_n, row_s, half, unroll
     )
-    out_n[0] = start_n[0]
-    out_s[0] = start_s[0]
-    for row in range(3):
-        out_n[row + 1] = start_n[row + 1] + jnp.transpose(row_n[row])[:levels]
-        out_s[row + 1] = start_s[row + 1] + jnp.transpose(row_s[row])[:levels]
-    for channel, ref in enumerate((col_n, col_s)):
-        for k in range(2):
-            to_dom[channel, k] = fold_column(ref, k, levels)
-            to_slab[channel, k] = fold_column(ref, 3 + k, levels)
-        to_down[channel] = fold_column(ref, 2, levels)
-        to_up[channel] = fold_column(ref, 5, levels)
+    for start, out, totals in ((start_n, out_n, row_n), (start_s, out_s, row_s)):
+        out[0] = start[0]
+        for row in range(3):
+            out[row + 1] = start[row + 1] + jnp.transpose(totals[row])[:levels]
+    for channel, (ref, totals) in enumerate(((col_n, row_n), (col_s, row_s))):
+        to_dom[channel, 0] = fold_column(ref, 0, levels)
+        to_dom[channel, 1] = fold_column(ref, 1, levels)
+        to_slab[channel, 0] = fold_column(ref, 2, levels)
+        to_slab[channel, 1] = fold_column(ref, 3, levels) + jnp.transpose(totals[3])[:levels]
+        to_edge[channel] = fold_column(ref, 4, levels)
 
 
 def finish_kernel(raw, own_n, own_s, *refs, levels):
-    from_dom, from_slab, from_up, from_down, density, laplace = refs
+    from_dom, from_slab, from_edge, density, laplace = refs
     for col in range(4):
         sums = []
         for channel, near in enumerate((own_n, own_s)):
@@ -440,9 +481,7 @@
             if col in (0, 1):
                 total = total + from_slab[channel, col]
             if col == 0:
-                total = total + from_up[channel]
-            if col == 1:
-                total = total + from_down[channel]
+                total = total + from_edge[channel]
             sums.append(total)
         filled = raw[pl.ds(col * levels * 4, levels, 4), :] > 0.5 * far_away
         n = jnp.where(filled, sums[0], 0.0)
@@ -456,11 +495,9 @@
     span = levels + 2
     f32, bf16 = jnp.float32, jnp.bfloat16
     return [
-        pltpu.VMEM((levels * 16, 128), f32),
-        pltpu.VMEM((3, levels * 16, 128), f32),
+        pltpu.VMEM((24, levels, 128), f32),
         pltpu.VMEM((4, cols * span, 16, 128), bf16),
         pltpu.VMEM((cols * (levels + 16), 128), f32),
-        pltpu.VMEM((levels * 32, 128), f32),
         pltpu.VMEM((rows * levels, 32, 128), bf16),
         pltpu.VMEM((cols * span * 8, 128), f32),
         pltpu.VMEM((cols * span * 8, 128), f32),
@@ -500,13 +537,13 @@
         for step, pack in zip(offsets, packs)
     ]
     column = (levels, 4, slots)
-    home, to_dom, to_slab, to_up, to_down = pl.pallas_call(
+    home, to_dom, to_slab, to_edge = pl.pallas_call(
         functools.partial(place_kernel, cells=cells, capacity=capacity, levels=levels),
         out_shape=[shape((cells, 4, slots), f32)]
         + [shape((2 * levels, 4, slots), f32)] * 2
-        + [shape(column, f32)] * 2,
+        + [shape(column, f32)],
         in_specs=[vmem] * 5 + [smem],
-        out_specs=[vmem] * 5,
+        out_specs=[vmem] * 4,
         scratch_shapes=[
             pltpu.VMEM((cells + 1, 4, slots), f32),
             pltpu.VMEM((4, 4, 128), i32),
@@ -535,8 +572,7 @@
 
     slab_raw = send(to_slab, -1, 0)
     dom_raw = send(to_dom, 0, -1)
-    up_raw = send(to_up, -1, -1)
-    down_raw = send(to_down, -1, 1)
+    edge_raw = send(to_edge, -1, -1)
     raw = rows_of(home)
     half = 128
     plane = (4, levels, slots)
@@ -563,41 +599,32 @@
         )(raw, *start)
 
     early_n, early_s = own_pairs(0, 1, 4)
-    far_n, far_s, ret_dom, ret_slab, ret_up, ret_down = pl.pallas_call(
+    far_n, far_s, ret_dom, ret_slab, ret_edge = pl.pallas_call(
         functools.partial(
             far_kernel, levels=levels, half=half, unroll=4, slabs=slabs, doms=doms
         ),
         out_shape=[shape(plane, f32)] * 2
         + [shape((2, 2, levels, slots), f32)] * 2
-        + [shape((2, levels, slots), f32)] * 2,
-        in_specs=[vmem] * 7,
-        out_specs=[vmem] * 6,
-        scratch_shapes=scratch_for(levels, 6, 3),
+        + [shape((2, levels, slots), f32)],
+        in_specs=[vmem] * 6,
+        out_specs=[vmem] * 5,
+        scratch_shapes=scratch_for(levels, 5, 4),
         compiler_params=params,
         cost_estimate=cost(30),
         name="far",
-    )(
-        raw,
-        rows_of(dom_raw),
-        rows_of(slab_raw),
-        rows_of(up_raw),
-        rows_of(down_raw),
-        early_n,
-        early_s,
-    )
+    )(raw, rows_of(dom_raw), rows_of(slab_raw), rows_of(edge_raw), early_n, early_s)
     from_slab = send(ret_slab, 1, 0)
     from_dom = send(ret_dom, 0, 1)
-    from_up = send(ret_up, 1, 1)
-    from_down = send(ret_down, 1, -1)
+    from_edge = send(ret_edge, 1, 1)
     own_n, own_s = own_pairs(1, 4, 4, far_n, far_s)
     density, laplace = pl.pallas_call(
         functools.partial(finish_kernel, levels=levels),
         out_shape=[shape(plane, f32)] * 2,
-        in_specs=[vmem] * 7,
+        in_specs=[vmem] * 6,
         out_specs=[vmem] * 2,
         compiler_params=params,
         name="finish",
-    )(raw, own_n, own_s, from_dom, from_slab, from_up, from_down)
+    )(raw, own_n, own_s, from_dom, from_slab, from_edge)
     final = (cells_x, cells_y, levels, slots)
     return density.reshape(final), laplace.reshape(final)
 

time: 169 us -> 161 us (0.953)
  starting transfers between devices: 29.4 us -> 24.1 us
    ppermute x8 -> x6, starting transfers between devices: 23 us -> 17.7 us  [send(): return lax.ppermute(value, both, route(step_slab, step_dom))]
    pallas_call x2, Pallas kernels: 57.1 us -> 55.3 us  [own_pairs(): pl.pallas_call(functools.partial(own_kernel, levels=levels, half=half, un...]
  transfers between devices with their start and end apart: 12 -> 10, of which waited for: 4 -> 4; matrix products, arithmetic and copies ran while one was open for 0% -> 0% of each run, Pallas kernels for 34% -> 34%
where the time goes in v3:
time: 161 us; the launch traced here: 160 us
  Pallas kernels  126 us (78%)
  starting transfers between devices  24.1 us (15%)
  waiting for transfers between devices  7.75 us (5%)
  local copies, waits for them, and re-layouts  2.16 us (1%)
    pallas_call x1, Pallas kernels, local(): pl.pallas_call(functools.partial(far_kernel, levels=levels, half=half, un...  58.5 us
    pallas_call x2, Pallas kernels, own_pairs(): pl.pallas_call(functools.partial(own_kernel, levels=levels, half=half, un...  55.3 us
    ppermute x6, starting transfers between devices, send(): return lax.ppermute(value, both, route(step_slab, step_dom))  17.7 us
    ppermute x4, waiting for transfers between devices, local(): lax.ppermute(pack, 'dom', [(i, (i + step) % doms) for i in range(doms)])  7.74 us
    ppermute x4, starting transfers between devices, local(): lax.ppermute(pack, 'dom', [(i, (i + step) % doms) for i in range(doms)])  6.32 us
    pallas_call x1, Pallas kernels, local(): pl.pallas_call(functools.partial(place_kernel, cells=cells, capacity=capa...  5.29 us
    pallas_call x1, Pallas kernels, local(): pl.pallas_call(functools.partial(pack_kernel, cells=cells, capacity=capac...  4.58 us
  transfers between devices with their start and end apart: 10, of which 4 were waited for; matrix products, arithmetic and copies ran while one was open for 0% of the time, Pallas kernels for 34%

profile of v3, /device:TPU:0, one launch (start us, length us, event | category | flops | bytes accessed | tf_op | source)
XLA Modules:
  0.0 160.4 jit_solution(12985911940585799330)
XLA Ops:
  0.6 4.6 %pack.1 = (f32[65,4,128]{2,1,0:T(4,128)}, f32[65,4,128]{2,1,0:T(4,128)}, f32[65,4,128]{2,1,0:T(4,128)}, f32[65,4,128]{2,1,0:T(4,128)}, f32[256,4,128]{2,1,0:T(4,128)}) custom-call(s32[2,128]{1,0:T(2,128)} %bitcast.13, f32[256,4,128]{2,1,0:T(4,128)} %bitcast.8), custom_call_target="tpu_custom_call" | custom-call | tf_op jit(solution)/shard_map/pack/pallas_call | solution.py:521
  5.2 5.1 %collective-permute-start = (f32[65,4,128]{2,1,0:T(4,128)}, f32[65,4,128]{2,1,0:T(4,128)S(1)}, u32[]{:S(2)}, u32[]{:S(2)}) collective-permute-start(f32[65,4,128]{2,1,0:T(4,128)} %get-tuple-element.22), channel_id=1, source_target_pairs={{0,6},{1,7},{2,0},{3,1},{4,2},{5,3},{6,4},{7,5},{8,14},{9,15},{10,... | collective-permute-start | bytes 399368 | tf_op jit(solution)/shard_map/ppermute | solution.py:536
  10.3 0.0 collective-permute-start.1
  10.4 0.5 collective-permute-start.2
  10.9 0.7 collective-permute-start.3
  11.5 3.1 %collective-permute-done.refs_0_ = f32[65,4,128]{2,1,0:T(4,128)S(1)} collective-permute-done((f32[65,4,128]{2,1,0:T(4,128)}, f32[65,4,128]{2,1,0:T(4,128)S(1)}, u32[]{:S(2)}, u32[]{:S(2)}) %collective-permute-start) | collective-permute-done | bytes 133152 | tf_op jit(solution)/shard_map/ppermute | solution.py:536
  14.6 0.0 copy-start
  14.6 2.9 %collective-permute-done.1.refs_1_ = f32[65,4,128]{2,1,0:T(4,128)S(1)} collective-permute-done((f32[65,4,128]{2,1,0:T(4,128)}, f32[65,4,128]{2,1,0:T(4,128)S(1)}, u32[]{:S(2)}, u32[]{:S(2)}) %collective-permute-start.1) | collective-permute-done | bytes 133152 | tf_op jit(solution)/shard_map/ppermute | solution.py:536
  17.4 0.0 copy-start.1
  17.4 0.3 collective-permute-done.2.refs_2_
  17.8 0.0 copy-start.2
  17.8 1.5 collective-permute-done.3.refs_3_
  19.3 0.0 copy-start.3
  19.3 0.0 copy-done
  19.3 0.0 copy-done.1
  19.3 0.0 copy-done.2
  19.3 0.6 copy-done.3
  19.9 5.3 %place.1 = (f32[256,4,128]{2,1,0:T(4,128)}, f32[128,4,128]{2,1,0:T(4,128)}, f32[128,4,128]{2,1,0:T(4,128)}, f32[64,4,128]{2,1,0:T(4,128)}) custom-call(f32[65,4,128]{2,1,0:T(4,128)} %copy-done, f32[65,4,128]{2,1,0:T(4,128)} %copy-done.1, f32[65,4,128]{2,1,0:T(4,128)} %copy-done.2, f32[65,4,128]{2,1,0:T(4,128)} %copy-done.3, ...), custom_call_target="tpu_custom_call" | custom-call | tf_op jit(solution)/shard_map/place/pallas_call | solution.py:540
  25.2 1.3 collective-permute-start.6
  26.5 1.3 collective-permute-start.4
  27.8 1.3 collective-permute-start.5
  29.1 24.4 %own.2 = (f32[4,64,128]{2,1,0:T(8,128)}, f32[4,64,128]{2,1,0:T(8,128)}) custom-call(f32[1024,128]{1,0:T(8,128)} %bitcast.9), custom_call_target="tpu_custom_call" | custom-call | flops 16357785600 | bytes 524288 | tf_op jit(solution)/shard_map/own/pallas_call | solution.py:588
  53.5 0.0 collective-permute-done.6
  53.5 0.0 copy-start.9
  53.5 0.0 collective-permute-done.4
  53.5 0.0 copy-start.7
  53.5 0.0 collective-permute-done.5
  53.5 0.0 copy-start.8
  53.5 0.6 copy-done.9
  54.2 0.1 copy-done.7
  54.2 0.1 copy-done.8
  54.3 58.5 %far.1 = (f32[4,64,128]{2,1,0:T(8,128)}, f32[4,64,128]{2,1,0:T(8,128)}, f32[2,2,64,128]{3,2,1,0:T(8,128)}, f32[2,2,64,128]{3,2,1,0:T(8,128)}, f32[2,64,128]{2,1,0:T(8,128)}) custom-call(f32[1024,128]{1,0:T(8,128)} %bitcast.10, f32[512,128]{1,0:T(8,128)} %bitcast.14, f32[512,128]{1,0:T(8,128)} %bitcast.15, f32[256,128]{1,0:T(8,128)} %bitcast.16, ...), custom_call_target="tpu_custom_call" | custom-call | flops 18874368000 | bytes 524288 | tf_op jit(solution)/shard_map/far/pallas_call | solution.py:602
  112.8 5.5 %collective-permute-start.9 = (f32[2,64,128]{2,1,0:T(8,128)}, f32[2,64,128]{2,1,0:T(8,128)S(1)}, u32[]{:S(2)}, u32[]{:S(2)}) collective-permute-start(f32[2,64,128]{2,1,0:T(8,128)} %get-tuple-element.39), channel_id=1, source_target_pairs={{0,9},{1,10},{2,11},{3,12},{4,13},{5,14},{6,15},{8,17},{9,18},{10,... | collective-permute-start | bytes 196616 | tf_op jit(solution)/shard_map/ppermute | solution.py:568
  118.3 3.5 %collective-permute-start.7 = (f32[2,2,64,128]{3,2,1,0:T(8,128)}, f32[2,2,64,128]{3,2,1,0:T(8,128)S(1)}, u32[]{:S(2)}, u32[]{:S(2)}) collective-permute-start(f32[2,2,64,128]{3,2,1,0:T(8,128)} %get-tuple-element.37), channel_id=1, source_target_pairs={{0,1},{1,2},{2,3},{3,4},{4,5},{5,6},{6,7},{8,9},{9,10},{10,11},{11... | collective-permute-start | bytes 393224 | tf_op jit(solution)/shard_map/ppermute | solution.py:568
  121.9 4.8 %collective-permute-start.8 = (f32[2,2,64,128]{3,2,1,0:T(8,128)}, f32[2,2,64,128]{3,2,1,0:T(8,128)S(1)}, u32[]{:S(2)}, u32[]{:S(2)}) collective-permute-start(f32[2,2,64,128]{3,2,1,0:T(8,128)} %get-tuple-element.38), channel_id=1, source_target_pairs={{0,8},{1,9},{2,10},{3,11},{4,12},{5,13},{6,14},{7,15},{8,16},{9,17... | collective-permute-start | bytes 393224 | tf_op jit(solution)/shard_map/ppermute | solution.py:568
  126.7 31.0 %own.3 = (f32[4,64,128]{2,1,0:T(8,128)}, f32[4,64,128]{2,1,0:T(8,128)}) custom-call(f32[1024,128]{1,0:T(8,128)} %bitcast.11, f32[4,64,128]{2,1,0:T(8,128)} %get-tuple-element.33.refs_0_, f32[4,64,128]{2,1,0:T(8,128)} %get-tuple-element.34.refs_1_), custom_call_target="tpu_custom_call" | custom-call | flops 16357785600 | bytes 524288 | tf_op jit(solution)/shard_map/own/pallas_call | solution.py:588
  157.7 0.0 collective-permute-done.9.refs_2_
  157.7 0.0 copy-start.6
  157.7 0.0 collective-permute-done.7.refs_0_
  157.7 0.0 copy-start.4
  157.7 0.0 collective-permute-done.8.refs_1_
  157.7 0.0 copy-start.5
  157.7 0.6 copy-done.6
  158.3 0.1 copy-done.4
  158.3 0.0 copy-done.5
  158.4 2.0 %finish.1 = (f32[4,64,128]{2,1,0:T(8,128)}, f32[4,64,128]{2,1,0:T(8,128)}) custom-call(f32[1024,128]{1,0:T(8,128)} %bitcast.12, f32[4,64,128]{2,1,0:T(8,128)} %get-tuple-element.35.own_n, f32[4,64,128]{2,1,0:T(8,128)} %get-tuple-element.36.own_s, f32[2,2,64,128]{3,2,1,0:T(8,128)} %copy-done.4, f32[2,2,64,128]{3,2,1,0:T(8,128)} %copy-done.5, ...), custom_call_target="tpu_custom_call" | custom-call | tf_op jit(solution)/shard_map/finish/pallas_call | solution.py:620
Async XLA Ops:
  5.2 9.4 %collective-permute-start = (f32[65,4,128]{2,1,0:T(4,128)}, f32[65,4,128]{2,1,0:T(4,128)S(1)}, u32[]{:S(2)}, u32[]{:S(2)}) collective-permute-start(f32[65,4,128]{2,1,0:T(4,128)} %get-tuple-element.22), channel_id=1, source_target_pairs={{0,6},{1,7},{2,0},{3,1},{4,2},{5,3},{6,4},{7,5},{8,14},{9,15},{10,... | collective-permute-start | bytes 399368 | tf_op jit(solution)/shard_map/ppermute | solution.py:536
  10.3 7.1 %collective-permute-start.1 = (f32[65,4,128]{2,1,0:T(4,128)}, f32[65,4,128]{2,1,0:T(4,128)S(1)}, u32[]{:S(2)}, u32[]{:S(2)}) collective-permute-start(f32[65,4,128]{2,1,0:T(4,128)} %get-tuple-element.23), channel_id=1, source_target_pairs={{0,7},{1,0},{2,1},{3,2},{4,3},{5,4},{6,5},{7,6},{8,15},{9,8},{10,9... | collective-permute-start | bytes 399368 | tf_op jit(solution)/shard_map/ppermute | solution.py:536
  10.4 7.4 %collective-permute-start.2 = (f32[65,4,128]{2,1,0:T(4,128)}, f32[65,4,128]{2,1,0:T(4,128)S(1)}, u32[]{:S(2)}, u32[]{:S(2)}) collective-permute-start(f32[65,4,128]{2,1,0:T(4,128)} %get-tuple-element.24), channel_id=1, source_target_pairs={{0,1},{1,2},{2,3},{3,4},{4,5},{5,6},{6,7},{7,0},{8,9},{9,10},{10,1... | collective-permute-start | bytes 399368 | tf_op jit(solution)/shard_map/ppermute | solution.py:536
  10.9 8.4 %collective-permute-start.3 = (f32[65,4,128]{2,1,0:T(4,128)}, f32[65,4,128]{2,1,0:T(4,128)S(1)}, u32[]{:S(2)}, u32[]{:S(2)}) collective-permute-start(f32[65,4,128]{2,1,0:T(4,128)} %get-tuple-element.25), channel_id=1, source_target_pairs={{0,2},{1,3},{2,4},{3,5},{4,6},{5,7},{6,0},{7,1},{8,10},{9,11},{10,... | collective-permute-start | bytes 399368 | tf_op jit(solution)/shard_map/ppermute | solution.py:536
  14.6 4.7 %copy-start = (f32[65,4,128]{2,1,0:T(4,128)}, f32[65,4,128]{2,1,0:T(4,128)S(1)}, u32[]{:S(2)}) copy-start(f32[65,4,128]{2,1,0:T(4,128)S(1)} %collective-permute-done.refs_0_) | copy-start | bytes 399364
  17.4 1.8 %copy-start.1 = (f32[65,4,128]{2,1,0:T(4,128)}, f32[65,4,128]{2,1,0:T(4,128)S(1)}, u32[]{:S(2)}) copy-start(f32[65,4,128]{2,1,0:T(4,128)S(1)} %collective-permute-done.1.refs_1_) | copy-start | bytes 399364
  17.8 1.5 copy-start.2
  19.3 0.7 copy-start.3
  25.2 28.3 %collective-permute-start.6 = (f32[64,4,128]{2,1,0:T(4,128)}, f32[64,4,128]{2,1,0:T(4,128)S(1)}, u32[]{:S(2)}, u32[]{:S(2)}) collective-permute-start(f32[64,4,128]{2,1,0:T(4,128)} %get-tuple-element.30), channel_id=1, source_target_pairs={{9,0},{10,1},{11,2},{12,3},{13,4},{14,5},{15,6},{17,8},{18,9},{19,... | collective-permute-start | bytes 393224 | tf_op jit(solution)/shard_map/ppermute | solution.py:568
  26.5 27.0 %collective-permute-start.4 = (f32[128,4,128]{2,1,0:T(4,128)}, f32[128,4,128]{2,1,0:T(4,128)S(1)}, u32[]{:S(2)}, u32[]{:S(2)}) collective-permute-start(f32[128,4,128]{2,1,0:T(4,128)} %get-tuple-element.28), channel_id=1, source_target_pairs={{1,0},{2,1},{3,2},{4,3},{5,4},{6,5},{7,6},{9,8},{10,9},{11,10},{12... | collective-permute-start | bytes 786440 | tf_op jit(solution)/shard_map/ppermute | solution.py:568
  27.8 25.7 %collective-permute-start.5 = (f32[128,4,128]{2,1,0:T(4,128)}, f32[128,4,128]{2,1,0:T(4,128)S(1)}, u32[]{:S(2)}, u32[]{:S(2)}) collective-permute-start(f32[128,4,128]{2,1,0:T(4,128)} %get-tuple-element.29), channel_id=1, source_target_pairs={{8,0},{9,1},{10,2},{11,3},{12,4},{13,5},{14,6},{15,7},{16,8},{17,9... | collective-permute-start | bytes 786440 | tf_op jit(solution)/shard_map/ppermute | solution.py:568
  53.5 0.7 copy-start.9
  53.5 0.7 copy-start.7
  53.5 0.8 copy-start.8
  112.8 44.8 %collective-permute-start.9 = (f32[2,64,128]{2,1,0:T(8,128)}, f32[2,64,128]{2,1,0:T(8,128)S(1)}, u32[]{:S(2)}, u32[]{:S(2)}) collective-permute-start(f32[2,64,128]{2,1,0:T(8,128)} %get-tuple-element.39), channel_id=1, source_target_pairs={{0,9},{1,10},{2,11},{3,12},{4,13},{5,14},{6,15},{8,17},{9,18},{10,... | collective-permute-start | bytes 196616 | tf_op jit(solution)/shard_map/ppermute | solution.py:568
  118.3 39.3 %collective-permute-start.7 = (f32[2,2,64,128]{3,2,1,0:T(8,128)}, f32[2,2,64,128]{3,2,1,0:T(8,128)S(1)}, u32[]{:S(2)}, u32[]{:S(2)}) collective-permute-start(f32[2,2,64,128]{3,2,1,0:T(8,128)} %get-tuple-element.37), channel_id=1, source_target_pairs={{0,1},{1,2},{2,3},{3,4},{4,5},{5,6},{6,7},{8,9},{9,10},{10,11},{11... | collective-permute-start | bytes 393224 | tf_op jit(solution)/shard_map/ppermute | solution.py:568
  121.9 35.8 %collective-permute-start.8 = (f32[2,2,64,128]{3,2,1,0:T(8,128)}, f32[2,2,64,128]{3,2,1,0:T(8,128)S(1)}, u32[]{:S(2)}, u32[]{:S(2)}) collective-permute-start(f32[2,2,64,128]{3,2,1,0:T(8,128)} %get-tuple-element.38), channel_id=1, source_target_pairs={{0,8},{1,9},{2,10},{3,11},{4,12},{5,13},{6,14},{7,15},{8,16},{9,17... | collective-permute-start | bytes 393224 | tf_op jit(solution)/shard_map/ppermute | solution.py:568
  157.7 0.6 copy-start.6
  157.7 0.7 copy-start.4
  157.7 0.7 copy-start.5

commit v4 on v3

--- a/solution.py
+++ b/solution.py
@@ -463,11 +463,14 @@
         for row in range(3):
             out[row + 1] = start[row + 1] + jnp.transpose(totals[row])[:levels]
     for channel, (ref, totals) in enumerate(((col_n, row_n), (col_s, row_s))):
-        to_dom[channel, 0] = fold_column(ref, 0, levels)
-        to_dom[channel, 1] = fold_column(ref, 1, levels)
-        to_slab[channel, 0] = fold_column(ref, 2, levels)
-        to_slab[channel, 1] = fold_column(ref, 3, levels) + jnp.transpose(totals[3])[:levels]
-        to_edge[channel] = fold_column(ref, 4, levels)
+        for k in range(2):
+            to_dom[channel, k] = jnp.where(next_dom, fold_column(ref, k, levels), 0.0)
+        near = fold_column(ref, 2, levels)
+        to_slab[channel, 0] = jnp.where(next_slab, near, 0.0)
+        near = fold_column(ref, 3, levels) + jnp.transpose(totals[3])[:levels]
+        to_slab[channel, 1] = jnp.where(next_slab, near, 0.0)
+        near = fold_column(ref, 4, levels)
+        to_edge[channel] = jnp.where(jnp.logical_and(next_slab, next_dom), near, 0.0)
 
 
 def finish_kernel(raw, own_n, own_s, *refs, levels):
@@ -557,12 +560,11 @@
     both = ("slab", "dom")
 
     def route(step_slab, step_dom):
-        pairs = []
-        for s in range(slabs):
-            for d in range(doms):
-                if 0 <= s + step_slab < slabs and 0 <= d + step_dom < doms:
-                    pairs.append((s * doms + d, (s + step_slab) * doms + d + step_dom))
-        return pairs
+        return [
+            (s * doms + d, (s + step_slab) % slabs * doms + (d + step_dom) % doms)
+            for s in range(slabs)
+            for d in range(doms)
+        ]
 
     def send(value, step_slab, step_dom):
         return lax.ppermute(value, both, route(step_slab, step_dom))

time: 161 us -> 150 us (0.932)
  starting transfers between devices: 24.1 us -> 13.3 us
    ppermute x6, starting transfers between devices: 17.7 us -> 7.03 us  [send(): return lax.ppermute(value, both, route(step_slab, step_dom))]
  transfers between devices with their start and end apart: 10 -> 10, of which waited for: 4 -> 4; matrix products, arithmetic and copies ran while one was open for 0% -> 0% of each run, Pallas kernels for 34% -> 37%
where the time goes in v4:
time: 150 us
  Pallas kernels  126 us (84%)
  starting transfers between devices  13.3 us (9%)
  waiting for transfers between devices  7.75 us (5%)
  local copies, waits for them, and re-layouts  2.16 us (1%)
    pallas_call x1, Pallas kernels, local(): pl.pallas_call(functools.partial(far_kernel, levels=levels, half=half, un...  58.4 us
    pallas_call x2, Pallas kernels, own_pairs(): pl.pallas_call(functools.partial(own_kernel, levels=levels, half=half, un...  55.3 us
    ppermute x4, waiting for transfers between devices, local(): lax.ppermute(pack, 'dom', [(i, (i + step) % doms) for i in range(doms)])  7.74 us
    ppermute x6, starting transfers between devices, send(): return lax.ppermute(value, both, route(step_slab, step_dom))  7.03 us
    ppermute x4, starting transfers between devices, local(): lax.ppermute(pack, 'dom', [(i, (i + step) % doms) for i in range(doms)])  6.32 us
    pallas_call x1, Pallas kernels, local(): pl.pallas_call(functools.partial(place_kernel, cells=cells, capacity=capa...  5.29 us
    pallas_call x1, Pallas kernels, local(): pl.pallas_call(functools.partial(pack_kernel, cells=cells, capacity=capac...  4.58 us
  transfers between devices with their start and end apart: 10, of which 4 were waited for; matrix products, arithmetic and copies ran while one was open for 0% of the time, Pallas kernels for 37%

profile of v4, /device:TPU:0, one launch (start us, length us, event | category | flops | bytes accessed | tf_op | source)
XLA Modules:
  0.0 149.6 jit_solution(16702517289139764685)
XLA Ops:
  0.6 4.6 %pack.1 = (f32[65,4,128]{2,1,0:T(4,128)}, f32[65,4,128]{2,1,0:T(4,128)}, f32[65,4,128]{2,1,0:T(4,128)}, f32[65,4,128]{2,1,0:T(4,128)}, f32[256,4,128]{2,1,0:T(4,128)}) custom-call(s32[2,128]{1,0:T(2,128)} %bitcast.13, f32[256,4,128]{2,1,0:T(4,128)} %bitcast.8), custom_call_target="tpu_custom_call" | custom-call | tf_op jit(solution)/shard_map/pack/pallas_call | solution.py:524
  5.2 5.1 %collective-permute-start = (f32[65,4,128]{2,1,0:T(4,128)}, f32[65,4,128]{2,1,0:T(4,128)S(1)}, u32[]{:S(2)}, u32[]{:S(2)}) collective-permute-start(f32[65,4,128]{2,1,0:T(4,128)} %get-tuple-element.22), channel_id=1, source_target_pairs={{0,6},{1,7},{2,0},{3,1},{4,2},{5,3},{6,4},{7,5},{8,14},{9,15},{10,... | collective-permute-start | bytes 399368 | tf_op jit(solution)/shard_map/ppermute | solution.py:539
  10.3 0.0 collective-permute-start.1
  10.4 0.5 collective-permute-start.2
  10.9 0.7 collective-permute-start.3
  11.5 3.1 %collective-permute-done.refs_0_ = f32[65,4,128]{2,1,0:T(4,128)S(1)} collective-permute-done((f32[65,4,128]{2,1,0:T(4,128)}, f32[65,4,128]{2,1,0:T(4,128)S(1)}, u32[]{:S(2)}, u32[]{:S(2)}) %collective-permute-start) | collective-permute-done | bytes 133152 | tf_op jit(solution)/shard_map/ppermute | solution.py:539
  14.6 0.0 copy-start
  14.6 2.9 %collective-permute-done.1.refs_1_ = f32[65,4,128]{2,1,0:T(4,128)S(1)} collective-permute-done((f32[65,4,128]{2,1,0:T(4,128)}, f32[65,4,128]{2,1,0:T(4,128)S(1)}, u32[]{:S(2)}, u32[]{:S(2)}) %collective-permute-start.1) | collective-permute-done | bytes 133152 | tf_op jit(solution)/shard_map/ppermute | solution.py:539
  17.4 0.0 copy-start.1
  17.4 0.3 collective-permute-done.2.refs_2_
  17.8 0.0 copy-start.2
  17.8 1.5 collective-permute-done.3.refs_3_
  19.3 0.0 copy-start.3
  19.3 0.0 copy-done
  19.3 0.0 copy-done.1
  19.3 0.0 copy-done.2
  19.3 0.6 copy-done.3
  19.9 5.3 %place.1 = (f32[256,4,128]{2,1,0:T(4,128)}, f32[128,4,128]{2,1,0:T(4,128)}, f32[128,4,128]{2,1,0:T(4,128)}, f32[64,4,128]{2,1,0:T(4,128)}) custom-call(f32[65,4,128]{2,1,0:T(4,128)} %copy-done, f32[65,4,128]{2,1,0:T(4,128)} %copy-done.1, f32[65,4,128]{2,1,0:T(4,128)} %copy-done.2, f32[65,4,128]{2,1,0:T(4,128)} %copy-done.3, ...), custom_call_target="tpu_custom_call" | custom-call | tf_op jit(solution)/shard_map/place/pallas_call | solution.py:543
  25.2 4.6 %collective-permute-start.6 = (f32[64,4,128]{2,1,0:T(4,128)}, f32[64,4,128]{2,1,0:T(4,128)S(1)}, u32[]{:S(2)}, u32[]{:S(2)}) collective-permute-start(f32[64,4,128]{2,1,0:T(4,128)} %get-tuple-element.30), channel_id=1, source_target_pairs={{0,31},{1,24},{2,25},{3,26},{4,27},{5,28},{6,29},{7,30},{8,7},{9,0... | collective-permute-start | bytes 393224 | tf_op jit(solution)/shard_map/ppermute | solution.py:570
  29.9 0.3 collective-permute-start.4
  30.2 0.5 collective-permute-start.5
  30.7 24.4 %own.2 = (f32[4,64,128]{2,1,0:T(8,128)}, f32[4,64,128]{2,1,0:T(8,128)}) custom-call(f32[1024,128]{1,0:T(8,128)} %bitcast.9), custom_call_target="tpu_custom_call" | custom-call | flops 16357785600 | bytes 524288 | tf_op jit(solution)/shard_map/own/pallas_call | solution.py:590
  55.1 0.0 collective-permute-done.6
  55.1 0.0 copy-start.9
  55.1 0.0 collective-permute-done.4
  55.1 0.0 copy-start.7
  55.1 0.0 collective-permute-done.5
  55.1 0.0 copy-start.8
  55.1 0.6 copy-done.9
  55.7 0.1 copy-done.7
  55.8 0.1 copy-done.8
  55.9 58.4 %far.1 = (f32[4,64,128]{2,1,0:T(8,128)}, f32[4,64,128]{2,1,0:T(8,128)}, f32[2,2,64,128]{3,2,1,0:T(8,128)}, f32[2,2,64,128]{3,2,1,0:T(8,128)}, f32[2,64,128]{2,1,0:T(8,128)}) custom-call(f32[1024,128]{1,0:T(8,128)} %bitcast.10, f32[512,128]{1,0:T(8,128)} %bitcast.14, f32[512,128]{1,0:T(8,128)} %bitcast.15, f32[256,128]{1,0:T(8,128)} %bitcast.16, ...), custom_call_target="tpu_custom_call" | custom-call | flops 18874368000 | bytes 524288 | tf_op jit(solution)/shard_map/far/pallas_call | solution.py:604
  114.4 1.0 collective-permute-start.9
  115.4 0.0 collective-permute-start.7
  115.4 0.5 collective-permute-start.8
  115.9 30.9 %own.3 = (f32[4,64,128]{2,1,0:T(8,128)}, f32[4,64,128]{2,1,0:T(8,128)}) custom-call(f32[1024,128]{1,0:T(8,128)} %bitcast.11, f32[4,64,128]{2,1,0:T(8,128)} %get-tuple-element.33.refs_0_, f32[4,64,128]{2,1,0:T(8,128)} %get-tuple-element.34.refs_1_), custom_call_target="tpu_custom_call" | custom-call | flops 16357785600 | bytes 524288 | tf_op jit(solution)/shard_map/own/pallas_call | solution.py:590
  146.9 0.0 collective-permute-done.9.refs_2_
  146.9 0.0 copy-start.6
  146.9 0.0 collective-permute-done.7.refs_0_
  146.9 0.0 copy-start.4
  146.9 0.0 collective-permute-done.8.refs_1_
  146.9 0.0 copy-start.5
  146.9 0.6 copy-done.6
  147.5 0.1 copy-done.4
  147.6 0.0 copy-done.5
  147.6 2.0 %finish.1 = (f32[4,64,128]{2,1,0:T(8,128)}, f32[4,64,128]{2,1,0:T(8,128)}) custom-call(f32[1024,128]{1,0:T(8,128)} %bitcast.12, f32[4,64,128]{2,1,0:T(8,128)} %get-tuple-element.35.own_n, f32[4,64,128]{2,1,0:T(8,128)} %get-tuple-element.36.own_s, f32[2,2,64,128]{3,2,1,0:T(8,128)} %copy-done.4, f32[2,2,64,128]{3,2,1,0:T(8,128)} %copy-done.5, ...), custom_call_target="tpu_custom_call" | custom-call | tf_op jit(solution)/shard_map/finish/pallas_call | solution.py:622
Async XLA Ops:
  5.2 9.4 %collective-permute-start = (f32[65,4,128]{2,1,0:T(4,128)}, f32[65,4,128]{2,1,0:T(4,128)S(1)}, u32[]{:S(2)}, u32[]{:S(2)}) collective-permute-start(f32[65,4,128]{2,1,0:T(4,128)} %get-tuple-element.22), channel_id=1, source_target_pairs={{0,6},{1,7},{2,0},{3,1},{4,2},{5,3},{6,4},{7,5},{8,14},{9,15},{10,... | collective-permute-start | bytes 399368 | tf_op jit(solution)/shard_map/ppermute | solution.py:539
  10.3 7.1 %collective-permute-start.1 = (f32[65,4,128]{2,1,0:T(4,128)}, f32[65,4,128]{2,1,0:T(4,128)S(1)}, u32[]{:S(2)}, u32[]{:S(2)}) collective-permute-start(f32[65,4,128]{2,1,0:T(4,128)} %get-tuple-element.23), channel_id=1, source_target_pairs={{0,7},{1,0},{2,1},{3,2},{4,3},{5,4},{6,5},{7,6},{8,15},{9,8},{10,9... | collective-permute-start | bytes 399368 | tf_op jit(solution)/shard_map/ppermute | solution.py:539
  10.4 7.4 %collective-permute-start.2 = (f32[65,4,128]{2,1,0:T(4,128)}, f32[65,4,128]{2,1,0:T(4,128)S(1)}, u32[]{:S(2)}, u32[]{:S(2)}) collective-permute-start(f32[65,4,128]{2,1,0:T(4,128)} %get-tuple-element.24), channel_id=1, source_target_pairs={{0,1},{1,2},{2,3},{3,4},{4,5},{5,6},{6,7},{7,0},{8,9},{9,10},{10,1... | collective-permute-start | bytes 399368 | tf_op jit(solution)/shard_map/ppermute | solution.py:539
  10.9 8.4 %collective-permute-start.3 = (f32[65,4,128]{2,1,0:T(4,128)}, f32[65,4,128]{2,1,0:T(4,128)S(1)}, u32[]{:S(2)}, u32[]{:S(2)}) collective-permute-start(f32[65,4,128]{2,1,0:T(4,128)} %get-tuple-element.25), channel_id=1, source_target_pairs={{0,2},{1,3},{2,4},{3,5},{4,6},{5,7},{6,0},{7,1},{8,10},{9,11},{10,... | collective-permute-start | bytes 399368 | tf_op jit(solution)/shard_map/ppermute | solution.py:539
  14.6 4.7 %copy-start = (f32[65,4,128]{2,1,0:T(4,128)}, f32[65,4,128]{2,1,0:T(4,128)S(1)}, u32[]{:S(2)}) copy-start(f32[65,4,128]{2,1,0:T(4,128)S(1)} %collective-permute-done.refs_0_) | copy-start | bytes 399364
  17.4 1.8 %copy-start.1 = (f32[65,4,128]{2,1,0:T(4,128)}, f32[65,4,128]{2,1,0:T(4,128)S(1)}, u32[]{:S(2)}) copy-start(f32[65,4,128]{2,1,0:T(4,128)S(1)} %collective-permute-done.1.refs_1_) | copy-start | bytes 399364
  17.8 1.5 %copy-start.2 = (f32[65,4,128]{2,1,0:T(4,128)}, f32[65,4,128]{2,1,0:T(4,128)S(1)}, u32[]{:S(2)}) copy-start(f32[65,4,128]{2,1,0:T(4,128)S(1)} %collective-permute-done.2.refs_2_) | copy-start | bytes 399364
  19.3 0.7 copy-start.3
  25.2 29.9 %collective-permute-start.6 = (f32[64,4,128]{2,1,0:T(4,128)}, f32[64,4,128]{2,1,0:T(4,128)S(1)}, u32[]{:S(2)}, u32[]{:S(2)}) collective-permute-start(f32[64,4,128]{2,1,0:T(4,128)} %get-tuple-element.30), channel_id=1, source_target_pairs={{0,31},{1,24},{2,25},{3,26},{4,27},{5,28},{6,29},{7,30},{8,7},{9,0... | collective-permute-start | bytes 393224 | tf_op jit(solution)/shard_map/ppermute | solution.py:570
  29.9 25.2 %collective-permute-start.4 = (f32[128,4,128]{2,1,0:T(4,128)}, f32[128,4,128]{2,1,0:T(4,128)S(1)}, u32[]{:S(2)}, u32[]{:S(2)}) collective-permute-start(f32[128,4,128]{2,1,0:T(4,128)} %get-tuple-element.28), channel_id=1, source_target_pairs={{0,7},{1,0},{2,1},{3,2},{4,3},{5,4},{6,5},{7,6},{8,15},{9,8},{10,9... | collective-permute-start | bytes 786440 | tf_op jit(solution)/shard_map/ppermute | solution.py:570
  30.2 24.9 %collective-permute-start.5 = (f32[128,4,128]{2,1,0:T(4,128)}, f32[128,4,128]{2,1,0:T(4,128)S(1)}, u32[]{:S(2)}, u32[]{:S(2)}) collective-permute-start(f32[128,4,128]{2,1,0:T(4,128)} %get-tuple-element.29), channel_id=1, source_target_pairs={{0,24},{1,25},{2,26},{3,27},{4,28},{5,29},{6,30},{7,31},{8,0},{9,1... | collective-permute-start | bytes 786440 | tf_op jit(solution)/shard_map/ppermute | solution.py:570
  55.1 0.7 copy-start.9
  55.1 0.7 copy-start.7
  55.1 0.8 copy-start.8
  114.4 32.5 %collective-permute-start.9 = (f32[2,64,128]{2,1,0:T(8,128)}, f32[2,64,128]{2,1,0:T(8,128)S(1)}, u32[]{:S(2)}, u32[]{:S(2)}) collective-permute-start(f32[2,64,128]{2,1,0:T(8,128)} %get-tuple-element.39), channel_id=1, source_target_pairs={{0,9},{1,10},{2,11},{3,12},{4,13},{5,14},{6,15},{7,8},{8,17},{9,18... | collective-permute-start | bytes 196616 | tf_op jit(solution)/shard_map/ppermute | solution.py:570
  115.4 31.5 %collective-permute-start.7 = (f32[2,2,64,128]{3,2,1,0:T(8,128)}, f32[2,2,64,128]{3,2,1,0:T(8,128)S(1)}, u32[]{:S(2)}, u32[]{:S(2)}) collective-permute-start(f32[2,2,64,128]{3,2,1,0:T(8,128)} %get-tuple-element.37), channel_id=1, source_target_pairs={{0,1},{1,2},{2,3},{3,4},{4,5},{5,6},{6,7},{7,0},{8,9},{9,10},{10,1... | collective-permute-start | bytes 393224 | tf_op jit(solution)/shard_map/ppermute | solution.py:570
  115.4 31.5 %collective-permute-start.8 = (f32[2,2,64,128]{3,2,1,0:T(8,128)}, f32[2,2,64,128]{3,2,1,0:T(8,128)S(1)}, u32[]{:S(2)}, u32[]{:S(2)}) collective-permute-start(f32[2,2,64,128]{3,2,1,0:T(8,128)} %get-tuple-element.38), channel_id=1, source_target_pairs={{0,8},{1,9},{2,10},{3,11},{4,12},{5,13},{6,14},{7,15},{8,16},{9,17... | collective-permute-start | bytes 393224 | tf_op jit(solution)/shard_map/ppermute | solution.py:570
  146.9 0.6 copy-start.6
  146.9 0.7 copy-start.4
  146.9 0.7 copy-start.5

commit v5 on v4

--- a/solution.py
+++ b/solution.py
@@ -303,7 +303,7 @@
         return lax.rsqrt(jnp.minimum(jnp.maximum(square, min_square), 1.0))
 
     def level_step(z):
-        mine = lax.broadcasted_iota(jnp.int32, (8, 128), 1) == z
+        found = {}
         for row, tiles in tasks:
             total = None
             fields = {}
@@ -352,16 +352,22 @@
                             at = pl.ds(pl.multiple_of((col * span + 1 + z + shift) * 8, 8), 8)
                             col_n[at, :] += down_n
                             col_s[at, :] += down_s
-                for totals, sums in ((row_n, sums_n), (row_s, sums_s)):
+                for channel, sums in enumerate((sums_n, sums_s)):
                     for g in range(groups):
-                        at = slice(part * half + g * 8, part * half + g * 8 + 8)
-                        totals[row, at, :] = jnp.where(
-                            mine, jnp.sum(sums[g], axis=1, keepdims=True), totals[row, at, :]
+                        found[channel, row, part * groups + g] = jnp.sum(
+                            sums[g], axis=1, keepdims=True
                         )
+        return found
 
     def some_levels(k, _):
-        for u in range(unroll):
-            level_step(k * unroll + u)
+        lane = lax.broadcasted_iota(jnp.int32, (8, 128), 1)
+        levels_found = [level_step(k * unroll + u) for u in range(unroll)]
+        for channel, row, g in levels_found[0]:
+            totals = (row_n, row_s)[channel]
+            value = totals[row, g * 8 : g * 8 + 8, :]
+            for u, found in enumerate(levels_found):
+                value = jnp.where(lane == k * unroll + u, found[channel, row, g], value)
+            totals[row, g * 8 : g * 8 + 8, :] = value
         return 0
 
     lax.fori_loop(0, levels // unroll, some_levels, 0)
@@ -600,7 +606,7 @@
             name="own",
         )(raw, *start)
 
-    early_n, early_s = own_pairs(0, 1, 4)
+    early_n, early_s = own_pairs(0, 1, 8)
     far_n, far_s, ret_dom, ret_slab, ret_edge = pl.pallas_call(
         functools.partial(
             far_kernel, levels=levels, half=half, unroll=4, slabs=slabs, doms=doms

time: 150 us -> 148 us (0.987)
  Pallas kernels: 126 us -> 124 us
where the time goes in v5:
time: 148 us
  Pallas kernels  124 us (84%)
  starting transfers between devices  13.4 us (9%)
  waiting for transfers between devices  7.75 us (5%)
  local copies, waits for them, and re-layouts  2.16 us (1%)
    pallas_call x1, Pallas kernels, local(): pl.pallas_call(functools.partial(far_kernel, levels=levels, half=half, un...  58.2 us
    pallas_call x2, Pallas kernels, own_pairs(): pl.pallas_call(functools.partial(own_kernel, levels=levels, half=half, un...  54.1 us
    ppermute x4, waiting for transfers between devices, local(): lax.ppermute(pack, 'dom', [(i, (i + step) % doms) for i in range(doms)])  7.74 us
    ppermute x6, starting transfers between devices, send(): return lax.ppermute(value, both, route(step_slab, step_dom))  7.04 us
    ppermute x4, starting transfers between devices, local(): lax.ppermute(pack, 'dom', [(i, (i + step) % doms) for i in range(doms)])  6.32 us
    pallas_call x1, Pallas kernels, local(): pl.pallas_call(functools.partial(place_kernel, cells=cells, capacity=capa...  5.29 us
    pallas_call x1, Pallas kernels, local(): pl.pallas_call(functools.partial(pack_kernel, cells=cells, capacity=capac...  4.58 us
  transfers between devices with their start and end apart: 10, of which 4 were waited for; matrix products, arithmetic and copies ran while one was open for 0% of the time, Pallas kernels for 37%

profile of v5, /device:TPU:0, one launch (start us, length us, event | category | flops | bytes accessed | tf_op | source)
XLA Modules:
  0.0 148.2 jit_solution(1076176476154926478)
XLA Ops:
  0.6 4.6 %pack.1 = (f32[65,4,128]{2,1,0:T(4,128)}, f32[65,4,128]{2,1,0:T(4,128)}, f32[65,4,128]{2,1,0:T(4,128)}, f32[65,4,128]{2,1,0:T(4,128)}, f32[256,4,128]{2,1,0:T(4,128)}) custom-call(s32[2,128]{1,0:T(2,128)} %bitcast.13, f32[256,4,128]{2,1,0:T(4,128)} %bitcast.8), custom_call_target="tpu_custom_call" | custom-call | tf_op jit(solution)/shard_map/pack/pallas_call | solution.py:530
  5.2 5.1 %collective-permute-start = (f32[65,4,128]{2,1,0:T(4,128)}, f32[65,4,128]{2,1,0:T(4,128)S(1)}, u32[]{:S(2)}, u32[]{:S(2)}) collective-permute-start(f32[65,4,128]{2,1,0:T(4,128)} %get-tuple-element.22), channel_id=1, source_target_pairs={{0,6},{1,7},{2,0},{3,1},{4,2},{5,3},{6,4},{7,5},{8,14},{9,15},{10,... | collective-permute-start | bytes 399368 | tf_op jit(solution)/shard_map/ppermute | solution.py:545
  10.3 0.0 collective-permute-start.1
  10.4 0.5 collective-permute-start.2
  10.9 0.7 collective-permute-start.3
  11.5 3.1 %collective-permute-done.refs_0_ = f32[65,4,128]{2,1,0:T(4,128)S(1)} collective-permute-done((f32[65,4,128]{2,1,0:T(4,128)}, f32[65,4,128]{2,1,0:T(4,128)S(1)}, u32[]{:S(2)}, u32[]{:S(2)}) %collective-permute-start) | collective-permute-done | bytes 133152 | tf_op jit(solution)/shard_map/ppermute | solution.py:545
  14.6 0.0 copy-start
  14.6 2.9 %collective-permute-done.1.refs_1_ = f32[65,4,128]{2,1,0:T(4,128)S(1)} collective-permute-done((f32[65,4,128]{2,1,0:T(4,128)}, f32[65,4,128]{2,1,0:T(4,128)S(1)}, u32[]{:S(2)}, u32[]{:S(2)}) %collective-permute-start.1) | collective-permute-done | bytes 133152 | tf_op jit(solution)/shard_map/ppermute | solution.py:545
  17.4 0.0 copy-start.1
  17.4 0.3 collective-permute-done.2.refs_2_
  17.8 0.0 copy-start.2
  17.8 1.5 %collective-permute-done.3.refs_3_ = f32[65,4,128]{2,1,0:T(4,128)S(1)} collective-permute-done((f32[65,4,128]{2,1,0:T(4,128)}, f32[65,4,128]{2,1,0:T(4,128)S(1)}, u32[]{:S(2)}, u32[]{:S(2)}) %collective-permute-start.3) | collective-permute-done | bytes 133152 | tf_op jit(solution)/shard_map/ppermute | solution.py:545
  19.3 0.0 copy-start.3
  19.3 0.0 copy-done
  19.3 0.0 copy-done.1
  19.3 0.0 copy-done.2
  19.3 0.6 copy-done.3
  19.9 5.3 %place.1 = (f32[256,4,128]{2,1,0:T(4,128)}, f32[128,4,128]{2,1,0:T(4,128)}, f32[128,4,128]{2,1,0:T(4,128)}, f32[64,4,128]{2,1,0:T(4,128)}) custom-call(f32[65,4,128]{2,1,0:T(4,128)} %copy-done, f32[65,4,128]{2,1,0:T(4,128)} %copy-done.1, f32[65,4,128]{2,1,0:T(4,128)} %copy-done.2, f32[65,4,128]{2,1,0:T(4,128)} %copy-done.3, ...), custom_call_target="tpu_custom_call" | custom-call | tf_op jit(solution)/shard_map/place/pallas_call | solution.py:549
  25.2 4.6 %collective-permute-start.6 = (f32[64,4,128]{2,1,0:T(4,128)}, f32[64,4,128]{2,1,0:T(4,128)S(1)}, u32[]{:S(2)}, u32[]{:S(2)}) collective-permute-start(f32[64,4,128]{2,1,0:T(4,128)} %get-tuple-element.30), channel_id=1, source_target_pairs={{0,31},{1,24},{2,25},{3,26},{4,27},{5,28},{6,29},{7,30},{8,7},{9,0... | collective-permute-start | bytes 393224 | tf_op jit(solution)/shard_map/ppermute | solution.py:576
  29.9 0.3 collective-permute-start.4
  30.2 0.5 collective-permute-start.5
  30.7 23.6 %own.2 = (f32[4,64,128]{2,1,0:T(8,128)}, f32[4,64,128]{2,1,0:T(8,128)}) custom-call(f32[1024,128]{1,0:T(8,128)} %bitcast.9), custom_call_target="tpu_custom_call" | custom-call | flops 16357785600 | bytes 524288 | tf_op jit(solution)/shard_map/own/pallas_call | solution.py:596
  54.3 0.0 collective-permute-done.6
  54.3 0.0 copy-start.9
  54.3 0.0 collective-permute-done.4
  54.3 0.0 copy-start.7
  54.3 0.0 collective-permute-done.5
  54.4 0.0 copy-start.8
  54.4 0.6 copy-done.9
  55.0 0.1 copy-done.7
  55.1 0.1 copy-done.8
  55.2 58.2 %far.1 = (f32[4,64,128]{2,1,0:T(8,128)}, f32[4,64,128]{2,1,0:T(8,128)}, f32[2,2,64,128]{3,2,1,0:T(8,128)}, f32[2,2,64,128]{3,2,1,0:T(8,128)}, f32[2,64,128]{2,1,0:T(8,128)}) custom-call(f32[1024,128]{1,0:T(8,128)} %bitcast.10, f32[512,128]{1,0:T(8,128)} %bitcast.14, f32[512,128]{1,0:T(8,128)} %bitcast.15, f32[256,128]{1,0:T(8,128)} %bitcast.16, ...), custom_call_target="tpu_custom_call" | custom-call | flops 18874368000 | bytes 524288 | tf_op jit(solution)/shard_map/far/pallas_call | solution.py:610
  113.4 1.0 collective-permute-start.9
  114.4 0.0 collective-permute-start.7
  114.4 0.5 collective-permute-start.8
  114.9 30.5 %own.3 = (f32[4,64,128]{2,1,0:T(8,128)}, f32[4,64,128]{2,1,0:T(8,128)}) custom-call(f32[1024,128]{1,0:T(8,128)} %bitcast.11, f32[4,64,128]{2,1,0:T(8,128)} %get-tuple-element.33.refs_0_, f32[4,64,128]{2,1,0:T(8,128)} %get-tuple-element.34.refs_1_), custom_call_target="tpu_custom_call" | custom-call | flops 16357785600 | bytes 524288 | tf_op jit(solution)/shard_map/own/pallas_call | solution.py:596
  145.4 0.0 collective-permute-done.9.refs_2_
  145.4 0.0 copy-start.6
  145.4 0.0 collective-permute-done.7.refs_0_
  145.5 0.0 copy-start.4
  145.5 0.0 collective-permute-done.8.refs_1_
  145.5 0.0 copy-start.5
  145.5 0.6 copy-done.6
  146.1 0.1 copy-done.4
  146.1 0.0 copy-done.5
  146.2 2.0 %finish.1 = (f32[4,64,128]{2,1,0:T(8,128)}, f32[4,64,128]{2,1,0:T(8,128)}) custom-call(f32[1024,128]{1,0:T(8,128)} %bitcast.12, f32[4,64,128]{2,1,0:T(8,128)} %get-tuple-element.35.own_n, f32[4,64,128]{2,1,0:T(8,128)} %get-tuple-element.36.own_s, f32[2,2,64,128]{3,2,1,0:T(8,128)} %copy-done.4, f32[2,2,64,128]{3,2,1,0:T(8,128)} %copy-done.5, ...), custom_call_target="tpu_custom_call" | custom-call | tf_op jit(solution)/shard_map/finish/pallas_call | solution.py:628
Async XLA Ops:
  5.2 9.4 %collective-permute-start = (f32[65,4,128]{2,1,0:T(4,128)}, f32[65,4,128]{2,1,0:T(4,128)S(1)}, u32[]{:S(2)}, u32[]{:S(2)}) collective-permute-start(f32[65,4,128]{2,1,0:T(4,128)} %get-tuple-element.22), channel_id=1, source_target_pairs={{0,6},{1,7},{2,0},{3,1},{4,2},{5,3},{6,4},{7,5},{8,14},{9,15},{10,... | collective-permute-start | bytes 399368 | tf_op jit(solution)/shard_map/ppermute | solution.py:545
  10.3 7.1 %collective-permute-start.1 = (f32[65,4,128]{2,1,0:T(4,128)}, f32[65,4,128]{2,1,0:T(4,128)S(1)}, u32[]{:S(2)}, u32[]{:S(2)}) collective-permute-start(f32[65,4,128]{2,1,0:T(4,128)} %get-tuple-element.23), channel_id=1, source_target_pairs={{0,7},{1,0},{2,1},{3,2},{4,3},{5,4},{6,5},{7,6},{8,15},{9,8},{10,9... | collective-permute-start | bytes 399368 | tf_op jit(solution)/shard_map/ppermute | solution.py:545
  10.4 7.4 %collective-permute-start.2 = (f32[65,4,128]{2,1,0:T(4,128)}, f32[65,4,128]{2,1,0:T(4,128)S(1)}, u32[]{:S(2)}, u32[]{:S(2)}) collective-permute-start(f32[65,4,128]{2,1,0:T(4,128)} %get-tuple-element.24), channel_id=1, source_target_pairs={{0,1},{1,2},{2,3},{3,4},{4,5},{5,6},{6,7},{7,0},{8,9},{9,10},{10,1... | collective-permute-start | bytes 399368 | tf_op jit(solution)/shard_map/ppermute | solution.py:545
  10.9 8.4 %collective-permute-start.3 = (f32[65,4,128]{2,1,0:T(4,128)}, f32[65,4,128]{2,1,0:T(4,128)S(1)}, u32[]{:S(2)}, u32[]{:S(2)}) collective-permute-start(f32[65,4,128]{2,1,0:T(4,128)} %get-tuple-element.25), channel_id=1, source_target_pairs={{0,2},{1,3},{2,4},{3,5},{4,6},{5,7},{6,0},{7,1},{8,10},{9,11},{10,... | collective-permute-start | bytes 399368 | tf_op jit(solution)/shard_map/ppermute | solution.py:545
  14.6 4.7 %copy-start = (f32[65,4,128]{2,1,0:T(4,128)}, f32[65,4,128]{2,1,0:T(4,128)S(1)}, u32[]{:S(2)}) copy-start(f32[65,4,128]{2,1,0:T(4,128)S(1)} %collective-permute-done.refs_0_) | copy-start | bytes 399364
  17.4 1.8 %copy-start.1 = (f32[65,4,128]{2,1,0:T(4,128)}, f32[65,4,128]{2,1,0:T(4,128)S(1)}, u32[]{:S(2)}) copy-start(f32[65,4,128]{2,1,0:T(4,128)S(1)} %collective-permute-done.1.refs_1_) | copy-start | bytes 399364
  17.8 1.5 %copy-start.2 = (f32[65,4,128]{2,1,0:T(4,128)}, f32[65,4,128]{2,1,0:T(4,128)S(1)}, u32[]{:S(2)}) copy-start(f32[65,4,128]{2,1,0:T(4,128)S(1)} %collective-permute-done.2.refs_2_) | copy-start | bytes 399364
  19.3 0.7 copy-start.3
  25.2 29.1 %collective-permute-start.6 = (f32[64,4,128]{2,1,0:T(4,128)}, f32[64,4,128]{2,1,0:T(4,128)S(1)}, u32[]{:S(2)}, u32[]{:S(2)}) collective-permute-start(f32[64,4,128]{2,1,0:T(4,128)} %get-tuple-element.30), channel_id=1, source_target_pairs={{0,31},{1,24},{2,25},{3,26},{4,27},{5,28},{6,29},{7,30},{8,7},{9,0... | collective-permute-start | bytes 393224 | tf_op jit(solution)/shard_map/ppermute | solution.py:576
  29.9 24.5 %collective-permute-start.4 = (f32[128,4,128]{2,1,0:T(4,128)}, f32[128,4,128]{2,1,0:T(4,128)S(1)}, u32[]{:S(2)}, u32[]{:S(2)}) collective-permute-start(f32[128,4,128]{2,1,0:T(4,128)} %get-tuple-element.28), channel_id=1, source_target_pairs={{0,7},{1,0},{2,1},{3,2},{4,3},{5,4},{6,5},{7,6},{8,15},{9,8},{10,9... | collective-permute-start | bytes 786440 | tf_op jit(solution)/shard_map/ppermute | solution.py:576
  30.2 24.2 %collective-permute-start.5 = (f32[128,4,128]{2,1,0:T(4,128)}, f32[128,4,128]{2,1,0:T(4,128)S(1)}, u32[]{:S(2)}, u32[]{:S(2)}) collective-permute-start(f32[128,4,128]{2,1,0:T(4,128)} %get-tuple-element.29), channel_id=1, source_target_pairs={{0,24},{1,25},{2,26},{3,27},{4,28},{5,29},{6,30},{7,31},{8,0},{9,1... | collective-permute-start | bytes 786440 | tf_op jit(solution)/shard_map/ppermute | solution.py:576
  54.3 0.7 copy-start.9
  54.3 0.7 copy-start.7
  54.4 0.8 copy-start.8
  113.4 32.1 %collective-permute-start.9 = (f32[2,64,128]{2,1,0:T(8,128)}, f32[2,64,128]{2,1,0:T(8,128)S(1)}, u32[]{:S(2)}, u32[]{:S(2)}) collective-permute-start(f32[2,64,128]{2,1,0:T(8,128)} %get-tuple-element.39), channel_id=1, source_target_pairs={{0,9},{1,10},{2,11},{3,12},{4,13},{5,14},{6,15},{7,8},{8,17},{9,18... | collective-permute-start | bytes 196616 | tf_op jit(solution)/shard_map/ppermute | solution.py:576
  114.4 31.1 %collective-permute-start.7 = (f32[2,2,64,128]{3,2,1,0:T(8,128)}, f32[2,2,64,128]{3,2,1,0:T(8,128)S(1)}, u32[]{:S(2)}, u32[]{:S(2)}) collective-permute-start(f32[2,2,64,128]{3,2,1,0:T(8,128)} %get-tuple-element.37), channel_id=1, source_target_pairs={{0,1},{1,2},{2,3},{3,4},{4,5},{5,6},{6,7},{7,0},{8,9},{9,10},{10,1... | collective-permute-start | bytes 393224 | tf_op jit(solution)/shard_map/ppermute | solution.py:576
  114.4 31.1 %collective-permute-start.8 = (f32[2,2,64,128]{3,2,1,0:T(8,128)}, f32[2,2,64,128]{3,2,1,0:T(8,128)S(1)}, u32[]{:S(2)}, u32[]{:S(2)}) collective-permute-start(f32[2,2,64,128]{3,2,1,0:T(8,128)} %get-tuple-element.38), channel_id=1, source_target_pairs={{0,8},{1,9},{2,10},{3,11},{4,12},{5,13},{6,14},{7,15},{8,16},{9,17... | collective-permute-start | bytes 393224 | tf_op jit(solution)/shard_map/ppermute | solution.py:576
  145.4 0.6 copy-start.6
  145.5 0.7 copy-start.4
  145.5 0.7 copy-start.5
